TPU v7x, 32 devices: a whole 2x2x4 slice. The times are simulated.
32 devices in a mesh: dp: 4 (over x, core), ctx: 2 (over y), tensor: 4 (over z).
Axes of the slice: x: 2, y: 2, z: 4, core: 2. Of those that a mesh axis runs over, the one named last changes fastest.
Arguments:
- inputs: bfloat16 [2048, 2048], P(('dp', 'ctx'), 'tensor'), may hold values from -6 to 6
- cotangent: bfloat16 [2048, 2048], P(('dp', 'ctx')), may hold values from -6 to 6
- segments: int32 [4, 512], P('dp'), may hold values from 0 to 15, as said below
- positions: int32 [4, 512], P('dp', 'ctx'), may hold values from 0 to 511, as said below
- attention_gain: bfloat16 [2048], replicated, may hold values from 0.5 to 1.5
- query_weight: bfloat16 [2048, 2048], P(None, 'tensor'), may hold values from -0.125 to 0.125
- key_weight: bfloat16 [2048, 1024], P(None, 'tensor'), may hold values from -0.125 to 0.125
- value_weight: bfloat16 [2048, 1024], P(None, 'tensor'), may hold values from -0.125 to 0.125
- query_gain: bfloat16 [128], replicated, may hold values from 0.5 to 1.5
- key_gain: bfloat16 [128], replicated, may hold values from 0.5 to 1.5
- output_weight: bfloat16 [2048, 2048], P('tensor'), may hold values from -0.75 to 0.75
- feed_gain: bfloat16 [2048], replicated, may hold values from 0.3 to 5, as said below
- gate_weight: bfloat16 [2048, 6144], P(None, 'tensor'), may hold values from -0.125 to 0.125
- up_weight: bfloat16 [2048, 6144], P(None, 'tensor'), may hold values from -0.125 to 0.125
- down_weight: bfloat16 [6144, 2048], P('tensor'), may hold values from -0.078125 to 0.078125
Outputs:
- outputs: bfloat16 [2048, 2048], P(('dp', 'ctx'), 'tensor')
- grad_inputs: float32 [2048, 2048], P(('dp', 'ctx'), 'tensor')
- grad_attention_gain: float32 [2048], P('tensor')
- grad_query_weight: float32 [2048, 2048], P(None, 'tensor')
- grad_key_weight: float32 [2048, 1024], P(None, 'tensor')
- grad_value_weight: float32 [2048, 1024], P(None, 'tensor')
- grad_query_gain: float32 [128], replicated
- grad_key_gain: float32 [128], replicated
- grad_output_weight: float32 [2048, 2048], P('tensor')
- grad_feed_gain: float32 [2048], P('tensor')
- grad_gate_weight: float32 [2048, 6144], P(None, 'tensor')
- grad_up_weight: float32 [2048, 6144], P(None, 'tensor')
- grad_down_weight: float32 [6144, 2048], P('tensor')
Inputs may be any that keep to these rules, and one draw needn't show every extreme that they name: `segments`: in each sequence the document numbers start at 0, never fall, and each document is one run of equal numbers; a sequence holds at most 16 documents. `positions`: a token's position counts from 0 at the first token of its document. `feed_gain`: positive gains.
All inputs are finite; a program needn't handle non-finite values.
Results may differ from a plain program's by a relative error of at most 0.024.
Values may be sent and summed in bfloat16 or wider, within the bound.
No kernel may reach another device: no remote copies, remote signals or barrier semaphores. Data moves between devices by JAX's collectives and lax.ppermute only.
A program may use at most 256 MiB of HBM per device.

v0:
```python
import jax
import jax.numpy as jnp
from jax import lax
from jax.sharding import PartitionSpec as P

HD = 128


EPS = 1e-06
THETA = 1000000.0
NEG = -1e30


def rope_tables(position_row):
    half = HD // 2
    freqs = jnp.exp(-(2.0 * jnp.arange(half, dtype=jnp.float32) / HD) * jnp.log(jnp.float32(THETA)))
    angles = position_row.astype(jnp.float32)[:, None] * freqs[None, :]
    return (jnp.cos(angles)[:, None, :], jnp.sin(angles)[:, None, :])


def rotate(value, cosine, sine):
    half = value.shape[-1] // 2
    first = value[..., :half]
    second = value[..., half:]
    return jnp.concatenate(
        [first * cosine - second * sine, second * cosine + first * sine], axis=-1
    )


def head_prepare(raw, gain, cosine, sine):
    count = raw.shape[0]
    heads = raw.reshape(count, -1, HD)
    normed = heads * lax.rsqrt(jnp.mean(heads * heads, axis=-1, keepdims=True) + EPS) * gain
    return rotate(normed, cosine, sine).reshape(count, -1)


def matmul(left, right):
    return jnp.dot(left, right, preferred_element_type=jnp.float32)


def per_device(
    inputs,
    cotangent,
    segments,
    positions,
    attention_gain,
    query_weight,
    key_weight,
    value_weight,
    query_gain,
    key_gain,
    output_weight,
    feed_gain,
    gate_weight,
    up_weight,
    down_weight,
):
    count = inputs.shape[0]
    shard = inputs.shape[1]
    width = cotangent.shape[1]
    column = lax.axis_index("tensor") * shard
    place = lax.axis_index("ctx")
    kv_local = key_weight.shape[1] // HD
    group = query_weight.shape[1] // key_weight.shape[1]
    factor = HD ** (-0.5)
    block = min(512, count)
    blocks = count // block
    gain_one = attention_gain.astype(jnp.float32)
    gain_two = feed_gain.astype(jnp.float32)
    gain_one_part = lax.dynamic_slice_in_dim(gain_one, column, shard)
    gain_two_part = lax.dynamic_slice_in_dim(gain_two, column, shard)
    cosine, sine = rope_tables(positions[0])
    gathered = lax.all_gather(inputs, "tensor", axis=1, tiled=True).astype(jnp.float32)
    inverse_one = lax.rsqrt(jnp.mean(gathered * gathered, axis=-1, keepdims=True) + EPS)
    unit_one = gathered * inverse_one
    normed_one = (unit_one * gain_one).astype(jnp.bfloat16)
    query_raw = matmul(normed_one, query_weight)
    key_raw = matmul(normed_one, key_weight)
    value_rows = matmul(normed_one, value_weight).astype(jnp.bfloat16)
    query_float, query_pull = jax.vjp(
        lambda raw, gain: head_prepare(raw, gain, cosine, sine),
        query_raw,
        query_gain.astype(jnp.float32),
    )
    key_float, key_pull = jax.vjp(
        lambda raw, gain: head_prepare(raw, gain, cosine, sine),
        key_raw,
        key_gain.astype(jnp.float32),
    )
    query_rows = query_float.astype(jnp.bfloat16)
    key_rows = key_float.astype(jnp.bfloat16)
    segment_row = segments[0]
    all_keys, all_values = (
        lax.all_gather(key_rows, "ctx", axis=0, tiled=True),
        lax.all_gather(value_rows, "ctx", axis=0, tiled=True),
    )
    total_keys = all_keys.shape[0]
    key_index = jnp.arange(total_keys, dtype=jnp.int32)
    row_offset = place * count
    key_heads = all_keys.reshape(total_keys, kv_local, HD)
    value_heads = all_values.reshape(total_keys, kv_local, HD)
    query_blocks = query_rows.reshape(blocks, block, kv_local, group, HD)

    def allowed_mask(index):
        start = index * block
        row_index = row_offset + start + jnp.arange(block, dtype=jnp.int32)
        row_segment = lax.dynamic_slice_in_dim(segment_row, row_offset + start, block)
        return (row_segment[:, None] == segment_row[None, :]) & (
            key_index[None, :] <= row_index[:, None]
        )

    def block_scores(rows, index):
        scores = (
            jnp.einsum("qhgd,khd->hgqk", rows, key_heads, preferred_element_type=jnp.float32)
            * factor
        )
        return jnp.where(allowed_mask(index)[None, None], scores, NEG)

    def forward_block(index):
        rows = query_blocks[index]
        scores = block_scores(rows, index)
        top = jnp.max(scores, axis=-1, keepdims=True)
        raised = jnp.exp(scores - top)
        total = jnp.sum(raised, axis=-1, keepdims=True)
        weights = (raised / total).astype(jnp.bfloat16)
        mixed = jnp.einsum(
            "hgqk,khd->qhgd", weights, value_heads, preferred_element_type=jnp.float32
        )
        return (mixed.astype(jnp.bfloat16), top + jnp.log(total))

    mixed_blocks, log_totals = lax.map(forward_block, jnp.arange(blocks, dtype=jnp.int32))
    mixed_rows = mixed_blocks.reshape(count, -1)
    attention_terms = matmul(mixed_rows, output_weight)
    branch = lax.psum_scatter(attention_terms, "tensor", scatter_dimension=1, tiled=True)
    resid_part = (inputs.astype(jnp.float32) + branch).astype(jnp.bfloat16)
    resid_rows = lax.all_gather(resid_part, "tensor", axis=1, tiled=True).astype(jnp.float32)
    inverse_two = lax.rsqrt(jnp.mean(resid_rows * resid_rows, axis=-1, keepdims=True) + EPS)
    unit_two = resid_rows * inverse_two
    normed_two = (unit_two * gain_two).astype(jnp.bfloat16)
    gate = matmul(normed_two, gate_weight)
    up_rows = matmul(normed_two, up_weight)
    sigmoid = jax.nn.sigmoid(gate)
    silu = gate * sigmoid
    hidden = (silu * up_rows).astype(jnp.bfloat16)
    feed = lax.psum_scatter(
        matmul(hidden, down_weight).astype(jnp.bfloat16), "tensor", scatter_dimension=1, tiled=True
    ).astype(jnp.float32)
    outputs = (resid_part.astype(jnp.float32) + feed).astype(jnp.bfloat16)
    grad_down = matmul(hidden.T, cotangent)
    grad_hidden = matmul(cotangent, down_weight.T)
    grad_gate = (grad_hidden * up_rows * sigmoid * (1.0 + gate * (1.0 - sigmoid))).astype(
        jnp.bfloat16
    )
    grad_up = (grad_hidden * silu).astype(jnp.bfloat16)
    grad_gate_w = matmul(normed_two.T, grad_gate)
    grad_up_w = matmul(normed_two.T, grad_up)
    grad_normed_two = matmul(grad_gate, gate_weight.T) + matmul(grad_up, up_weight.T)
    unit_two_part = lax.dynamic_slice_in_dim(unit_two, column, shard, 1)
    grad_out_part = lax.dynamic_slice_in_dim(cotangent, column, shard, 1).astype(jnp.float32)
    grad_two_part = lax.psum_scatter(grad_normed_two, "tensor", scatter_dimension=1, tiled=True)
    row_term_two = jnp.sum(gain_two_part * grad_two_part * unit_two_part, axis=-1)
    row_total_two = lax.psum(row_term_two, "tensor")
    grad_feed_gain = jnp.sum(grad_two_part * unit_two_part, axis=0)
    grad_resid = (
        grad_out_part
        + inverse_two * (gain_two_part * grad_two_part)
        - unit_two_part * (inverse_two / width) * row_total_two[:, None]
    )
    grad_resid_rows = lax.all_gather(grad_resid.astype(jnp.bfloat16), "tensor", axis=1, tiled=True)
    grad_output_w = matmul(mixed_rows.T, grad_resid_rows)
    grad_mixed = matmul(grad_resid_rows, output_weight.T).astype(jnp.bfloat16)
    grad_mixed_blocks = grad_mixed.reshape(blocks, block, kv_local, group, HD)

    def backward_block(carry, index):
        key_total, value_total = carry
        rows = query_blocks[index]
        grad_rows = grad_mixed_blocks[index]
        scores = block_scores(rows, index)
        probs = jnp.exp(scores - log_totals[index])
        grad_probs = jnp.einsum(
            "qhgd,khd->hgqk", grad_rows, value_heads, preferred_element_type=jnp.float32
        )
        delta = jnp.sum(probs * grad_probs, axis=-1, keepdims=True)
        grad_scores = (probs * (grad_probs - delta)).astype(jnp.bfloat16)
        grad_query = (
            jnp.einsum("hgqk,khd->qhgd", grad_scores, key_heads, preferred_element_type=jnp.float32)
            * factor
        )
        key_total = (
            key_total
            + jnp.einsum("hgqk,qhgd->khd", grad_scores, rows, preferred_element_type=jnp.float32)
            * factor
        )
        value_total = value_total + jnp.einsum(
            "hgqk,qhgd->khd",
            probs.astype(jnp.bfloat16),
            grad_rows,
            preferred_element_type=jnp.float32,
        )
        return ((key_total, value_total), grad_query)

    empty = jnp.zeros((total_keys, kv_local, HD), jnp.float32)
    (key_total, value_total), grad_query_blocks = lax.scan(
        backward_block, (empty, empty), jnp.arange(blocks, dtype=jnp.int32)
    )
    grad_query_rows = grad_query_blocks.reshape(count, -1)
    key_total = key_total.reshape(total_keys, -1)
    value_total = value_total.reshape(total_keys, -1)
    grad_key_rot, grad_value = (
        lax.psum_scatter(
            key_total.astype(jnp.bfloat16), "ctx", scatter_dimension=0, tiled=True
        ).astype(jnp.float32),
        lax.psum_scatter(
            value_total.astype(jnp.bfloat16), "ctx", scatter_dimension=0, tiled=True
        ).astype(jnp.float32),
    )
    grad_query_raw, grad_query_gain = query_pull(grad_query_rows)
    grad_key_raw, grad_key_gain = key_pull(grad_key_rot)
    grad_query_low = grad_query_raw.astype(jnp.bfloat16)
    grad_key_low = grad_key_raw.astype(jnp.bfloat16)
    grad_value_low = grad_value.astype(jnp.bfloat16)
    grad_query_w = matmul(normed_one.T, grad_query_low)
    grad_key_w = matmul(normed_one.T, grad_key_low)
    grad_value_w = matmul(normed_one.T, grad_value_low)
    grad_normed_one = (
        matmul(grad_query_low, query_weight.T)
        + matmul(grad_key_low, key_weight.T)
        + matmul(grad_value_low, value_weight.T)
    )
    grad_one_part = lax.psum_scatter(
        grad_normed_one.astype(jnp.bfloat16), "tensor", scatter_dimension=1, tiled=True
    ).astype(jnp.float32)
    unit_one_part = lax.dynamic_slice_in_dim(unit_one, column, shard, 1)
    row_term_one = jnp.sum(gain_one_part * grad_one_part * unit_one_part, axis=-1)
    row_total_one, query_gain_total, key_gain_total = lax.psum(
        (row_term_one, grad_query_gain, grad_key_gain), "tensor"
    )
    grad_inputs = (
        grad_resid
        + inverse_one * (gain_one_part * grad_one_part)
        - unit_one_part * (inverse_one / width) * row_total_one[:, None]
    )
    grad_attention_gain = jnp.sum(grad_one_part * unit_one_part, axis=0)
    summed = (
        lax.psum(grad_attention_gain.astype(jnp.bfloat16), ("dp", "ctx")).astype(jnp.float32),
        lax.psum(grad_query_w.astype(jnp.bfloat16), ("dp", "ctx")).astype(jnp.float32),
        lax.psum(grad_key_w.astype(jnp.bfloat16), ("dp", "ctx")).astype(jnp.float32),
        lax.psum(grad_value_w.astype(jnp.bfloat16), ("dp", "ctx")).astype(jnp.float32),
        lax.psum(query_gain_total.astype(jnp.bfloat16), ("dp", "ctx")).astype(jnp.float32),
        lax.psum(key_gain_total.astype(jnp.bfloat16), ("dp", "ctx")).astype(jnp.float32),
        lax.psum(grad_output_w.astype(jnp.bfloat16), ("dp", "ctx")).astype(jnp.float32),
        lax.psum(grad_feed_gain.astype(jnp.bfloat16), ("dp", "ctx")).astype(jnp.float32),
        lax.psum(grad_gate_w.astype(jnp.bfloat16), ("dp", "ctx")).astype(jnp.float32),
        lax.psum(grad_up_w.astype(jnp.bfloat16), ("dp", "ctx")).astype(jnp.float32),
        lax.psum(grad_down.astype(jnp.bfloat16), ("dp", "ctx")).astype(jnp.float32),
    )
    return (outputs, grad_inputs) + tuple(summed)


def solution(mesh):
    in_specs = (
        P(("dp", "ctx"), "tensor"),
        P(("dp", "ctx"), None),
        P("dp", None),
        P("dp", "ctx"),
        P(),
        P(None, "tensor"),
        P(None, "tensor"),
        P(None, "tensor"),
        P(),
        P(),
        P("tensor", None),
        P(),
        P(None, "tensor"),
        P(None, "tensor"),
        P("tensor", None),
    )
    out_specs = (
        P(("dp", "ctx"), "tensor"),
        P(("dp", "ctx"), "tensor"),
        P("tensor"),
        P(None, "tensor"),
        P(None, "tensor"),
        P(None, "tensor"),
        P(),
        P(),
        P("tensor", None),
        P("tensor"),
        P(None, "tensor"),
        P(None, "tensor"),
        P("tensor", None),
    )
    return jax.shard_map(
        per_device, mesh=mesh, in_specs=in_specs, out_specs=out_specs, check_vma=False
    )
```

profile of v0, /device:TPU:0, one launch (start us, length us, event | category | flops | bytes accessed | tf_op | source)
XLA Modules:
  0.0 698.1 jit_solution(3110859281240040887)
XLA Ops:
  15.3 24.9 %all-gather.4.cloned.1.call-done = bf16[256,2048]{1,0:T(8,128)(2,1)} async-done(((bf16[256,512]{1,0:T(8,128)(2,1)}), bf16[256,2048]{1,0:T(8,128)(2,1)}) %all-gather.4.cloned.1.call-update) | async-done | bytes 1048592 | tf_op jit(solution)/shard_map/all_gather | solution.py:73
  42.3 2.0 convolution_convert_fusion.10
  44.4 5.8 all_gather.16
  50.9 2.0 multiply_reduce_fusion.7
  54.4 5.8 all_gather.17
  68.2 2.0 fusion.40
  70.3 43.8 %reduce-scatter.7.cloned.1.call-done = f32[256,512]{1,0:T(8,128)} async-done(((f32[256,2048]{1,0:T(8,128)}), f32[256,512]{1,0:T(8,128)}) %reduce-scatter.7.cloned.1.call-update) | async-done | bytes 524304 | tf_op jit(solution)/shard_map/reduce_scatter | solution.py:134
  114.1 1.8 add_convert_fusion.1
  116.1 27.2 %all-gather.6.cloned.1.call-done = bf16[256,2048]{1,0:T(8,128)(2,1)} async-done(((bf16[256,512]{1,0:T(8,128)(2,1)}), bf16[256,2048]{1,0:T(8,128)(2,1)}) %all-gather.6.cloned.1.call-update) | async-done | bytes 1048592 | tf_op jit(solution)/shard_map/all_gather | solution.py:136
  143.3 1.7 fusion.3
  145.6 5.8 fusion.33
  151.4 1.9 fusion.34
  153.3 3.3 multiply_convert_fusion.2
  156.7 1.8 fusion.41
  158.5 3.2 convolution_add_fusion.1
  164.1 41.2 %reduce-scatter.11.cloned.1.call-done = f32[256,512]{1,0:T(8,128)} async-done(((f32[256,2048]{1,0:T(8,128)}), f32[256,512]{1,0:T(8,128)}) %reduce-scatter.11.cloned.1.call-update) | async-done | bytes 524304 | tf_op jit(solution)/shard_map/reduce_scatter | solution.py:160
  205.3 2.0 multiply_reduce_fusion
  207.2 10.5 %psum.105 = f32[256]{0:T(256)} all-reduce(f32[256]{0:T(256)} %get-tuple-element.70), channel_id=1, replica_groups=mesh['dp'=4,'ctx'=2,'tensor'=4] {'tensor'}, use_global_device_ids=true, to_apply=%region_10.11 | all-reduce | flops 256 | bytes 2048 | tf_op jit(solution)/shard_map/psum | solution.py:162
  217.7 2.4 fusion.37
  220.9 25.7 %all-gather.8.cloned.1.call-done = bf16[256,2048]{1,0:T(8,128)(2,1)} async-done(((bf16[256,512]{1,0:T(8,128)(2,1)}), bf16[256,2048]{1,0:T(8,128)(2,1)}) %all-gather.8.cloned.1.call-update) | async-done | bytes 1048592 | tf_op jit(solution)/shard_map/all_gather | solution.py:169
  246.5 2.7 convolution_convert_fusion.8
  249.2 1.8 copy.115
  251.0 2.4 fusion.4
  256.2 2.2 fusion.12
  258.6 5.9 convolution_convert_fusion.7
  268.6 2.2 multiply_reduce_fusion.1
  271.0 1.6 fusion.21
  275.1 7.0 %reduce-scatter.15.cloned.1.call-done = bf16[256,256]{0,1:T(8,128)(2,1)} async-done(((bf16[512,256]{0,1:T(8,128)(2,1)}), bf16[256,256]{0,1:T(8,128)(2,1)}) %reduce-scatter.15.cloned.1.call-update) | async-done | bytes 131088 | tf_op jit(solution)/shard_map/reduce_scatter | solution.py:213
  282.1 1.9 fusion.43
  284.0 1.8 fusion.1
  285.9 6.1 convolution_convert_fusion
  292.0 4.7 convolution_convert_fusion.1
  296.6 4.6 convolution_convert_fusion.2
  301.3 2.0 convolution_convert_fusion.3
  303.4 2.2 convolution_convert_fusion.4
  305.5 1.6 convolution_convert_fusion.5
  309.7 2.5 reduce-scatter.9.cloned.1.call-done
  312.1 1.7 add_convert_fusion
  313.8 27.1 %reduce-scatter.17.cloned.1.call-done = bf16[256,512]{1,0:T(8,128)(2,1)} async-done(((bf16[256,2048]{1,0:T(8,128)(2,1)}), bf16[256,512]{1,0:T(8,128)(2,1)}) %reduce-scatter.17.cloned.1.call-update) | async-done | bytes 262160 | tf_op jit(solution)/shard_map/reduce_scatter | solution.py:230
  342.1 9.7 %all-reduce.4 = (f32[256]{0:T(256)S(1)}, bf16[128]{0:T(256)(128)(2,1)S(1)}, bf16[128]{0:T(256)(128)(2,1)S(1)}) all-reduce(f32[256]{0:T(256)S(1)} %get-tuple-element.72, f32[128]{0:T(128)S(1)} %copy-done.63, f32[128]{0:T(128)S(1)} %copy-done.64), channel_id=1, replica_groups=mesh['dp'=4,'ctx'=2,'tensor'=4] {'tensor'}, use_global_device_ids=true, to_apply=%region_18.19 | all-reduce | flops 512 | bytes 3584 | tf_op jit(solution)/shard_map/psum | solution.py:235
  351.8 14.4 %all-reduce.5 = (bf16[512]{0:T(512)(128)(2,1)S(1)}, bf16[128]{0:T(256)(128)(2,1)S(1)}, bf16[128]{0:T(256)(128)(2,1)S(1)}, bf16[512]{0:T(512)(128)(2,1)S(1)}) all-reduce(bf16[512]{0:T(512)(128)(2,1)S(1)} %get-tuple-element.71, bf16[128]{0:T(256)(128)(2,1)S(1)} %get-tuple-element.78, ...), channel_id=1, replica_groups=mesh['dp'=4,'ctx'=2,'tensor'=4] {'dp','ctx'}, use_global_device_ids=true, to_apply=%region_20.21 | all-reduce | flops 1280 | bytes 5120 | tf_op jit(solution)/shard_map/psum | solution.py:245
  368.4 2.1 fusion.18
  370.5 287.1 %all-reduce.9.cloned.1.call-done = (bf16[2048,512]{1,0:T(8,128)(2,1)}, bf16[2048,256]{1,0:T(8,128)(2,1)}, bf16[2048,256]{1,0:T(8,128)(2,1)}, bf16[512,2048]{1,0:...) async-done(((bf16[2048,512]{1,0:T(8,128)(2,1)}, bf16[2048,256]{1,0:T(8,128)(2,1)}, bf16[2048,256]{1,0:T(8,128)(2,1)}, ...) | async-done | bytes 25165840 | tf_op jit(solution)/shard_map/psum | solution.py:246
  657.6 4.3 convert_element_type.251
  665.8 2.7 convert_element_type.261
  668.4 9.5 %convert_element_type.265 = f32[2048,1536]{1,0:T(8,128)} convert(bf16[2048,1536]{1,0:T(8,128)(2,1)} %get-tuple-element.101) | non-fusion elementwise | flops 3145728 | bytes 18874368 | tf_op jit(solution)/shard_map/convert_element_type | solution.py:253
  677.9 6.6 convert_element_type.267
  684.5 6.3 convert_element_type.269
  (238 shorter events, 43.6 us)
Async XLA Ops:
  7.2 61.0 %copy-start = (bf16[512,2048]{1,0:T(8,128)(2,1)S(1)}, bf16[512,2048]{1,0:T(8,128)(2,1)}, u32[]{:S(2)}) copy-start(bf16[512,2048]{1,0:T(8,128)(2,1)} %param.25) | copy-start | bytes 6291460
  7.2 33.1 %all-gather.4.cloned.1.call-start = ((), (), s32[]{:S(2)}) async-start(), calls=%async_computation.6 | async-start | bytes 1310720 | tf_op jit(solution)/shard_map/all_gather | solution.py:73
  7.9 106.1 %reduce-scatter.7.cloned.1.call-start = ((), (), s32[]{:S(2)}) async-start(), calls=%async_computation.7 | async-start | bytes 2621440 | tf_op jit(solution)/shard_map/reduce_scatter | solution.py:134
  8.6 55.5 %copy-start.58 = (f32[128]{0:T(128)}, f32[128]{0:T(128)S(1)}, u32[]{:S(2)}) copy-start(f32[128]{0:T(128)S(1)} %convert_element_type.215) | copy-start | bytes 1540
  11.2 49.0 %copy-start.56 = (f32[2048]{0:T(1024)}, f32[2048]{0:T(1024)S(1)}, u32[]{:S(2)}) copy-start(f32[2048]{0:T(1024)S(1)} %convert_element_type.208) | copy-start | bytes 24580
  11.7 28.5 %copy-start.16 = (f32[256,64]{1,0:T(8,128)}, f32[256,64]{1,0:T(8,128)S(1)}, u32[]{:S(2)}) copy-start(f32[256,64]{1,0:T(8,128)S(1)} %get-tuple-element.120) | copy-start | bytes 196612
  41.8 9.1 %copy-start.9 = (bf16[256,2048]{1,0:T(8,128)(2,1)S(1)}, bf16[256,2048]{1,0:T(8,128)(2,1)}, u32[]{:S(2)}) copy-start(bf16[256,2048]{1,0:T(8,128)(2,1)} %all-gather.4.cloned.1.call-done) | copy-start | bytes 3145732
  42.3 17.8 %copy-start.50 = (f32[256]{0:T(256)}, f32[256]{0:T(256)S(1)}, u32[]{:S(2)}) copy-start(f32[256]{0:T(256)S(1)} %get-tuple-element.122) | copy-start | bytes 3076
  50.9 9.3 %copy-start.22 = (bf16[2048,512]{1,0:T(8,128)(2,1)S(1)}, bf16[2048,512]{1,0:T(8,128)(2,1)}, u32[]{:S(2)}) copy-start(bf16[2048,512]{1,0:T(8,128)(2,1)} %param.20) | copy-start | bytes 6291460
  53.0 7.2 %copy-start.54 = (f32[256,2]{0,1:T(2,128)}, f32[256,2]{0,1:T(2,128)S(1)}, u32[]{:S(2)}) copy-start(f32[256,2]{0,1:T(2,128)S(1)} %get-tuple-element.125) | copy-start | bytes 6148
  70.2 43.8 %copy-start.30 = (bf16[256,512]{1,0:T(8,128)(2,1)S(1)}, bf16[256,512]{1,0:T(8,128)(2,1)}, u32[]{:S(2)}) copy-start(bf16[256,512]{1,0:T(8,128)(2,1)} %param.15) | copy-start | bytes 786436
  70.2 45.9 %copy-start.52 = (bf16[2048]{0:T(1024)(128)(2,1)S(1)}, bf16[2048]{0:T(1024)(128)(2,1)}, u32[]{:S(2)}) copy-start(bf16[2048]{0:T(1024)(128)(2,1)} %param.26) | copy-start | bytes 12292
  70.3 73.1 %all-gather.6.cloned.1.call-start = ((), (), s32[]{:S(2)}) async-start(), calls=%async_computation.8 | async-start | bytes 1310720 | tf_op jit(solution)/shard_map/all_gather | solution.py:136
  115.9 89.4 %reduce-scatter.11.cloned.1.call-start = ((), (), s32[]{:S(2)}) async-start(), calls=%async_computation.10 | async-start | bytes 2621440 | tf_op jit(solution)/shard_map/reduce_scatter | solution.py:160
  143.3 8.0 %slice-start.4 = ((s8[6291456]{0:T(1024)(128)(4,1)}), s8[4194304]{0:T(1024)(128)(4,1)S(1)}, s32[]{:S(2)}) async-start(s8[6291456]{0:T(1024)(128)(4,1)} %bitcast.132), calls=%async_computation.20 | async-start | bytes 8388608
  143.3 10.0 %slice-start.8 = ((s8[6291456]{0:T(1024)(128)(4,1)}), s8[4194304]{0:T(1024)(128)(4,1)S(1)}, s32[]{:S(2)}) async-start(s8[6291456]{0:T(1024)(128)(4,1)} %bitcast.136), calls=%async_computation.24 | async-start | bytes 8388608
  145.6 5.8 copy-start.4
  145.6 5.8 slice-start.5
  145.6 7.8 %slice-start.9 = ((s8[6291456]{0:T(1024)(128)(4,1)}), s8[2097152]{0:T(1024)(128)(4,1)S(1)}, s32[]{:S(2)}) async-start(s8[6291456]{0:T(1024)(128)(4,1)} %bitcast.136), calls=%async_computation.25 | async-start | bytes 4194304
  151.4 7.1 %slice-start.6 = ((s8[6291456]{0:T(1024)(128)(4,1)}), s8[4194304]{0:T(1024)(128)(4,1)S(1)}, s32[]{:S(2)}) async-start(s8[6291456]{0:T(1024)(128)(4,1)} %bitcast.134), calls=%async_computation.22 | async-start | bytes 8388608
  153.3 5.2 slice-start.7
  161.7 84.8 %all-gather.8.cloned.1.call-start = ((), (), s32[]{:S(2)}) async-start(), calls=%async_computation.11 | async-start | bytes 1310720 | tf_op jit(solution)/shard_map/all_gather | solution.py:169
  220.1 52.5 %reduce-scatter.13.cloned.1.call-start = ((), (), s32[]{:S(2)}) async-start(), calls=%async_computation.12 | async-start | bytes 393216 | tf_op jit(solution)/shard_map/reduce_scatter | solution.py:210
  256.1 26.0 %reduce-scatter.15.cloned.1.call-start = ((), (), s32[]{:S(2)}) async-start(), calls=%async_computation.13 | async-start | bytes 393216 | tf_op jit(solution)/shard_map/reduce_scatter | solution.py:213
  258.3 53.8 %reduce-scatter.9.cloned.1.call-start = ((), (), s32[]{:S(2)}) async-start(), calls=%async_computation.9 | async-start | bytes 1310720 | tf_op jit(solution)/shard_map/reduce_scatter | solution.py:145
  258.6 6.0 copy-start.8
  258.6 6.0 copy-start.13
  264.6 76.4 %reduce-scatter.17.cloned.1.call-start = ((), (), s32[]{:S(2)}) async-start(), calls=%async_computation.14 | async-start | bytes 1310720 | tf_op jit(solution)/shard_map/reduce_scatter | solution.py:230
  267.0 3.8 copy-start.46
  267.0 4.0 copy-start.59
  268.6 5.1 copy-start.39
  268.6 5.1 copy-start.41
  275.1 8.9 %copy-start.33 = (bf16[256,4,128]{2,1,0:T(4,128)(2,1)S(1)}, bf16[256,4,128]{2,1,0:T(4,128)(2,1)}, u32[]{:S(2)}) copy-start(bf16[256,4,128]{2,1,0:T(4,128)(2,1)} %fusion.21) | copy-start | bytes 786436
  285.8 6.1 copy-start.37
  285.9 371.8 %all-reduce.9.cloned.1.call-start = ((), (), s32[]{:S(2)}) async-start(), calls=%async_computation.15 | async-start | bytes 50331648 | tf_op jit(solution)/shard_map/psum | solution.py:246
  292.0 4.7 copy-start.35
  296.6 4.6 copy-start.29
  296.6 4.6 copy-start.32
  309.4 32.6 %copy-start.63 = (f32[128]{0:T(128)S(1)}, f32[128]{0:T(128)}, u32[]{:S(2)}) copy-start(f32[128]{0:T(128)} %get-tuple-element.73) | copy-start | bytes 1540
  309.4 32.6 %copy-start.64 = (f32[128]{0:T(128)S(1)}, f32[128]{0:T(128)}, u32[]{:S(2)}) copy-start(f32[128]{0:T(128)} %get-tuple-element.75) | copy-start | bytes 1540
  309.4 42.3 %copy-start.62 = (bf16[512]{0:T(512)(128)(2,1)S(1)}, bf16[512]{0:T(512)(128)(2,1)}, u32[]{:S(2)}) copy-start(bf16[512]{0:T(512)(128)(2,1)} %get-tuple-element.69) | copy-start | bytes 3076
  309.4 59.0 %copy-start.61 = (f32[256]{0:T(256)S(1)}, f32[256]{0:T(256)}, u32[]{:S(2)}) copy-start(f32[256]{0:T(256)} %get-tuple-element.121) | copy-start | bytes 3076
  657.6 4.3 copy-start.27
  665.8 12.2 %slice-start.2 = ((s8[6291456]{0:T(1024)(128)(4,1)}), s8[4194304]{0:T(1024)(128)(4,1)S(1)}, s32[]{:S(2)}) async-start(s8[6291456]{0:T(1024)(128)(4,1)} %bitcast.107), calls=%async_computation.18 | async-start | bytes 8388608
  668.4 9.5 %slice-start.3 = ((s8[6291456]{0:T(1024)(128)(4,1)}), s8[2097152]{0:T(1024)(128)(4,1)S(1)}, s32[]{:S(2)}) async-start(s8[6291456]{0:T(1024)(128)(4,1)} %bitcast.107), calls=%async_computation.19 | async-start | bytes 4194304
  668.4 16.1 %slice-start = ((s8[6291456]{0:T(1024)(128)(4,1)}), s8[4194304]{0:T(1024)(128)(4,1)S(1)}, s32[]{:S(2)}) async-start(s8[6291456]{0:T(1024)(128)(4,1)} %bitcast.105), calls=%async_computation.16 | async-start | bytes 8388608
  677.9 6.6 slice-start.1
  684.5 6.3 copy-start.1
  (37 other events, 72.5 us)
Sparse Core Ops, SparseCore 0:
  9.6 30.6 all-gather.3
  70.4 43.6 reduce-scatter.6
  116.0 27.2 all-gather.5
  161.9 43.3 reduce-scatter.10
  220.2 26.2 all-gather.7
  256.2 11.1 reduce-scatter.12
  270.4 11.6 reduce-scatter.14
  284.9 27.1 reduce-scatter.8
  315.1 25.7 reduce-scatter.16
  347.0 310.6 all-reduce.8
where the time goes:
time: 704 us; the launch traced here: 698 us
  waiting for transfers between devices  487 us (69%)
  other arithmetic  67.8 us (10%)
  matrix products  66.2 us (9%)
  blocking collectives  46.2 us (7%)
  between operations  15.5 us (2%)
  local copies, waits for them, and re-layouts  14.4 us (2%)
    psum x1, waiting for transfers between devices, per_device(): lax.psum(grad_query_w.astype(jnp.bfloat16), ('dp', 'ctx'))  287 us
    dot_general x21, matrix products, matmul(): return jnp.dot(left, right, preferred_element_type=jnp.float32)  59.1 us
    reduce_scatter x1, waiting for transfers between devices, per_device(): lax.psum_scatter(attention_terms, 'tensor', scatter_dimension=1, tiled=True)  43.8 us
    reduce_scatter x1, waiting for transfers between devices, per_device(): lax.psum_scatter(grad_normed_two, 'tensor', scatter_dimension=1, tiled=True)  41.2 us
    all_gather x1, waiting for transfers between devices, per_device(): lax.all_gather(resid_part, 'tensor', axis=1, tiled=True).astype(jnp.float32)  27.2 us
    reduce_scatter x1, waiting for transfers between devices, per_device(): lax.psum_scatter(grad_normed_one.astype(jnp.bfloat16), 'tensor', scatter_...  27.1 us
    all_gather x1, waiting for transfers between devices, per_device(): lax.all_gather(grad_resid.astype(jnp.bfloat16), 'tensor', axis=1, tiled=T...  25.7 us
    all_gather x1, waiting for transfers between devices, per_device(): lax.all_gather(inputs, 'tensor', axis=1, tiled=True).astype(jnp.float32)  24.9 us
  transfers between devices with their start and end apart: 10, of which 9 were waited for; matrix products, arithmetic and copies ran while one was open for 9% of the time, Pallas kernels for 0%

commit v1 on v0

v1 whole, which is shorter than its diff:
```python
import jax
import jax.numpy as jnp
from jax import lax
from jax.sharding import PartitionSpec as P

HD = 128
EPS = 1e-06
THETA = 1000000.0
NEG = -1e30
BF = jnp.bfloat16
F32 = jnp.float32


def swap(value, axis, bit):
    size = lax.axis_size(axis)
    return lax.ppermute(value, axis, [(i, i ^ bit) for i in range(size)])


def bits_of(size):
    out = []
    bit = 1
    while bit < size:
        out.append(bit)
        bit *= 2
    return out


def gather_pieces(value, axis):
    pieces = {0: value}
    for bit in reversed(bits_of(lax.axis_size(axis))):
        for s in list(pieces):
            pieces[s | bit] = swap(pieces[s], axis, bit)
    return [pieces[s] for s in range(len(pieces))]


def scatter_pieces(pieces, axis):
    pieces = dict(enumerate(pieces))
    size = lax.axis_size(axis)
    for bit in bits_of(size):
        keep = [s for s in sorted(pieces, reverse=True) if not s & bit]
        for s in keep:
            total = pieces[s].astype(F32) + swap(pieces[s | bit].astype(BF), axis, bit).astype(F32)
            pieces[s] = total
            del pieces[s | bit]
    return pieces[0]


def in_order(pieces, index):
    count = len(pieces)
    blocks = list(pieces)
    for bit in bits_of(count):
        flag = (index & bit) != 0
        blocks = [jnp.where(flag, blocks[s ^ bit], blocks[s]) for s in range(count)]
    return jnp.concatenate(blocks, axis=-1)


def out_of_order(value, index, count):
    width = value.shape[-1] // count
    return [
        lax.dynamic_slice_in_dim(value, (index ^ s) * width, width, value.ndim - 1)
        for s in range(count)
    ]


def plane_far():
    far = [("dp", bit) for bit in bits_of(lax.axis_size("dp")) if bit > 1]
    return far + [("ctx", bit) for bit in bits_of(lax.axis_size("ctx"))]


def plane_gather(value):
    half = value.shape[0] // 2
    far = plane_far()
    out = []
    for part, order in ((value[:half], far), (value[half:], far[::-1])):
        rows = [part]
        for count, (axis, bit) in enumerate(order):
            more = [swap(r, axis, bit) for r in rows]
            rows = [jnp.concatenate(rows + more, axis=0)] if count == 0 else rows + more
        if lax.axis_size("dp") > 1:
            rows = rows + [swap(r, "dp", 1) for r in rows]
        out += rows
    return out


def plane_sum_halving(value, order):
    kept = []
    for axis, bit in order:
        flag = ((lax.axis_index(axis) // bit) % 2).astype(jnp.int32)
        half = value.shape[0] // 2
        keep = lax.dynamic_slice_in_dim(value, flag * half, half, 0)
        send = lax.dynamic_slice_in_dim(value, (1 - flag) * half, half, 0)
        value = (keep.astype(F32) + swap(send, axis, bit).astype(F32)).astype(BF)
        kept.append(flag)
    for (axis, bit), flag in zip(reversed(order), reversed(kept)):
        other = swap(value, axis, bit)
        value = jnp.where(
            flag == 0,
            jnp.concatenate([value, other], axis=0),
            jnp.concatenate([other, value], axis=0),
        )
    return value


def rope_tables(position_row):
    half = HD // 2
    freqs = jnp.exp(-(2.0 * jnp.arange(half, dtype=F32) / HD) * jnp.log(F32(THETA)))
    angles = position_row.astype(F32)[:, None] * freqs[None, :]
    return (jnp.cos(angles)[:, None, :], jnp.sin(angles)[:, None, :])


def rotate(value, cosine, sine):
    half = value.shape[-1] // 2
    first = value[..., :half]
    second = value[..., half:]
    return jnp.concatenate(
        [first * cosine - second * sine, second * cosine + first * sine], axis=-1
    )


def head_prepare(raw, gain, cosine, sine):
    count = raw.shape[0]
    heads = raw.reshape(count, -1, HD)
    normed = heads * lax.rsqrt(jnp.mean(heads * heads, axis=-1, keepdims=True) + EPS) * gain
    return rotate(normed, cosine, sine).reshape(count, -1)


def matmul(left, right):
    return jnp.dot(left, right, preferred_element_type=F32)


def matmul_nt(left, right):
    return lax.dot_general(left, right, (((1,), (1,)), ((), ())), preferred_element_type=F32)


def matmul_tn(left, right):
    return lax.dot_general(left, right, (((0,), (0,)), ((), ())), preferred_element_type=F32)


def per_device(
    inputs,
    cotangent,
    segments,
    positions,
    attention_gain,
    query_weight,
    key_weight,
    value_weight,
    query_gain,
    key_gain,
    output_weight,
    feed_gain,
    gate_weight,
    up_weight,
    down_weight,
):
    count = inputs.shape[0]
    shard = inputs.shape[1]
    width = cotangent.shape[1]
    tensor = lax.axis_size("tensor")
    me = lax.axis_index("tensor")
    column = me * shard
    place = lax.axis_index("ctx")
    core = lax.axis_index("dp") % 2
    kv_local = key_weight.shape[1] // HD
    group = query_weight.shape[1] // key_weight.shape[1]
    factor = HD ** (-0.5)
    gain_one = attention_gain.astype(F32)
    gain_two = feed_gain.astype(F32)
    gain_one_part = lax.dynamic_slice_in_dim(gain_one, column, shard)

    input_pieces = gather_pieces(inputs, "tensor")
    all_cotangent = plane_gather(cotangent)
    gathered = in_order(input_pieces, me).astype(F32)
    inverse_one = lax.rsqrt(jnp.mean(gathered * gathered, axis=-1, keepdims=True) + EPS)
    unit_one = gathered * inverse_one
    normed_one = (unit_one * gain_one).astype(BF)
    cosine, sine = rope_tables(positions[0])
    value_rows = matmul(normed_one, value_weight).astype(BF)
    key_raw = matmul(normed_one, key_weight)
    key_float, key_pull = jax.vjp(
        lambda raw, gain: head_prepare(raw, gain, cosine, sine), key_raw, key_gain.astype(F32)
    )
    key_rows = key_float.astype(BF)
    kv_rows = jnp.concatenate([key_rows, value_rows], axis=1)
    kv_pieces = gather_pieces(kv_rows, "ctx")
    query_raw = matmul(normed_one, query_weight)
    query_float, query_pull = jax.vjp(
        lambda raw, gain: head_prepare(raw, gain, cosine, sine), query_raw, query_gain.astype(F32)
    )
    query_rows = query_float.astype(BF)
    all_normed_one = plane_gather(normed_one)

    segment_row = segments[0]
    blocks = len(kv_pieces)
    kv_all = jnp.concatenate(kv_pieces, axis=0)
    kv_width = key_rows.shape[1]
    total_keys = kv_all.shape[0]
    key_heads = kv_all[:, :kv_width].reshape(total_keys, kv_local, HD)
    value_heads = kv_all[:, kv_width:].reshape(total_keys, kv_local, HD)
    block_iota = jnp.arange(count, dtype=jnp.int32)
    row_index = place * count + block_iota
    key_index = jnp.concatenate([(place ^ s) * count + block_iota for s in range(blocks)])
    row_segment = lax.dynamic_slice_in_dim(segment_row, place * count, count)
    key_segment = jnp.concatenate(
        [lax.dynamic_slice_in_dim(segment_row, (place ^ s) * count, count) for s in range(blocks)]
    )
    allowed = (row_segment[:, None] == key_segment[None, :]) & (
        key_index[None, :] <= row_index[:, None]
    )
    query_heads = query_rows.reshape(count, kv_local, group, HD)
    scores = (
        jnp.einsum("qhgd,khd->hgqk", query_heads, key_heads, preferred_element_type=F32) * factor
    )
    scores = jnp.where(allowed[None, None], scores, NEG)
    top = jnp.max(scores, axis=-1, keepdims=True)
    raised = jnp.exp(scores - top)
    total = jnp.sum(raised, axis=-1, keepdims=True)
    probs = raised / total
    weights = probs.astype(BF)
    mixed = jnp.einsum("hgqk,khd->qhgd", weights, value_heads, preferred_element_type=F32)
    mixed_rows = mixed.astype(BF).reshape(count, -1)
    branch_part = matmul(mixed_rows, output_weight).astype(BF)
    branch = scatter_pieces(out_of_order(branch_part, me, tensor), "tensor")
    resid_part = (inputs.astype(F32) + branch).astype(BF)
    resid_rows = in_order(gather_pieces(resid_part, "tensor"), me).astype(F32)

    inverse_two = lax.rsqrt(jnp.mean(resid_rows * resid_rows, axis=-1, keepdims=True) + EPS)
    unit_two = resid_rows * inverse_two
    normed_two = (unit_two * gain_two).astype(BF)
    all_normed_two = plane_gather(normed_two)

    def feed_forward(rows, grads, gate_w, up_w, down_w):
        gate = matmul(rows, gate_w)
        up = matmul(rows, up_w)
        sigmoid = jax.nn.sigmoid(gate)
        silu = gate * sigmoid
        hidden = (silu * up).astype(BF)
        grad_hidden = matmul_nt(grads, down_w)
        grad_gate = (grad_hidden * up * sigmoid * (1.0 + gate * (1.0 - sigmoid))).astype(BF)
        grad_up = (grad_hidden * silu).astype(BF)
        return hidden, grad_gate, grad_up

    hidden, grad_gate, grad_up = feed_forward(
        normed_two, cotangent, gate_weight, up_weight, down_weight
    )
    grad_normed_two = (matmul_nt(grad_gate, gate_weight) + matmul_nt(grad_up, up_weight)).astype(BF)
    grad_two_part = scatter_pieces(out_of_order(grad_normed_two, me, tensor), "tensor")
    grad_two = in_order(gather_pieces(grad_two_part.astype(BF), "tensor"), me).astype(F32)
    feed_part = matmul(hidden, down_weight).astype(BF)
    feed = scatter_pieces(out_of_order(feed_part, me, tensor), "tensor")
    outputs = (resid_part.astype(F32) + feed).astype(BF)

    row_total_two = jnp.sum(gain_two * grad_two * unit_two, axis=-1, keepdims=True)
    feed_sums = jnp.sum(grad_two * unit_two, axis=0)
    grad_resid = (
        cotangent.astype(F32)
        + inverse_two * (gain_two * grad_two)
        - unit_two * (inverse_two / width) * row_total_two
    )
    grad_resid_low = grad_resid.astype(BF)
    grad_resid_part = lax.dynamic_slice_in_dim(grad_resid, column, shard, 1)

    grad_mixed = matmul_nt(grad_resid_low, output_weight).astype(BF)
    grad_heads = grad_mixed.reshape(count, kv_local, group, HD)
    grad_probs = jnp.einsum("qhgd,khd->hgqk", grad_heads, value_heads, preferred_element_type=F32)
    delta = jnp.sum(probs * grad_probs, axis=-1, keepdims=True)
    grad_scores = (probs * (grad_probs - delta)).astype(BF)
    grad_keys = (
        jnp.einsum("hgqk,qhgd->khd", grad_scores, query_heads, preferred_element_type=F32) * factor
    ).reshape(total_keys, -1)
    grad_values = jnp.einsum(
        "hgqk,qhgd->khd", weights, grad_heads, preferred_element_type=F32
    ).reshape(total_keys, -1)
    grad_kv = jnp.concatenate([grad_keys, grad_values], axis=1)
    grad_kv = scatter_pieces(
        [grad_kv[s * count : (s + 1) * count] for s in range(blocks)], "ctx"
    )
    grad_query_rows = (
        jnp.einsum("hgqk,khd->qhgd", grad_scores, key_heads, preferred_element_type=F32) * factor
    ).reshape(count, -1)
    grad_query_raw, grad_query_gain = query_pull(grad_query_rows)
    grad_key_raw, grad_key_gain = key_pull(grad_kv[:, :kv_width])
    grad_query_low = grad_query_raw.astype(BF)
    grad_key_low = grad_key_raw.astype(BF)
    grad_value_low = grad_kv[:, kv_width:].astype(BF)

    grad_normed_one = (
        matmul_nt(grad_query_low, query_weight)
        + matmul_nt(grad_key_low, key_weight)
        + matmul_nt(grad_value_low, value_weight)
    )
    row_term_one = jnp.sum(gain_one * grad_normed_one * unit_one, axis=-1)
    attention_sums = jnp.sum(grad_normed_one * unit_one, axis=0)
    small = jnp.concatenate(
        [row_term_one, feed_sums * (1.0 / tensor), attention_sums, grad_query_gain, grad_key_gain]
    )
    for bit in bits_of(tensor):
        small = small + swap(small, "tensor", bit)
    row_total_one = small[:count, None]
    small = small[count:]
    for axis in ("dp", "ctx"):
        for bit in bits_of(lax.axis_size(axis)):
            small = small + swap(small, axis, bit)
    grad_one_part = scatter_pieces(
        out_of_order(grad_normed_one.astype(BF), me, tensor), "tensor"
    )
    unit_one_part = lax.dynamic_slice_in_dim(unit_one, column, shard, 1)
    grad_inputs = (
        grad_resid_part
        + inverse_one * (gain_one_part * grad_one_part)
        - unit_one_part * (inverse_one / width) * row_total_one
    )
    grad_feed_gain = lax.dynamic_slice_in_dim(small, column, shard)
    grad_attention_gain = lax.dynamic_slice_in_dim(small, width + column, shard)
    grad_query_gain = small[2 * width : 2 * width + HD]
    grad_key_gain = small[2 * width + HD :]

    order = [("dp", 1)] + plane_far() if lax.axis_size("dp") > 1 else plane_far()
    grad_output_w = plane_sum_halving(matmul_tn(mixed_rows, grad_resid_low).astype(BF), order)
    grad_output_w = grad_output_w.astype(F32)
    grad_low = jnp.concatenate([grad_query_low, grad_key_low, grad_value_low], axis=1)
    rows_one = jnp.concatenate(all_normed_one, axis=0)
    grads_one = jnp.concatenate(plane_gather(grad_low), axis=0)
    q_width = query_weight.shape[1]
    grad_query_w = matmul_tn(rows_one, grads_one[:, :q_width])
    grad_key_w = matmul_tn(rows_one, grads_one[:, q_width : q_width + kv_width])
    grad_value_w = matmul_tn(rows_one, grads_one[:, q_width + kv_width :])

    half = gate_weight.shape[1] // 2
    rows_two = jnp.concatenate(all_normed_two, axis=0)
    rows_cot = jnp.concatenate(all_cotangent, axis=0)
    gate_half = lax.dynamic_slice_in_dim(gate_weight, core * half, half, 1)
    up_half = lax.dynamic_slice_in_dim(up_weight, core * half, half, 1)
    down_half = lax.dynamic_slice_in_dim(down_weight, core * half, half, 0)
    all_hidden, all_grad_gate, all_grad_up = feed_forward(
        rows_two, rows_cot, gate_half, up_half, down_half
    )

    def both_halves(mine, axis):
        other = swap(mine.astype(BF), "dp", 1).astype(F32)
        return jnp.where(
            core == 0,
            jnp.concatenate([mine, other], axis=axis),
            jnp.concatenate([other, mine], axis=axis),
        )

    grad_down_w = both_halves(matmul_tn(all_hidden, rows_cot), 0)
    grad_gate_w = both_halves(matmul_tn(rows_two, all_grad_gate), 1)
    grad_up_w = both_halves(matmul_tn(rows_two, all_grad_up), 1)

    return (
        outputs,
        grad_inputs,
        grad_attention_gain,
        grad_query_w,
        grad_key_w,
        grad_value_w,
        grad_query_gain,
        grad_key_gain,
        grad_output_w,
        grad_feed_gain,
        grad_gate_w,
        grad_up_w,
        grad_down_w,
    )


def solution(mesh):
    in_specs = (
        P(("dp", "ctx"), "tensor"),
        P(("dp", "ctx"), None),
        P("dp", None),
        P("dp", "ctx"),
        P(),
        P(None, "tensor"),
        P(None, "tensor"),
        P(None, "tensor"),
        P(),
        P(),
        P("tensor", None),
        P(),
        P(None, "tensor"),
        P(None, "tensor"),
        P("tensor", None),
    )
    out_specs = (
        P(("dp", "ctx"), "tensor"),
        P(("dp", "ctx"), "tensor"),
        P("tensor"),
        P(None, "tensor"),
        P(None, "tensor"),
        P(None, "tensor"),
        P(),
        P(),
        P("tensor", None),
        P("tensor"),
        P(None, "tensor"),
        P(None, "tensor"),
        P("tensor", None),
    )
    return jax.shard_map(
        per_device, mesh=mesh, in_specs=in_specs, out_specs=out_specs, check_vma=False
    )
```

time: 704 us -> 506 us (0.72)
  waiting for transfers between devices: 487 us -> 140 us
  matrix products: 66.2 us -> 141 us
  starting transfers between devices: 0.8 us -> 65.5 us
  local copies, waits for them, and re-layouts: 14.4 us -> 76 us
  blocking collectives: 46.2 us -> 0 us
  between operations: 15.5 us -> 2.81 us
    psum x1 -> x0, waiting for transfers between devices: 287 us -> none  [per_device(): lax.psum(grad_query_w.astype(jnp.bfloat16), ('dp', 'ctx'))]
    ppermute x0 -> x69, waiting for transfers between devices: none -> 140 us  [swap(): return lax.ppermute(value, axis, [(i, i ^ bit) for i in range(size)])]
    reduce_scatter x6 -> x0, waiting for transfers between devices: 121 us -> none  [the longest x1 43.8 us: per_device(): lax.psum_scatter(attention_terms, 'tensor', scatter_dimension=1, tiled=True)]
    all_gather x3 -> x0, waiting for transfers between devices: 77.8 us -> none  [the longest x1 27.2 us: per_device(): lax.all_gather(resid_part, 'tensor', axis=1, tiled=True).astype(jnp.float32)]
    dot_general x27 -> x29, matrix products: 66.2 us -> 137 us  [the longest x7 65.9 us: matmul_tn(): lax.dot_general(left, right, (((0,), (0,)), ((), ())), preferred_element_...]
    ppermute x0 -> x69, starting transfers between devices: none -> 65.5 us  [swap(): return lax.ppermute(value, axis, [(i, i ^ bit) for i in range(size)])]
    unnamed x152 -> x244, local copies, waits for them, and re-layouts: 7.18 us -> 55 us
    psum x3 -> x0, blocking collectives: 34.6 us -> none  [the longest x1 14.4 us: per_device(): lax.psum(grad_attention_gain.astype(jnp.bfloat16), ('dp', 'ctx'))]
  transfers between devices with their start and end apart: 10 -> 69, of which waited for: 9 -> 25; matrix products, arithmetic and copies ran while one was open for 9% -> 54% of each run, Pallas kernels for 0% -> 0%
where the time goes in v1:
time: 506 us; the launch traced here: 496 us
  matrix products  141 us (28%)
  waiting for transfers between devices  140 us (28%)
  local copies, waits for them, and re-layouts  76 us (15%)
  other arithmetic  70.9 us (14%)
  starting transfers between devices  65.5 us (13%)
    ppermute x69, waiting for transfers between devices, swap(): return lax.ppermute(value, axis, [(i, i ^ bit) for i in range(size)])  140 us
    dot_general x7, matrix products, matmul_tn(): lax.dot_general(left, right, (((0,), (0,)), ((), ())), preferred_element_...  65.9 us
    ppermute x69, starting transfers between devices, swap(): return lax.ppermute(value, axis, [(i, i ^ bit) for i in range(size)])  65.5 us
    unnamed x244, local copies, waits for them, and re-layouts  55 us
    dot_general x8, matrix products, matmul_nt(): lax.dot_general(left, right, (((1,), (1,)), ((), ())), preferred_element_...  33.1 us
    dot_general x9, matrix products, matmul(): return jnp.dot(left, right, preferred_element_type=F32)  28.6 us
    select_n x3, other arithmetic, both_halves(): jnp.where(core == 0, jnp.concatenate([mine, other], axis=axis), jnp.conca...  26.9 us
  transfers between devices with their start and end apart: 69, of which 25 were waited for; matrix products, arithmetic and copies ran while one was open for 54% of the time, Pallas kernels for 0%

profile of v1, /device:TPU:0, one launch (start us, length us, event | category | flops | bytes accessed | tf_op | source)
XLA Modules:
  0.0 496.2 jit_solution(6035335912586836634)
XLA Ops:
  0.7 4.1 collective-permute-start
  11.9 6.1 %fusion.87 = f32[256,1536]{1,0:T(8,128)} fusion(bf16[256,2048]{1,0:T(8,128)(2,1)} %param.16, bf16[1536,2048]{1,0:T(8,128)(2,1)} %param.29), kind=kOutput, calls=%fused_computation.272 | convolution fusion | flops 1610612736 | bytes 8912896 | tf_op jit(solution)/shard_map/dot_general | solution.py:132
  47.0 3.9 fusion.79
  50.9 3.1 convolution_convert_fusion.4
  62.8 3.5 collective-permute-start.6
  68.2 5.1 %collective-permute-done.28 = bf16[128,2048]{1,0:T(8,128)(2,1)S(1)} collective-permute-done((bf16[128,2048]{1,0:T(8,128)(2,1)S(1)}, bf16[128,2048]{1,0:T(8,128)(2,1)S(1)}, u32[]{:S(2)}, u32[]{:S(2)}) %collective-permute-start.28) | collective-permute-done | bytes 524320 | tf_op jit(solution)/shard_map/ppermute | solution.py:16
  76.5 3.3 collective-permute-start.7
  80.7 14.7 %collective-permute-done.32 = bf16[128,2048]{1,0:T(8,128)(2,1)S(1)} collective-permute-done((bf16[128,2048]{1,0:T(8,128)(2,1)S(1)}, bf16[128,2048]{1,0:T(8,128)(2,1)S(1)}, u32[]{:S(2)}, u32[]{:S(2)}) %collective-permute-start.32) | collective-permute-done | bytes 524320 | tf_op jit(solution)/shard_map/ppermute | solution.py:16
  101.8 3.9 collective-permute-done.9
  105.7 5.2 %collective-permute-done.8 = bf16[256,512]{1,0:T(8,128)(2,1)S(1)} collective-permute-done((bf16[256,512]{1,0:T(8,128)(2,1)S(1)}, bf16[256,512]{1,0:T(8,128)(2,1)S(1)}, u32[]{:S(2)}, u32[]{:S(2)}) %collective-permute-start.8) | collective-permute-done | bytes 262176 | tf_op jit(solution)/shard_map/ppermute | solution.py:16
  117.4 3.4 fusion.42
  120.8 5.8 %fusion.14 = bf16[256,2048]{1,0:T(8,128)(2,1)S(1)} fusion(f32[256,2048]{1,0:T(8,128)} %fusion.42, bf16[2048,1536]{1,0:T(8,128)(2,1)} %param.28, f32[256,1536]{1,0:T(8,128)S(1)} %copy-done.79, f32[256,1536]{1,0:T(8,128)} %copy-done.80), kind=kOutput, calls=%fused_computation.32 | convolution fusion | flops 1614020608 | bytes 12582912 | tf_op jit(solution)/shard_map/dot_general | solution.py:132
  134.8 4.1 collective-permute-done.11
  139.7 10.5 %collective-permute-done.14 = bf16[256,512]{1,0:T(8,128)(2,1)S(1)} collective-permute-done((bf16[256,512]{1,0:T(8,128)(2,1)S(1)}, bf16[256,512]{1,0:T(8,128)(2,1)S(1)}, u32[]{:S(2)}, u32[]{:S(2)}) %collective-permute-start.14) | collective-permute-done | bytes 262176 | tf_op jit(solution)/shard_map/ppermute | solution.py:16
  150.2 3.3 collective-permute-start.12
  153.5 6.2 %collective-permute-done.10 = bf16[256,512]{1,0:T(8,128)(2,1)S(1)} collective-permute-done((bf16[256,512]{1,0:T(8,128)(2,1)S(1)}, bf16[256,512]{1,0:T(8,128)(2,1)S(1)}, u32[]{:S(2)}, u32[]{:S(2)}) %collective-permute-start.10) | collective-permute-done | bytes 262176 | tf_op jit(solution)/shard_map/ppermute | solution.py:16
  162.3 7.2 %collective-permute-done.12 = bf16[256,512]{1,0:T(8,128)(2,1)S(1)} collective-permute-done((bf16[256,512]{1,0:T(8,128)(2,1)S(1)}, bf16[256,512]{1,0:T(8,128)(2,1)S(1)}, u32[]{:S(2)}, u32[]{:S(2)}) %collective-permute-start.12) | collective-permute-done | bytes 262176 | tf_op jit(solution)/shard_map/ppermute | solution.py:16
  170.8 3.9 collective-permute-done.15
  178.7 9.5 %collective-permute-done.54 = bf16[128,2048]{1,0:T(8,128)(2,1)S(1)} collective-permute-done((bf16[128,2048]{1,0:T(8,128)(2,1)S(1)}, bf16[128,2048]{1,0:T(8,128)(2,1)S(1)}, u32[]{:S(2)}, u32[]{:S(2)}) %collective-permute-start.54) | collective-permute-done | bytes 524320 | tf_op jit(solution)/shard_map/ppermute | solution.py:16
  191.2 11.9 %collective-permute-done.33 = bf16[256,2048]{1,0:T(8,128)(2,1)} collective-permute-done((bf16[256,2048]{1,0:T(8,128)(2,1)}, bf16[256,2048]{1,0:T(8,128)(2,1)}, u32[]{:S(2)}, u32[]{:S(2)}) %collective-permute-start.33) | collective-permute-done | bytes 1048608 | tf_op jit(solution)/shard_map/ppermute | solution.py:16
  205.4 8.9 %fusion.8 = f32[2048,768]{1,0:T(8,128)} fusion(bf16[2048,2048]{1,0:T(8,128)(2,1)S(1)} %constant_dynamic-update-slice_fusion.31, bf16[1536,2048]{1,0:T(8,128)(2,1)S(1)} %bitcast.167, s32[]{:T(128)S(6)} %select_n.288), kind=kOutput, calls=%fused_computation.15 | convolution fusion | flops 6442450944 | bytes 17825796 | tf_op jit(solution)/shard_map/dot_general | solution.py:132
  214.4 3.3 collective-permute-done.17
  224.8 3.3 fusion.50
  256.0 3.0 fusion.88
  259.2 3.2 convolution_add_fusion
  268.9 3.6 collective-permute-done.24
  285.6 3.3 collective-permute-done.40
  292.4 2.9 collective-permute-done.36
  302.7 3.1 collective-permute-done.22
  309.8 22.1 %collective-permute-done.55 = bf16[256,2048]{1,0:T(8,128)(2,1)S(1)} collective-permute-done((bf16[256,2048]{1,0:T(8,128)(2,1)S(1)}, bf16[256,2048]{1,0:T(8,128)(2,1)S(1)}, u32[]{:S(2)}, u32[]{:S(2)}) %collective-permute-start.55) | collective-permute-done | bytes 1048608 | tf_op jit(solution)/shard_map/ppermute | solution.py:16
  332.0 7.2 %collective-permute-done.41 = bf16[256,1024]{1,0:T(8,128)(2,1)S(1)} collective-permute-done((bf16[256,1024]{1,0:T(8,128)(2,1)S(1)}, bf16[256,1024]{1,0:T(8,128)(2,1)S(1)}, u32[]{:S(2)}, u32[]{:S(2)}) %collective-permute-start.41) | collective-permute-done | bytes 524320 | tf_op jit(solution)/shard_map/ppermute | solution.py:16
  342.7 6.4 %fusion.24 = f32[2048,512]{1,0:T(8,128)} fusion(bf16[2048,2048]{1,0:T(8,128)(2,1)S(1)} %constant_dynamic-update-slice_fusion.1, bf16[2048,1024]{1,0:T(8,128)(2,1)S(1)} %constant_dynamic-update-slice_fusion.11), kind=kOutput, calls=%fused_computation.43 | convolution fusion | flops 4294967296 | bytes 14680064 | tf_op jit(solution)/shard_map/dot_general | solution.py:136
  349.0 4.7 collective-permute-done.45
  355.2 8.7 %fusion.4 = f32[2048,768]{1,0:T(8,128)} fusion(bf16[2048,2048]{1,0:T(8,128)(2,1)S(1)} %constant_dynamic-update-slice_fusion.21, bf16[2048,1536]{1,0:T(8,128)(2,1)S(1)} %bitcast.171, s32[]{:T(128)S(6)} %select_n.288), kind=kOutput, calls=%fused_computation.11 | convolution fusion | flops 6442450944 | bytes 17825796 | tf_op jit(solution)/shard_map/dot_general | solution.py:128
  364.0 8.6 %fusion.6 = f32[2048,768]{1,0:T(8,128)} fusion(bf16[2048,2048]{1,0:T(8,128)(2,1)S(1)} %constant_dynamic-update-slice_fusion.21, bf16[2048,1536]{1,0:T(8,128)(2,1)S(1)} %bitcast.175, s32[]{:T(128)S(6)} %select_n.288), kind=kOutput, calls=%fused_computation.13 | convolution fusion | flops 6442450944 | bytes 17825796 | tf_op jit(solution)/shard_map/dot_general | solution.py:128
  372.6 16.0 %fusion.80 = (bf16[2048,768]{0,1:T(8,128)(2,1)}, f32[2048,768]{0,1:T(8,128)S(1)}) fusion(bf16[2048,2048]{1,0:T(8,128)(2,1)} %copy-done.57, f32[2048,768]{1,0:T(8,128)} %fusion.4, f32[2048,768]{1,0:T(8,128)} %fusion.8, f32[2048,768]{1,0:T(8,128)} %fusion.6), kind=kOutput, calls=%fused_computation.265 | convolution fusion | flops 6459752448 | bytes 36700160 | tf_op jit(solution)/shard_map/dot_general | solution.py:136
  390.1 15.2 %fusion.81 = (bf16[2048,768]{0,1:T(8,128)(2,1)}, f32[2048,768]{0,1:T(8,128)}) fusion(bf16[2048,2048]{1,0:T(8,128)(2,1)} %copy-done.57, f32[2048,768]{1,0:T(8,128)} %fusion.8, f32[2048,768]{1,0:T(8,128)} %fusion.4), kind=kOutput, calls=%fused_computation.266 | convolution fusion | flops 6453460992 | bytes 30408704 | tf_op jit(solution)/shard_map/dot_general | solution.py:136
  407.6 14.7 %fusion.82 = (bf16[768,2048]{1,0:T(8,128)(2,1)}, f32[768,2048]{1,0:T(8,128)}) fusion(bf16[2048,2048]{1,0:T(8,128)(2,1)} %copy-done.56, f32[2048,768]{1,0:T(8,128)} %fusion.6, f32[2048,768]{1,0:T(8,128)} %fusion.4), kind=kOutput, calls=%fused_computation.267 | convolution fusion | flops 6453460992 | bytes 30408704 | tf_op jit(solution)/shard_map/dot_general | solution.py:136
  423.2 7.6 %fusion.35 = f32[2048,256]{1,0:T(8,128)} fusion(bf16[2048,2048]{1,0:T(8,128)(2,1)} %copy-done.58, bf16[2048,1024]{1,0:T(8,128)(2,1)S(1)} %constant_dynamic-update-slice_fusion.11), kind=kOutput, calls=%fused_computation.70 | convolution fusion | flops 2147483648 | bytes 11534336 | tf_op jit(solution)/shard_map/dot_general | solution.py:136
  430.8 4.0 fusion.37
  434.8 2.9 fusion.26
  438.5 5.9 %maximum_select_fusion = f32[2048,1536]{0,1:T(8,128)} fusion(f32[2048,768]{0,1:T(8,128)S(1)} %convert_element_type.330, f32[2048,768]{0,1:T(8,128)S(1)} %get-tuple-element.126, pred[]{:T(512)S(6)} %eq.40), kind=kLoop, calls=%fused_computation.1 | loop fusion | flops 9437184 | bytes 25165824 | tf_op jit(solution)/shard_map/jit(_where)/select_n | solution.py:341
  444.4 12.6 %copy.86 = f32[2048,1536]{1,0:T(8,128)} copy(f32[2048,1536]{0,1:T(8,128)} %maximum_select_fusion) | data formatting | bytes 25165824
  457.0 2.7 convert_element_type.333
  459.7 10.5 %maximum_select_fusion.1 = f32[2048,1536]{0,1:T(8,128)} fusion(f32[2048,768]{0,1:T(8,128)S(1)} %convert_element_type.333, f32[2048,768]{0,1:T(8,128)} %get-tuple-element.128, pred[]{:T(512)S(6)} %eq.40), kind=kLoop, calls=%fused_computation.2 | loop fusion | flops 9437184 | bytes 25165824 | tf_op jit(solution)/shard_map/jit(_where)/select_n | solution.py:341
  470.2 12.6 %copy.87 = f32[2048,1536]{1,0:T(8,128)} copy(f32[2048,1536]{0,1:T(8,128)} %maximum_select_fusion.1) | data formatting | bytes 25165824
  482.8 2.7 convert_element_type.336
  485.5 10.5 %maximum_select_fusion.2 = f32[1536,2048]{1,0:T(8,128)} fusion(f32[768,2048]{1,0:T(8,128)S(1)} %convert_element_type.336, f32[768,2048]{1,0:T(8,128)} %get-tuple-element.130, pred[]{:T(512)S(6)} %eq.40), kind=kLoop, calls=%fused_computation.3 | loop fusion | flops 9437184 | bytes 25165824 | tf_op jit(solution)/shard_map/jit(_where)/select_n | solution.py:341
  (491 shorter events, 164.5 us)
Async XLA Ops:
  0.7 17.9 %collective-permute-start = (bf16[256,512]{1,0:T(8,128)(2,1)}, bf16[256,512]{1,0:T(8,128)(2,1)S(1)}, u32[]{:S(2)}, u32[]{:S(2)}) collective-permute-start(bf16[256,512]{1,0:T(8,128)(2,1)} %param.15), channel_id=1, source_target_pairs={{0,2},{1,3},{2,0},{3,1},{4,6},{5,7},{6,4},{7,5},{8,10},{9,11},{10,... | collective-permute-start | bytes 786440 | tf_op jit(solution)/shard_map/ppermute | solution.py:16
  4.8 18.4 %collective-permute-start.2 = (bf16[256,512]{1,0:T(8,128)(2,1)}, bf16[256,512]{1,0:T(8,128)(2,1)S(1)}, u32[]{:S(2)}, u32[]{:S(2)}) collective-permute-start(bf16[256,512]{1,0:T(8,128)(2,1)} %param.15), channel_id=1, source_target_pairs={{0,1},{1,0},{2,3},{3,2},{4,5},{5,4},{6,7},{7,6},{8,9},{9,8},{10,11... | collective-permute-start | bytes 786440 | tf_op jit(solution)/shard_map/ppermute | solution.py:16
  8.8 51.9 %collective-permute-start.62 = (bf16[128,2048]{1,0:T(8,128)(2,1)}, bf16[128,2048]{1,0:T(8,128)(2,1)}, u32[]{:S(2)}, u32[]{:S(2)}) collective-permute-start(bf16[128,2048]{1,0:T(8,128)(2,1)} %get-tuple-element.64), channel_id=1, source_target_pairs={{0,4},{4,0},{1,5},{5,1},{2,6},{6,2},{3,7},{7,3},{8,12},{12,8},{9,1... | collective-permute-start | bytes 1572872 | tf_op jit(solution)/shard_map/ppermute | solution.py:16
  10.3 46.9 %collective-permute-start.58 = (bf16[128,2048]{1,0:T(8,128)(2,1)}, bf16[128,2048]{1,0:T(8,128)(2,1)}, u32[]{:S(2)}, u32[]{:S(2)}) collective-permute-start(bf16[128,2048]{1,0:T(8,128)(2,1)} %get-tuple-element.66), channel_id=1, source_target_pairs={{0,16},{8,24},{16,0},{24,8},{1,17},{9,25},{17,1},{25,9},{2,18},{10... | collective-permute-start | bytes 1572872 | tf_op jit(solution)/shard_map/ppermute | solution.py:16
  30.7 14.5 %collective-permute-start.3 = (bf16[256,512]{0,1:T(8,128)(2,1)}, bf16[256,512]{0,1:T(8,128)(2,1)}, u32[]{:S(2)}, u32[]{:S(2)}) collective-permute-start(bf16[256,512]{0,1:T(8,128)(2,1)} %pad_maximum_fusion.14), channel_id=1, source_target_pairs={{0,4},{4,0},{1,5},{5,1},{2,6},{6,2},{3,7},{7,3},{8,12},{12,8},{9,1... | collective-permute-start | bytes 786440 | tf_op jit(solution)/shard_map/ppermute | solution.py:16
  58.5 41.1 %collective-permute-start.60 = (bf16[256,2048]{1,0:T(8,128)(2,1)S(1)}, bf16[256,2048]{1,0:T(8,128)(2,1)S(1)}, u32[]{:S(2)}, u32[]{:S(2)}) collective-permute-start(bf16[256,2048]{1,0:T(8,128)(2,1)S(1)} %pad_maximum_fusion.7), channel_id=1, source_target_pairs={{0,8},{8,0},{16,24},{24,16},{1,9},{9,1},{17,25},{25,17},{2,10},{10... | collective-permute-start | bytes 3145736 | tf_op jit(solution)/shard_map/ppermute | solution.py:16
  58.6 38.0 %collective-permute-start.59 = (bf16[256,2048]{1,0:T(8,128)(2,1)S(1)}, bf16[256,2048]{1,0:T(8,128)(2,1)S(1)}, u32[]{:S(2)}, u32[]{:S(2)}) collective-permute-start(bf16[256,2048]{1,0:T(8,128)(2,1)S(1)} %pad_maximum_fusion.7), channel_id=1, source_target_pairs={{0,4},{4,0},{1,5},{5,1},{2,6},{6,2},{3,7},{7,3},{8,12},{12,8},{9,1... | collective-permute-start | bytes 3145736 | tf_op jit(solution)/shard_map/ppermute | solution.py:16
  59.3 14.0 %collective-permute-start.28 = (bf16[128,2048]{1,0:T(8,128)(2,1)S(1)}, bf16[128,2048]{1,0:T(8,128)(2,1)S(1)}, u32[]{:S(2)}, u32[]{:S(2)}) collective-permute-start(bf16[128,2048]{1,0:T(8,128)(2,1)S(1)} %copy-done.27), channel_id=1, source_target_pairs={{0,16},{8,24},{16,0},{24,8},{1,17},{9,25},{17,1},{25,9},{2,18},{10... | collective-permute-start | bytes 1572872 | tf_op jit(solution)/shard_map/ppermute | solution.py:16
  61.9 13.8 %collective-permute-start.4 = (bf16[256,512]{1,0:T(8,128)(2,1)S(1)}, bf16[256,512]{1,0:T(8,128)(2,1)S(1)}, u32[]{:S(2)}, u32[]{:S(2)}) collective-permute-start(bf16[256,512]{1,0:T(8,128)(2,1)S(1)} %get-tuple-element.87), channel_id=1, source_target_pairs={{0,1},{1,0},{2,3},{3,2},{4,5},{5,4},{6,7},{7,6},{8,9},{9,8},{10,11... | collective-permute-start | bytes 786440 | tf_op jit(solution)/shard_map/ppermute | solution.py:16
  73.3 22.1 %collective-permute-start.32 = (bf16[128,2048]{1,0:T(8,128)(2,1)S(1)}, bf16[128,2048]{1,0:T(8,128)(2,1)S(1)}, u32[]{:S(2)}, u32[]{:S(2)}) collective-permute-start(bf16[128,2048]{1,0:T(8,128)(2,1)S(1)} %copy-done.26), channel_id=1, source_target_pairs={{0,4},{4,0},{1,5},{5,1},{2,6},{6,2},{3,7},{7,3},{8,12},{12,8},{9,1... | collective-permute-start | bytes 1572872 | tf_op jit(solution)/shard_map/ppermute | solution.py:16
  75.7 101.5 %collective-permute-start.63 = (bf16[256,2048]{1,0:T(8,128)(2,1)S(1)}, bf16[256,2048]{1,0:T(8,128)(2,1)S(1)}, u32[]{:S(2)}, u32[]{:S(2)}) collective-permute-start(bf16[256,2048]{1,0:T(8,128)(2,1)S(1)} %pad_maximum_fusion.8), channel_id=1, source_target_pairs={{0,16},{8,24},{16,0},{24,8},{1,17},{9,25},{17,1},{25,9},{2,18},{10... | collective-permute-start | bytes 3145736 | tf_op jit(solution)/shard_map/ppermute | solution.py:16
  76.5 20.7 %collective-permute-start.7 = (bf16[256,512]{1,0:T(8,128)(2,1)S(1)}, bf16[256,512]{1,0:T(8,128)(2,1)S(1)}, u32[]{:S(2)}, u32[]{:S(2)}) collective-permute-start(bf16[256,512]{1,0:T(8,128)(2,1)S(1)} %add_convert_fusion.8), channel_id=1, source_target_pairs={{0,2},{1,3},{2,0},{3,1},{4,6},{5,7},{6,4},{7,5},{8,10},{9,11},{10,... | collective-permute-start | bytes 786440 | tf_op jit(solution)/shard_map/ppermute | solution.py:16
  95.4 65.8 %collective-permute-start.30 = (bf16[256,2048]{1,0:T(8,128)(2,1)S(1)}, bf16[256,2048]{1,0:T(8,128)(2,1)S(1)}, u32[]{:S(2)}, u32[]{:S(2)}) collective-permute-start(bf16[256,2048]{1,0:T(8,128)(2,1)S(1)} %pad_maximum_fusion.3), channel_id=1, source_target_pairs={{0,8},{8,0},{16,24},{24,16},{1,9},{9,1},{17,25},{25,17},{2,10},{10... | collective-permute-start | bytes 3145736 | tf_op jit(solution)/shard_map/ppermute | solution.py:16
  97.2 13.6 %collective-permute-start.8 = (bf16[256,512]{1,0:T(8,128)(2,1)S(1)}, bf16[256,512]{1,0:T(8,128)(2,1)S(1)}, u32[]{:S(2)}, u32[]{:S(2)}) collective-permute-start(bf16[256,512]{1,0:T(8,128)(2,1)S(1)} %collective-permute-done.7), channel_id=1, source_target_pairs={{0,1},{1,0},{2,3},{3,2},{4,5},{5,4},{6,7},{7,6},{8,9},{9,8},{10,11... | collective-permute-start | bytes 786440 | tf_op jit(solution)/shard_map/ppermute | solution.py:16
  99.6 32.2 %collective-permute-start.29 = (bf16[256,2048]{1,0:T(8,128)(2,1)S(1)}, bf16[256,2048]{1,0:T(8,128)(2,1)}, u32[]{:S(2)}, u32[]{:S(2)}) collective-permute-start(bf16[256,2048]{1,0:T(8,128)(2,1)S(1)} %pad_maximum_fusion.3), channel_id=1, source_target_pairs={{0,4},{4,0},{1,5},{5,1},{2,6},{6,2},{3,7},{7,3},{8,12},{12,8},{9,1... | collective-permute-start | bytes 3145736 | tf_op jit(solution)/shard_map/ppermute | solution.py:16
  130.4 39.8 %collective-permute-start.13 = (bf16[256,512]{1,0:T(8,128)(2,1)S(1)}, bf16[256,512]{1,0:T(8,128)(2,1)S(1)}, u32[]{:S(2)}, u32[]{:S(2)}) collective-permute-start(bf16[256,512]{1,0:T(8,128)(2,1)S(1)} %get-tuple-element.79), channel_id=1, source_target_pairs={{0,1},{1,0},{2,3},{3,2},{4,5},{5,4},{6,7},{7,6},{8,9},{9,8},{10,11... | collective-permute-start | bytes 786440 | tf_op jit(solution)/shard_map/ppermute | solution.py:16
  131.9 18.3 %collective-permute-start.14 = (bf16[256,512]{1,0:T(8,128)(2,1)S(1)}, bf16[256,512]{1,0:T(8,128)(2,1)S(1)}, u32[]{:S(2)}, u32[]{:S(2)}) collective-permute-start(bf16[256,512]{1,0:T(8,128)(2,1)S(1)} %get-tuple-element.80), channel_id=1, source_target_pairs={{0,1},{1,0},{2,3},{3,2},{4,5},{5,4},{6,7},{7,6},{8,9},{9,8},{10,11... | collective-permute-start | bytes 786440 | tf_op jit(solution)/shard_map/ppermute | solution.py:16
  138.9 20.8 %collective-permute-start.10 = (bf16[256,512]{1,0:T(8,128)(2,1)S(1)}, bf16[256,512]{1,0:T(8,128)(2,1)S(1)}, u32[]{:S(2)}, u32[]{:S(2)}) collective-permute-start(bf16[256,512]{1,0:T(8,128)(2,1)S(1)} %get-tuple-element.81), channel_id=1, source_target_pairs={{0,1},{1,0},{2,3},{3,2},{4,5},{5,4},{6,7},{7,6},{8,9},{9,8},{10,11... | collective-permute-start | bytes 786440 | tf_op jit(solution)/shard_map/ppermute | solution.py:16
  150.2 19.3 %collective-permute-start.12 = (bf16[256,512]{1,0:T(8,128)(2,1)S(1)}, bf16[256,512]{1,0:T(8,128)(2,1)S(1)}, u32[]{:S(2)}, u32[]{:S(2)}) collective-permute-start(bf16[256,512]{1,0:T(8,128)(2,1)S(1)} %add_convert_fusion.7), channel_id=1, source_target_pairs={{0,2},{1,3},{2,0},{3,1},{4,6},{5,7},{6,4},{7,5},{8,10},{9,11},{10,... | collective-permute-start | bytes 786440 | tf_op jit(solution)/shard_map/ppermute | solution.py:16
  159.7 15.6 %collective-permute-start.50 = (bf16[128,2048]{1,0:T(8,128)(2,1)S(1)}, bf16[128,2048]{1,0:T(8,128)(2,1)S(1)}, u32[]{:S(2)}, u32[]{:S(2)}) collective-permute-start(bf16[128,2048]{1,0:T(8,128)(2,1)S(1)} %get-tuple-element.69), channel_id=1, source_target_pairs={{0,16},{8,24},{16,0},{24,8},{1,17},{9,25},{17,1},{25,9},{2,18},{10... | collective-permute-start | bytes 1572872 | tf_op jit(solution)/shard_map/ppermute | solution.py:16
  169.4 19.9 %collective-permute-start.61 = (bf16[256,2048]{1,0:T(8,128)(2,1)S(1)}, bf16[256,2048]{1,0:T(8,128)(2,1)S(1)}, u32[]{:S(2)}, u32[]{:S(2)}) collective-permute-start(bf16[256,2048]{1,0:T(8,128)(2,1)S(1)} %collective-permute-done.59), channel_id=1, source_target_pairs={{0,8},{8,0},{16,24},{24,16},{1,9},{9,1},{17,25},{25,17},{2,10},{10... | collective-permute-start | bytes 3145736 | tf_op jit(solution)/shard_map/ppermute | solution.py:16
  170.3 20.4 %collective-permute-start.64 = (bf16[256,2048]{1,0:T(8,128)(2,1)S(1)}, bf16[256,2048]{1,0:T(8,128)(2,1)S(1)}, u32[]{:S(2)}, u32[]{:S(2)}) collective-permute-start(bf16[256,2048]{1,0:T(8,128)(2,1)S(1)} %pad_maximum_fusion.8), channel_id=1, source_target_pairs={{0,8},{8,0},{16,24},{24,16},{1,9},{9,1},{17,25},{25,17},{2,10},{10... | collective-permute-start | bytes 3145736 | tf_op jit(solution)/shard_map/ppermute | solution.py:16
  174.7 13.6 %collective-permute-start.54 = (bf16[128,2048]{1,0:T(8,128)(2,1)S(1)}, bf16[128,2048]{1,0:T(8,128)(2,1)S(1)}, u32[]{:S(2)}, u32[]{:S(2)}) collective-permute-start(bf16[128,2048]{1,0:T(8,128)(2,1)S(1)} %get-tuple-element.67), channel_id=1, source_target_pairs={{0,4},{4,0},{1,5},{5,1},{2,6},{6,2},{3,7},{7,3},{8,12},{12,8},{9,1... | collective-permute-start | bytes 1572872 | tf_op jit(solution)/shard_map/ppermute | solution.py:16
  175.3 99.3 %collective-permute-start.34 = (bf16[256,2048]{1,0:T(8,128)(2,1)}, bf16[256,2048]{1,0:T(8,128)(2,1)}, u32[]{:S(2)}, u32[]{:S(2)}) collective-permute-start(bf16[256,2048]{1,0:T(8,128)(2,1)} %pad_maximum_fusion.4), channel_id=1, source_target_pairs={{0,8},{8,0},{16,24},{24,16},{1,9},{9,1},{17,25},{25,17},{2,10},{10... | collective-permute-start | bytes 3145736 | tf_op jit(solution)/shard_map/ppermute | solution.py:16
  177.2 25.9 %collective-permute-start.33 = (bf16[256,2048]{1,0:T(8,128)(2,1)}, bf16[256,2048]{1,0:T(8,128)(2,1)}, u32[]{:S(2)}, u32[]{:S(2)}) collective-permute-start(bf16[256,2048]{1,0:T(8,128)(2,1)} %pad_maximum_fusion.4), channel_id=1, source_target_pairs={{0,16},{8,24},{16,0},{24,8},{1,17},{9,25},{17,1},{25,9},{2,18},{10... | collective-permute-start | bytes 3145736 | tf_op jit(solution)/shard_map/ppermute | solution.py:16
  188.2 15.1 %collective-permute-start.65 = (bf16[256,2048]{1,0:T(8,128)(2,1)S(1)}, bf16[256,2048]{1,0:T(8,128)(2,1)S(1)}, u32[]{:S(2)}, u32[]{:S(2)}) collective-permute-start(bf16[256,2048]{1,0:T(8,128)(2,1)S(1)} %collective-permute-done.63), channel_id=1, source_target_pairs={{0,8},{8,0},{16,24},{24,16},{1,9},{9,1},{17,25},{25,17},{2,10},{10... | collective-permute-start | bytes 3145736 | tf_op jit(solution)/shard_map/ppermute | solution.py:16
  189.3 13.9 %collective-permute-start.16 = (bf16[256,512]{1,0:T(8,128)(2,1)S(1)}, bf16[256,512]{1,0:T(8,128)(2,1)S(1)}, u32[]{:S(2)}, u32[]{:S(2)}) collective-permute-start(bf16[256,512]{1,0:T(8,128)(2,1)S(1)} %add_convert_fusion.4), channel_id=1, source_target_pairs={{0,2},{1,3},{2,0},{3,1},{4,6},{5,7},{6,4},{7,5},{8,10},{9,11},{10,... | collective-permute-start | bytes 786440 | tf_op jit(solution)/shard_map/ppermute | solution.py:16
  190.7 73.3 %collective-permute-start.31 = (bf16[256,2048]{1,0:T(8,128)(2,1)}, bf16[256,2048]{1,0:T(8,128)(2,1)}, u32[]{:S(2)}, u32[]{:S(2)}) collective-permute-start(bf16[256,2048]{1,0:T(8,128)(2,1)} %collective-permute-done.29), channel_id=1, source_target_pairs={{0,8},{8,0},{16,24},{24,16},{1,9},{9,1},{17,25},{25,17},{2,10},{10... | collective-permute-start | bytes 3145736 | tf_op jit(solution)/shard_map/ppermute | solution.py:16
  203.1 75.6 %collective-permute-start.35 = (bf16[256,2048]{1,0:T(8,128)(2,1)}, bf16[256,2048]{1,0:T(8,128)(2,1)}, u32[]{:S(2)}, u32[]{:S(2)}) collective-permute-start(bf16[256,2048]{1,0:T(8,128)(2,1)} %collective-permute-done.33), channel_id=1, source_target_pairs={{0,8},{8,0},{16,24},{24,16},{1,9},{9,1},{17,25},{25,17},{2,10},{10... | collective-permute-start | bytes 3145736 | tf_op jit(solution)/shard_map/ppermute | solution.py:16
  203.3 14.3 %collective-permute-start.17 = (bf16[256,512]{1,0:T(8,128)(2,1)S(1)}, bf16[256,512]{1,0:T(8,128)(2,1)S(1)}, u32[]{:S(2)}, u32[]{:S(2)}) collective-permute-start(bf16[256,512]{1,0:T(8,128)(2,1)S(1)} %collective-permute-done.16), channel_id=1, source_target_pairs={{0,1},{1,0},{2,3},{3,2},{4,5},{5,4},{6,7},{7,6},{8,9},{9,8},{10,11... | collective-permute-start | bytes 786440 | tf_op jit(solution)/shard_map/ppermute | solution.py:16
  214.4 86.4 %collective-permute-start.52 = (bf16[256,2048]{1,0:T(8,128)(2,1)}, bf16[256,2048]{1,0:T(8,128)(2,1)}, u32[]{:S(2)}, u32[]{:S(2)}) collective-permute-start(bf16[256,2048]{1,0:T(8,128)(2,1)} %pad_maximum_fusion.5), channel_id=1, source_target_pairs={{0,8},{8,0},{16,24},{24,16},{1,9},{9,1},{17,25},{25,17},{2,10},{10... | collective-permute-start | bytes 3145736 | tf_op jit(solution)/shard_map/ppermute | solution.py:16
  239.0 13.7 %collective-permute-start.19 = (bf16[256,512]{0,1:T(8,128)(2,1)}, bf16[256,512]{0,1:T(8,128)(2,1)}, u32[]{:S(2)}, u32[]{:S(2)}) collective-permute-start(bf16[256,512]{0,1:T(8,128)(2,1)} %fusion.47), channel_id=1, source_target_pairs={{0,4},{4,0},{1,5},{5,1},{2,6},{6,2},{3,7},{7,3},{8,12},{12,8},{9,1... | collective-permute-start | bytes 786440 | tf_op jit(solution)/shard_map/ppermute | solution.py:16
  252.6 45.2 %collective-permute-start.51 = (bf16[256,2048]{1,0:T(8,128)(2,1)}, bf16[256,2048]{1,0:T(8,128)(2,1)}, u32[]{:S(2)}, u32[]{:S(2)}) collective-permute-start(bf16[256,2048]{1,0:T(8,128)(2,1)} %pad_maximum_fusion.5), channel_id=1, source_target_pairs={{0,4},{4,0},{1,5},{5,1},{2,6},{6,2},{3,7},{7,3},{8,12},{12,8},{9,1... | collective-permute-start | bytes 3145736 | tf_op jit(solution)/shard_map/ppermute | solution.py:16
  274.1 34.9 %collective-permute-start.44 = (bf16[256,2048]{1,0:T(8,128)(2,1)S(1)}, bf16[256,2048]{1,0:T(8,128)(2,1)S(1)}, u32[]{:S(2)}, u32[]{:S(2)}) collective-permute-start(bf16[256,2048]{1,0:T(8,128)(2,1)S(1)} %copy-done.38), channel_id=1, source_target_pairs={{0,8},{8,0},{16,24},{24,16},{1,9},{9,1},{17,25},{25,17},{2,10},{10... | collective-permute-start | bytes 3145736 | tf_op jit(solution)/shard_map/ppermute | solution.py:16
  302.3 52.6 %collective-permute-start.56 = (bf16[256,2048]{1,0:T(8,128)(2,1)S(1)}, bf16[256,2048]{1,0:T(8,128)(2,1)S(1)}, u32[]{:S(2)}, u32[]{:S(2)}) collective-permute-start(bf16[256,2048]{1,0:T(8,128)(2,1)S(1)} %copy-done.41), channel_id=1, source_target_pairs={{0,8},{8,0},{16,24},{24,16},{1,9},{9,1},{17,25},{25,17},{2,10},{10... | collective-permute-start | bytes 3145736 | tf_op jit(solution)/shard_map/ppermute | solution.py:16
  305.9 26.1 %collective-permute-start.55 = (bf16[256,2048]{1,0:T(8,128)(2,1)S(1)}, bf16[256,2048]{1,0:T(8,128)(2,1)S(1)}, u32[]{:S(2)}, u32[]{:S(2)}) collective-permute-start(bf16[256,2048]{1,0:T(8,128)(2,1)S(1)} %copy-done.41), channel_id=1, source_target_pairs={{0,16},{8,24},{16,0},{24,8},{1,17},{9,25},{17,1},{25,9},{2,18},{10... | collective-permute-start | bytes 3145736 | tf_op jit(solution)/shard_map/ppermute | solution.py:16
  308.5 31.3 %collective-permute-start.42 = (bf16[256,1024]{1,0:T(8,128)(2,1)S(1)}, bf16[256,1024]{1,0:T(8,128)(2,1)S(1)}, u32[]{:S(2)}, u32[]{:S(2)}) collective-permute-start(bf16[256,1024]{1,0:T(8,128)(2,1)S(1)} %pad_maximum_fusion.13), channel_id=1, source_target_pairs={{0,8},{8,0},{16,24},{24,16},{1,9},{9,1},{17,25},{25,17},{2,10},{10... | collective-permute-start | bytes 1572872 | tf_op jit(solution)/shard_map/ppermute | solution.py:16
  308.6 30.6 %collective-permute-start.41 = (bf16[256,1024]{1,0:T(8,128)(2,1)S(1)}, bf16[256,1024]{1,0:T(8,128)(2,1)S(1)}, u32[]{:S(2)}, u32[]{:S(2)}) collective-permute-start(bf16[256,1024]{1,0:T(8,128)(2,1)S(1)} %pad_maximum_fusion.13), channel_id=1, source_target_pairs={{0,16},{8,24},{16,0},{24,8},{1,17},{9,25},{17,1},{25,9},{2,18},{10... | collective-permute-start | bytes 1572872 | tf_op jit(solution)/shard_map/ppermute | solution.py:16
  309.1 30.1 %collective-permute-start.39 = (bf16[256,1024]{1,0:T(8,128)(2,1)S(1)}, bf16[256,1024]{1,0:T(8,128)(2,1)S(1)}, u32[]{:S(2)}, u32[]{:S(2)}) collective-permute-start(bf16[256,1024]{1,0:T(8,128)(2,1)S(1)} %collective-permute-done.37), channel_id=1, source_target_pairs={{0,8},{8,0},{16,24},{24,16},{1,9},{9,1},{17,25},{25,17},{2,10},{10... | collective-permute-start | bytes 1572872 | tf_op jit(solution)/shard_map/ppermute | solution.py:16
  332.0 22.6 %collective-permute-start.53 = (bf16[256,2048]{1,0:T(8,128)(2,1)}, bf16[256,2048]{1,0:T(8,128)(2,1)S(1)}, u32[]{:S(2)}, u32[]{:S(2)}) collective-permute-start(bf16[256,2048]{1,0:T(8,128)(2,1)} %collective-permute-done.51), channel_id=1, source_target_pairs={{0,8},{8,0},{16,24},{24,16},{1,9},{9,1},{17,25},{25,17},{2,10},{10... | collective-permute-start | bytes 3145736 | tf_op jit(solution)/shard_map/ppermute | solution.py:16
  339.2 15.8 %collective-permute-start.57 = (bf16[256,2048]{1,0:T(8,128)(2,1)S(1)}, bf16[256,2048]{1,0:T(8,128)(2,1)S(1)}, u32[]{:S(2)}, u32[]{:S(2)}) collective-permute-start(bf16[256,2048]{1,0:T(8,128)(2,1)S(1)} %collective-permute-done.55), channel_id=1, source_target_pairs={{0,8},{8,0},{16,24},{24,16},{1,9},{9,1},{17,25},{25,17},{2,10},{10... | collective-permute-start | bytes 3145736 | tf_op jit(solution)/shard_map/ppermute | solution.py:16
  339.9 13.9 %collective-permute-start.45 = (bf16[128,2048]{1,0:T(8,128)(2,1)S(1)}, bf16[128,2048]{1,0:T(8,128)(2,1)S(1)}, u32[]{:S(2)}, u32[]{:S(2)}) collective-permute-start(bf16[128,2048]{1,0:T(8,128)(2,1)S(1)} %constant_dynamic-slice_fusion.1), channel_id=1, source_target_pairs={{0,16},{8,24},{16,0},{24,8},{1,17},{9,25},{17,1},{25,9},{2,18},{10... | collective-permute-start | bytes 1572872 | tf_op jit(solution)/shard_map/ppermute | solution.py:16
  353.9 34.6 %collective-permute-start.46 = (bf16[64,2048]{1,0:T(8,128)(2,1)S(1)}, bf16[64,2048]{1,0:T(8,128)(2,1)S(1)}, u32[]{:S(2)}, u32[]{:S(2)}) collective-permute-start(bf16[64,2048]{1,0:T(8,128)(2,1)S(1)} %constant_dynamic-slice_fusion), channel_id=1, source_target_pairs={{0,4},{4,0},{1,5},{5,1},{2,6},{6,2},{3,7},{7,3},{8,12},{12,8},{9,1... | collective-permute-start | bytes 786440 | tf_op jit(solution)/shard_map/ppermute | solution.py:16
  388.6 17.3 %collective-permute-start.47 = (bf16[64,2048]{1,0:T(8,128)(2,1)S(1)}, bf16[64,2048]{1,0:T(8,128)(2,1)S(1)}, u32[]{:S(2)}, u32[]{:S(2)}) collective-permute-start(bf16[64,2048]{1,0:T(8,128)(2,1)S(1)} %add_convert_fusion.2), channel_id=1, source_target_pairs={{0,4},{4,0},{1,5},{5,1},{2,6},{6,2},{3,7},{7,3},{8,12},{12,8},{9,1... | collective-permute-start | bytes 786440 | tf_op jit(solution)/shard_map/ppermute | solution.py:16
  405.4 32.3 %collective-permute-start.66 = (bf16[2048,768]{0,1:T(8,128)(2,1)S(1)}, bf16[2048,768]{0,1:T(8,128)(2,1)S(1)}, u32[]{:S(2)}, u32[]{:S(2)}) collective-permute-start(bf16[2048,768]{0,1:T(8,128)(2,1)S(1)} %copy-done.76), channel_id=1, source_target_pairs={{0,8},{8,0},{16,24},{24,16},{1,9},{9,1},{17,25},{25,17},{2,10},{10... | collective-permute-start | bytes 9437192 | tf_op jit(solution)/shard_map/ppermute | solution.py:16
  405.4 51.6 %collective-permute-start.67 = (bf16[2048,768]{0,1:T(8,128)(2,1)}, bf16[2048,768]{0,1:T(8,128)(2,1)}, u32[]{:S(2)}, u32[]{:S(2)}) collective-permute-start(bf16[2048,768]{0,1:T(8,128)(2,1)} %get-tuple-element.127), channel_id=1, source_target_pairs={{0,8},{8,0},{16,24},{24,16},{1,9},{9,1},{17,25},{25,17},{2,10},{10... | collective-permute-start | bytes 9437192 | tf_op jit(solution)/shard_map/ppermute | solution.py:16
  406.0 16.3 %collective-permute-start.48 = (bf16[128,2048]{1,0:T(8,128)(2,1)S(1)}, bf16[128,2048]{1,0:T(8,128)(2,1)S(1)}, u32[]{:S(2)}, u32[]{:S(2)}) collective-permute-start(bf16[128,2048]{1,0:T(8,128)(2,1)S(1)} %maximum_select_fusion.5), channel_id=1, source_target_pairs={{0,16},{8,24},{16,0},{24,8},{1,17},{9,25},{17,1},{25,9},{2,18},{10... | collective-permute-start | bytes 1572872 | tf_op jit(solution)/shard_map/ppermute | solution.py:16
  422.3 60.5 %collective-permute-start.68 = (bf16[768,2048]{1,0:T(8,128)(2,1)}, bf16[768,2048]{1,0:T(8,128)(2,1)}, u32[]{:S(2)}, u32[]{:S(2)}) collective-permute-start(bf16[768,2048]{1,0:T(8,128)(2,1)} %get-tuple-element.129), channel_id=1, source_target_pairs={{0,8},{8,0},{16,24},{24,16},{1,9},{9,1},{17,25},{25,17},{2,10},{10... | collective-permute-start | bytes 9437192 | tf_op jit(solution)/shard_map/ppermute | solution.py:16
  (124 other events, 1059.3 us)

commit v2 on v1

v2 whole, which is shorter than its diff:
```python
import functools

import jax
import jax.numpy as jnp
from jax import lax
from jax.experimental import pallas as pl
from jax.experimental.pallas import tpu as pltpu
from jax.sharding import PartitionSpec as P

HD = 128
EPS = 1e-06
THETA = 1000000.0
NEG = -1e30
BF = jnp.bfloat16
F32 = jnp.float32
MIB = 1024 * 1024
VMEM_LIMIT = 63 * MIB + 900 * 1024
EXTRA = 16
SCALE = 1


def swap(value, axis, bit):
    size = lax.axis_size(axis)
    return lax.ppermute(value, axis, [(i, i ^ bit) for i in range(size)])


def bits_of(size):
    out = []
    bit = 1
    while bit < size:
        out.append(bit)
        bit *= 2
    return out


def gather_pieces(value, axis):
    pieces = {0: value}
    for bit in reversed(bits_of(lax.axis_size(axis))):
        for s in list(pieces):
            pieces[s | bit] = swap(pieces[s], axis, bit)
    return [pieces[s] for s in range(len(pieces))]


def send_pieces(pieces, axis):
    size = lax.axis_size(axis)
    return [
        lax.ppermute(pieces[s], axis, [(i, i ^ s) for i in range(size)])
        for s in sorted(range(1, size), key=lambda s: -s)
    ]


def send_all(value, axis):
    size = lax.axis_size(axis)
    pieces = {0: value}
    for s in range(size - 1, 0, -1):
        pieces[s] = lax.ppermute(value, axis, [(i, i ^ s) for i in range(size)])
    return [pieces[s] for s in range(size)]


def first_half(pieces, axis, *later):
    pieces = dict(enumerate(pieces))
    for s in [s for s in sorted(pieces, reverse=True) if not s & 1]:
        other = order_after(swap(pieces.pop(s | 1), axis, 1), *later)
        pieces[s] = (pieces[s].astype(F32) + other.astype(F32)).astype(BF if s else F32)
    return pieces


def second_half(pieces, axis, *earlier):
    for bit in bits_of(lax.axis_size(axis))[1:]:
        for s in [s for s in sorted(pieces, reverse=True) if not s & bit]:
            other = swap(order_after(pieces.pop(s | bit), *earlier), axis, bit)
            pieces[s] = (pieces[s].astype(F32) + other.astype(F32)).astype(BF if s else F32)
    return pieces[0]


def total_of(own, others):
    total = own.astype(F32)
    for other in others:
        total = total + other.astype(F32)
    return total


def far_masks():
    size = lax.axis_size("ctx")
    bits = [size * bit for bit in bits_of(lax.axis_size("dp")) if bit > 1] + bits_of(size)
    masks = [0]
    for bit in bits:
        masks = masks + [mask | bit for mask in masks]
    return masks


def send_plane(value, mask):
    if mask == 0:
        return value
    size = lax.axis_size("dp") * lax.axis_size("ctx")
    return lax.ppermute(value, ("dp", "ctx"), [(i, i ^ mask) for i in range(size)])


def plane_all(value):
    return lax.all_gather(value, ("dp", "ctx"), axis=0, tiled=True)


def sum_tensor(value):
    return lax.psum_scatter(value, "tensor", scatter_dimension=1, tiled=True)


def has_pair():
    return lax.axis_size("dp") > 1


def partners(parts, *earlier):
    if not has_pair():
        return []
    return [swap(order_after(part, *earlier), "dp", 1) for part in parts]


def order_after(value, *earlier):
    return lax.optimization_barrier((value, *earlier))[0] if earlier else value


def pieces_of(order, index, shard):
    return pl.multiple_of((index ^ order) * shard, shard)


def dot(left, right):
    return jnp.dot(left, right, preferred_element_type=F32)


def dot_nt(left, right):
    return lax.dot_general(left, right, (((1,), (1,)), ((), ())), preferred_element_type=F32)


def dot_tn(left, right):
    return lax.dot_general(left, right, (((0,), (0,)), ((), ())), preferred_element_type=F32)


def shape(*dims, dtype=BF):
    return jax.ShapeDtypeStruct(dims, dtype)


def size_of(arrays):
    return sum(a.size * a.dtype.itemsize for a in arrays)


def cost(flops, moved):
    return pl.CostEstimate(
        flops=int(flops) // SCALE, bytes_accessed=int(moved) // SCALE, transcendentals=0
    )


class Loads:
    def __init__(self, copies, buffers):
        self.copies = dict(enumerate(copies))
        self.buffers = buffers

    def __getitem__(self, index):
        if isinstance(index, slice):
            return [self[i] for i in range(*index.indices(len(self.buffers)))]
        if index in self.copies:
            self.copies.pop(index).wait()
        return self.buffers[index]

    def finish(self):
        for index in list(self.copies):
            self[index]


ANY = pl.BlockSpec(memory_space=pl.ANY)
SMEM = pl.BlockSpec(memory_space=pltpu.SMEM)


def kernel_call(body, ids, arrays, outs, flops, name, after=(), scratch=()):
    count, extra, results = len(arrays), len(after), len(outs)

    def run(ids, *refs):
        sources = refs[:count]
        out_refs = refs[count + extra : count + extra + results]
        buffers = refs[count + extra + results : 2 * count + extra + results]
        sems = refs[2 * count + extra + results]
        copies = [
            pltpu.make_async_copy(source, buffer, sems.at[i])
            for i, (source, buffer) in enumerate(zip(sources, buffers))
        ]
        for copy in copies:
            copy.start()
        loads = Loads(copies, buffers)
        body(ids, loads, *out_refs, *refs[2 * count + extra + results + 1 :])
        loads.finish()

    moved = size_of(arrays) + size_of(outs)
    return pl.pallas_call(
        run,
        out_shape=tuple(outs),
        in_specs=[SMEM] + [ANY] * (count + extra),
        out_specs=tuple(pl.BlockSpec(memory_space=pltpu.VMEM) for _ in outs),
        scratch_shapes=[pltpu.VMEM(a.shape, a.dtype) for a in arrays]
        + [pltpu.SemaphoreType.DMA((count,))]
        + [pltpu.VMEM(a.shape, a.dtype) for a in scratch],
        compiler_params=pltpu.CompilerParams(vmem_limit_bytes=VMEM_LIMIT),
        cost_estimate=cost(flops, moved),
        name=name,
    )(ids, *arrays, *after)


def turn(value):
    return pltpu.roll(value, HD // 2, 1)


def head_forward(raw, gain, cosine, sine):
    scale = lax.rsqrt(jnp.mean(raw * raw, axis=-1, keepdims=True) + EPS)
    normed = raw * scale * gain
    return normed * cosine + turn(normed) * sine


def head_backward(grad, raw, gain, cosine, sine):
    scale = lax.rsqrt(jnp.mean(raw * raw, axis=-1, keepdims=True) + EPS)
    unit = raw * scale
    grad_normed = grad * cosine + turn(grad * sine)
    grad_gain = jnp.sum(grad_normed * unit, axis=0, keepdims=True)
    inner = grad_normed * gain
    grad_raw = scale * (inner - unit * jnp.mean(inner * unit, axis=-1, keepdims=True))
    return grad_raw, grad_gain


def key_value_body(count, ids, loads, normed_ref, kv, raw_ref, inverse_ref):
    pieces = loads[:count]
    rows, shard = pieces[0].shape
    squares = 0.0
    for piece in pieces:
        x = piece[...].astype(F32)
        squares += jnp.sum(x * x, axis=-1, keepdims=True)
    inverse = lax.rsqrt(squares * (1.0 / (shard * count)) + EPS)
    inverse_ref[...] = inverse
    gain, key_gain, cosine, sine, wk, wv = loads[count : count + 6]
    kv_width = wk.shape[1]
    key_raw = jnp.zeros((rows, kv_width), F32)
    values = jnp.zeros((rows, kv_width), F32)
    for s in range(count):
        off = pieces_of(s, ids[0], shard)
        normed = (pieces[s][...].astype(F32) * inverse * gain[:, pl.ds(off, shard)]).astype(BF)
        normed_ref[:, pl.ds(off, shard)] = normed
        key_raw += dot(normed, wk[pl.ds(off, shard), :])
        values += dot(normed, wv[pl.ds(off, shard), :])
    raw_ref[...] = key_raw
    for h in range(kv_width // HD):
        cols = slice(h * HD, (h + 1) * HD)
        out = head_forward(key_raw[:, cols], key_gain[...], cosine[...], sine[...])
        kv[:, cols] = out.astype(BF)
    kv[:, kv_width:] = values.astype(BF)


def query_body(ids, loads, q_ref, raw_ref):
    normed, wq, query_gain, cosine, sine = loads[:5]
    raw = dot(normed[...], wq[...])
    raw_ref[...] = raw
    for h in range(wq.shape[1] // HD):
        cols = slice(h * HD, (h + 1) * HD)
        out = head_forward(raw[:, cols], query_gain[...], cosine[...], sine[...])
        q_ref[:, cols] = out.astype(BF)


def head_probs(ids, q, blocks, head, group, row_segment, key_segments):
    rows = q.shape[0]
    kv = head // group
    cols = slice(head * HD, (head + 1) * HD)
    row_index = ids[1] * rows + lax.broadcasted_iota(jnp.int32, (rows, rows), 0)
    parts = []
    for s, block in enumerate(blocks):
        scores = dot_nt(q[:, cols], block[:, kv * HD : (kv + 1) * HD]) * HD ** (-0.5)
        key_index = (ids[1] ^ s) * rows + lax.broadcasted_iota(jnp.int32, (rows, rows), 1)
        allowed = (row_segment[...] == key_segments[s][...]) & (key_index <= row_index)
        parts.append(jnp.where(allowed, scores, NEG))
    top = parts[0].max(axis=-1, keepdims=True)
    for part in parts[1:]:
        top = jnp.maximum(top, part.max(axis=-1, keepdims=True))
    parts = [jnp.exp(part - top) for part in parts]
    total = sum(jnp.sum(part, axis=-1, keepdims=True) for part in parts)
    share = 1.0 / total
    return [part * share for part in parts]


def attention_body(count, group, blocks, ids, loads, mixed_ref, *outs):
    q, row_segment = loads[:2]
    kvs = loads[2 : 2 + blocks]
    key_segments = loads[2 + blocks : 2 + 2 * blocks]
    kv_width = kvs[0].shape[1] // 2
    for h in range(q.shape[1] // HD):
        probs = head_probs(ids, q, kvs, h, group, row_segment, key_segments)
        start = kv_width + (h // group) * HD
        mixed = sum(
            dot(p.astype(BF), block[:, start : start + HD]) for p, block in zip(probs, kvs)
        )
        mixed_ref[:, h * HD : (h + 1) * HD] = mixed.astype(BF)
    wo = loads[2 + 2 * blocks]
    shard = wo.shape[1] // count
    for s in range(count):
        off = pieces_of(s, ids[0], shard)
        outs[s][...] = dot(mixed_ref[...], wo[:, pl.ds(off, shard)]).astype(BF)


def second_norm_body(count, ids, loads, normed_ref, resid_ref, inverse_ref):
    pieces = loads[:count]
    gain = loads[count]
    rows, shard = pieces[0].shape
    squares = 0.0
    for piece in pieces:
        x = piece[...].astype(F32)
        squares += jnp.sum(x * x, axis=-1, keepdims=True)
    inverse = lax.rsqrt(squares * (1.0 / (shard * count)) + EPS)
    inverse_ref[...] = inverse
    for s in range(count):
        off = pieces_of(s, ids[0], shard)
        cols = pl.ds(off, shard)
        x = pieces[s][...]
        resid_ref[:, cols] = x
        normed_ref[:, cols] = (x.astype(F32) * inverse * gain[:, cols]).astype(BF)


def gated_terms(gate, up, grad_hidden):
    sigmoid = jax.nn.sigmoid(gate)
    silu = gate * sigmoid
    grad_gate = grad_hidden * up * sigmoid * (1.0 + gate * (1.0 - sigmoid))
    return silu * up, grad_gate, grad_hidden * silu


def feed_forward_body(tile, extra, ids, normed_hbm, cot_hbm, wg_hbm, wu_hbm, wd_hbm, *refs):
    refs = refs[extra:]
    grad_out, feed_out, normed, cot, wg, wu, wd, total, feed, sems = refs
    units = wg.shape[1]
    tiles = units // tile
    first = [
        pltpu.make_async_copy(normed_hbm, normed, sems.at[3 * tiles]),
        pltpu.make_async_copy(cot_hbm, cot, sems.at[3 * tiles + 1]),
    ]

    def weights(t):
        cols = pl.ds(pl.multiple_of(t * tile, tile), tile)
        return [
            pltpu.make_async_copy(wg_hbm.at[:, cols], wg.at[:, cols], sems.at[t]),
            pltpu.make_async_copy(wu_hbm.at[:, cols], wu.at[:, cols], sems.at[tiles + t]),
            pltpu.make_async_copy(wd_hbm.at[cols, :], wd.at[cols, :], sems.at[2 * tiles + t]),
        ]

    for copy in first:
        copy.start()
    for t in range(tiles):
        for copy in weights(t):
            copy.start()
    total[...] = jnp.zeros_like(total)
    feed[...] = jnp.zeros_like(feed)
    for copy in first:
        copy.wait()

    def step(t, carry):
        cols = pl.ds(pl.multiple_of(t * tile, tile), tile)
        gate_copy, up_copy, down_copy = weights(t)
        gate_copy.wait()
        up_copy.wait()
        down_copy.wait()
        gate = dot(normed[...], wg[:, cols])
        up = dot(normed[...], wu[:, cols])
        grad_hidden = dot_nt(cot[...], wd[cols, :])
        hidden, grad_gate, grad_up = gated_terms(gate, up, grad_hidden)
        total[...] += dot_nt(grad_gate.astype(BF), wg[:, cols]) + dot_nt(
            grad_up.astype(BF), wu[:, cols]
        )
        feed[...] += dot(hidden.astype(BF), wd[cols, :])
        return carry

    lax.fori_loop(0, tiles, step, 0)
    grad_out[...] = total[...].astype(BF)
    feed_out[...] = feed[...].astype(BF)


def feed_forward(ids, normed, cot, wg, wu, wd, after=()):
    rows, width = cot.shape
    units = wg.shape[1]
    tile = max(t for t in (512, 384, 256, 128) if units % t == 0)
    arrays = [normed, cot, wg, wu, wd]
    outs = [shape(rows, width)] * 2
    moved = size_of(arrays) + size_of(outs)
    return pl.pallas_call(
        functools.partial(feed_forward_body, tile, len(after)),
        out_shape=outs,
        in_specs=[SMEM] + [ANY] * (5 + len(after)),
        out_specs=[pl.BlockSpec(memory_space=pltpu.VMEM) for _ in outs],
        scratch_shapes=[pltpu.VMEM(a.shape, a.dtype) for a in arrays]
        + [
            pltpu.VMEM((rows, width), F32),
            pltpu.VMEM((rows, width), F32),
            pltpu.SemaphoreType.DMA((3 * (units // tile) + 2,)),
        ],
        compiler_params=pltpu.CompilerParams(
            vmem_limit_bytes=VMEM_LIMIT
        ),
        cost_estimate=cost(12 * rows * width * units, moved),
        name="feed_forward",
    )(ids, *arrays, *after)


def middle_body(count, group, blocks, ids, loads, own_ref, low_ref, sums_ref, *outs):
    grads, resid, inverse_ref, gain, cot = loads[:5]
    rows, width = grads.shape
    shard = width // count
    inverse = inverse_ref[...]
    row_total = 0.0
    for s in range(count):
        cols = pl.ds(pieces_of(s, ids[0], shard), shard)
        product = grads[:, cols].astype(F32) * (resid[:, cols].astype(F32) * inverse)
        sums_ref[:, cols] = jnp.sum(product, axis=0, keepdims=True)
        row_total += jnp.sum(product * gain[:, cols], axis=-1, keepdims=True)
    scale = row_total * inverse * (1.0 / width)
    wo = loads[5]
    mixed = jnp.zeros((rows, wo.shape[0]), F32)
    for s in range(count):
        cols = pl.ds(pieces_of(s, ids[0], shard), shard)
        unit = resid[:, cols].astype(F32) * inverse
        grad = (
            cot[:, cols].astype(F32)
            + inverse * (gain[:, cols] * grads[:, cols].astype(F32))
            - unit * scale
        )
        if s == 0:
            own_ref[...] = grad
        low = grad.astype(BF)
        low_ref[:, cols] = low
        mixed += dot_nt(low, wo[:, cols])
    attention_backward(group, blocks, ids, loads[6:], mixed.astype(BF), *outs)


def attention_backward(group, blocks, ids, loads, grads, low_ref, gain_ref, own_ref, *others):
    q, row_segment = loads[:2]
    kvs = loads[2 : 2 + blocks]
    key_segments = loads[2 + blocks : 2 + 2 * blocks]
    raw, query_gain, cosine, sine = loads[2 + 2 * blocks : 6 + 2 * blocks]
    kv_width = kvs[0].shape[1] // 2
    factor = HD ** (-0.5)
    gain_total = jnp.zeros((1, HD), F32)
    outs = [own_ref] + list(others)
    for kv in range(kv_width // HD):
        key_cols = slice(kv * HD, (kv + 1) * HD)
        value_cols = slice(kv_width + kv * HD, kv_width + (kv + 1) * HD)
        key_sums = [0.0] * blocks
        value_sums = [0.0] * blocks
        for h in range(kv * group, (kv + 1) * group):
            cols = slice(h * HD, (h + 1) * HD)
            probs = head_probs(ids, q, kvs, h, group, row_segment, key_segments)
            grad = grads[:, cols]
            grad_probs = [dot_nt(grad, block[:, value_cols]) for block in kvs]
            delta = sum(jnp.sum(p * g, axis=-1, keepdims=True) for p, g in zip(probs, grad_probs))
            scores = [(p * (g - delta)).astype(BF) for p, g in zip(probs, grad_probs)]
            grad_query = sum(dot(g, block[:, key_cols]) for g, block in zip(scores, kvs)) * factor
            for s in range(blocks):
                key_sums[s] += dot_tn(scores[s], q[:, cols])
                value_sums[s] += dot_tn(probs[s].astype(BF), grad)
            grad_raw, grad_gain = head_backward(
                grad_query, raw[:, cols], query_gain[...], cosine[...], sine[...]
            )
            low_ref[:, cols] = grad_raw.astype(BF)
            gain_total += grad_gain
        for s in range(blocks):
            outs[s][:, key_cols] = (key_sums[s] * factor).astype(outs[s].dtype)
            outs[s][:, value_cols] = value_sums[s].astype(outs[s].dtype)
    gain_ref[...] = gain_total


def key_backward_body(blocks, ids, loads, low_ref, gain_ref):
    sums = loads[:blocks]
    raw, key_gain, cosine, sine, query_low = loads[blocks : blocks + 5]
    q_width = query_low.shape[1]
    kv_width = raw.shape[1]
    low_ref[:, :q_width] = query_low[...]
    total = sums[0][...]
    for other in sums[1:]:
        total = total + other[...].astype(F32)
    gain_total = jnp.zeros((1, HD), F32)
    for h in range(kv_width // HD):
        cols = slice(h * HD, (h + 1) * HD)
        grad_raw, grad_gain = head_backward(
            total[:, cols], raw[:, cols], key_gain[...], cosine[...], sine[...]
        )
        low_ref[:, q_width + h * HD : q_width + (h + 1) * HD] = grad_raw.astype(BF)
        gain_total += grad_gain
    low_ref[:, q_width + kv_width :] = total[:, kv_width:].astype(BF)
    gain_ref[...] = gain_total


def first_grad_body(count, ids, loads, *outs):
    pieces = loads[:count]
    inverse_ref, gain, query_sums, key_sums, grads, wq, wk, wv = loads[count : count + 8]
    rows, shard = pieces[0].shape
    q_width, kv_width = wq.shape[1], wk.shape[1]
    inverse = inverse_ref[...]
    row_total = jnp.zeros((rows, 1), F32)
    for s in range(count):
        cols = pl.ds(pieces_of(s, ids[0], shard), shard)
        grad = (
            dot_nt(grads[:, :q_width], wq[cols, :])
            + dot_nt(grads[:, q_width : q_width + kv_width], wk[cols, :])
            + dot_nt(grads[:, q_width + kv_width :], wv[cols, :])
        )
        product = grad * (pieces[s][...].astype(F32) * inverse)
        outs[s][:rows, :] = grad.astype(BF)
        outs[s][rows:, :] = jnp.zeros((EXTRA, shard), BF)
        outs[s][rows : rows + 1, :] = jnp.sum(product, axis=0, keepdims=True).astype(BF)
        row_total += jnp.sum(product * gain[:, cols], axis=-1, keepdims=True)
    turned = jnp.broadcast_to(row_total, (rows, HD)).T[:1]
    small = jnp.concatenate([turned, query_sums[...], key_sums[...]], axis=1).astype(BF)
    for s in range(count):
        for r in range(small.shape[1] // shard):
            row = rows + 1 + r
            outs[s][row : row + 1, :] = small[:, r * shard : (r + 1) * shard]


def feed_weight_body(parts, extra, last, block, ids, *refs):
    rows_hbm, cots_hbm = refs[:parts], refs[parts : 2 * parts]
    wg_hbm, wu_hbm, wd_hbm = refs[2 * parts : 2 * parts + 3]
    refs = refs[2 * parts + 3 + extra :]
    dwg, dwu, dwd = refs[:3]
    lows = refs[3:6] if last else ()
    refs = refs[6:] if last else refs[3:]
    rows, cots, hid, gates, ups, wg, wu, wd, gate_out, up_out, down_out = refs[:11]
    refs = refs[11:]
    if last:
        gate_held, up_held, down_held, gate_cut, up_cut, down_cut = refs[:6]
        refs = refs[6:]
    row_sems, cot_sems, weight_sems, held_sems, out_sems = refs
    width = rows.shape[1]
    size = rows_hbm[0].shape[0]
    group = min(2, parts)
    chunk = group * size
    steps = wg_hbm.shape[1] // block // 2
    tile = width // 2

    def mine(b):
        return pl.ds(pl.multiple_of((ids[2] * steps + b) * block, block), block)

    def weights(b, slot):
        return [
            pltpu.make_async_copy(wg_hbm.at[:, mine(b)], wg.at[slot], weight_sems.at[slot, 0]),
            pltpu.make_async_copy(wu_hbm.at[:, mine(b)], wu.at[slot], weight_sems.at[slot, 1]),
            pltpu.make_async_copy(wd_hbm.at[mine(b), :], wd.at[slot], weight_sems.at[slot, 2]),
        ]

    def tile_at(t):
        return pl.ds(pl.multiple_of(t * tile, tile), tile)

    def held(b, t):
        at = tile_at(t)
        pairs = [
            (dwg.at[at, mine(b)], gate_held.at[at, :]),
            (dwu.at[at, mine(b)], up_held.at[at, :]),
            (dwd.at[mine(b), at], down_held.at[:, at]),
        ]
        return [pltpu.make_async_copy(a, c, held_sems.at[t, i]) for i, (a, c) in enumerate(pairs)]

    def results(b, t):
        at = tile_at(t)
        low = pl.ds(pl.multiple_of(b * block, block), block)
        pairs = [
            (gate_out.at[at, :], dwg.at[at, mine(b)]),
            (up_out.at[at, :], dwu.at[at, mine(b)]),
            (down_out.at[:, at], dwd.at[mine(b), at]),
        ]
        if last:
            pairs += [
                (gate_cut.at[at, :], lows[0].at[at, low]),
                (up_cut.at[at, :], lows[1].at[at, low]),
                (down_cut.at[:, at], lows[2].at[low, at]),
            ]
        return [pltpu.make_async_copy(a, c, out_sems.at[t, i]) for i, (a, c) in enumerate(pairs)]

    for copy in weights(0, 0):
        copy.start()
    for i in range(parts):
        place = pl.ds(i * size, size)
        pltpu.make_async_copy(rows_hbm[i], rows.at[place, :], row_sems.at[i // group]).start()
        pltpu.make_async_copy(cots_hbm[i], cots.at[place, :], cot_sems.at[i // group]).start()

    def one_block(b, carry):
        slot = lax.rem(b, 2)
        for copy in weights(b, slot):
            copy.wait()
        if last:
            for t in range(2):
                for copy in held(b, t):
                    copy.start()

        @pl.when(b + 1 < steps)
        def _():
            for copy in weights(b + 1, 1 - slot):
                copy.start()

        def recompute(c, carry):
            place = pl.ds(pl.multiple_of(c * chunk, chunk), chunk)

            @pl.when(b == 0)
            def _():
                pltpu.make_async_copy(rows.at[place, :], rows.at[place, :], row_sems.at[c]).wait()
                pltpu.make_async_copy(cots.at[place, :], cots.at[place, :], cot_sems.at[c]).wait()

            own = rows[place, :]
            gate = dot(own, wg[slot])
            up = dot(own, wu[slot])
            grad_hidden = dot_nt(cots[place, :], wd[slot])
            hidden, grad_gate, grad_up = gated_terms(gate, up, grad_hidden)
            hid[place, :] = hidden.astype(BF)
            gates[place, :] = grad_gate.astype(BF)
            ups[place, :] = grad_up.astype(BF)
            return carry

        lax.fori_loop(0, parts // group, recompute, 0)

        def products(t, carry):
            @pl.when(b > 0)
            def _():
                for copy in results(b, t):
                    copy.wait()

            cols = tile_at(t)
            down = dot_tn(hid[...], cots[:, cols])
            gate = dot_tn(rows[:, cols], gates[...])
            up = dot_tn(rows[:, cols], ups[...])
            if last:
                for copy in held(b, t):
                    copy.wait()
                down = (down + down_held[:, cols]).astype(BF)
                gate = (gate + gate_held[cols, :]).astype(BF)
                up = (up + up_held[cols, :]).astype(BF)
                down_cut[:, cols] = down
                gate_cut[cols, :] = gate
                up_cut[cols, :] = up
            down_out[:, cols] = down.astype(F32)
            gate_out[cols, :] = gate.astype(F32)
            up_out[cols, :] = up.astype(F32)
            for copy in results(b, t):
                copy.start()
            return carry

        lax.fori_loop(0, 2, products, 0)
        return carry

    lax.fori_loop(0, steps, one_block, 0)
    for t in range(2):
        for copy in results(0, t):
            copy.wait()


def feed_weights(ids, rows, cots, wg, wu, wd, block, held, last, after=()):
    parts = len(rows)
    size, width = rows[0].shape
    tokens = size * parts
    units = wg.shape[1]
    held = list(held or ())
    outs = [
        shape(width, units, dtype=F32),
        shape(width, units, dtype=F32),
        shape(units, width, dtype=F32),
    ]
    tiles = [
        shape(width, block, dtype=F32),
        shape(width, block, dtype=F32),
        shape(block, width, dtype=F32),
    ]
    scratch = [
        shape(tokens, width),
        shape(tokens, width),
        shape(tokens, block),
        shape(tokens, block),
        shape(tokens, block),
        shape(2, width, block),
        shape(2, width, block),
        shape(2, block, width),
        *tiles,
    ]
    if last:
        outs += [shape(width, units // 2), shape(width, units // 2), shape(units // 2, width)]
        scratch += [*tiles, shape(width, block), shape(width, block), shape(block, width)]
    if not held and last:
        held = [jnp.zeros(o.shape, F32) for o in outs[:3]]
    extra = len(held) + len(after)
    return pl.pallas_call(
        functools.partial(feed_weight_body, parts, extra, last, block),
        out_shape=outs,
        in_specs=[SMEM] + [ANY] * (2 * parts + 3 + extra),
        out_specs=[ANY] * len(outs),
        scratch_shapes=[pltpu.VMEM(a.shape, a.dtype) for a in scratch]
        + [
            pltpu.SemaphoreType.DMA((parts,)),
            pltpu.SemaphoreType.DMA((parts,)),
            pltpu.SemaphoreType.DMA((2, 3)),
            pltpu.SemaphoreType.DMA((2, 3)),
            pltpu.SemaphoreType.DMA((2, 6)),
        ],
        input_output_aliases={4 + 2 * parts + i: i for i in range(len(held))},
        compiler_params=pltpu.CompilerParams(vmem_limit_bytes=VMEM_LIMIT),
        cost_estimate=cost(6 * tokens * width * units, 4 * tokens * width),
        name="feed_weights",
    )(ids, *rows, *cots, wg, wu, wd, *held, *after)


def assemble_body(extra, ids, gate_low, up_low, down_low, *refs):
    dwg, dwu, dwd = refs[-3:]
    dwg[...] = gate_low[...].astype(F32)
    dwu[...] = up_low[...].astype(F32)
    dwd[...] = down_low[...].astype(F32)


def assemble(ids, lows, block, held, after=()):
    width, units = held[0].shape
    steps = units // block // 2
    tile = width // 2
    cols_in = pl.BlockSpec((tile, block), lambda b, i, ids: (i, b))
    rows_in = pl.BlockSpec((block, tile), lambda b, i, ids: (b, i))
    cols_out = pl.BlockSpec((tile, block), lambda b, i, ids: (i, (1 - ids[2]) * steps + b))
    rows_out = pl.BlockSpec((block, tile), lambda b, i, ids: ((1 - ids[2]) * steps + b, i))
    return pl.pallas_call(
        functools.partial(assemble_body, len(after)),
        out_shape=[shape(*a.shape, dtype=F32) for a in held],
        grid_spec=pltpu.PrefetchScalarGridSpec(
            num_scalar_prefetch=1,
            grid=(steps, 2),
            in_specs=[cols_in, cols_in, rows_in] + [ANY] * (3 + len(after)),
            out_specs=[cols_out, cols_out, rows_out],
        ),
        input_output_aliases={4: 0, 5: 1, 6: 2},
        compiler_params=pltpu.CompilerParams(vmem_limit_bytes=VMEM_LIMIT),
        cost_estimate=cost(0, 9 * width * units),
        name="assemble",
    )(ids, *lows, *held, *after)


def projection_body(parts, tile, extra, ids, *refs):
    rows_hbm, grads_hbm = refs[:parts], refs[parts : 2 * parts]
    refs = refs[2 * parts + extra :]
    outs_hbm = refs[:3]
    rows, grads, *outs, row_sems, grad_sem, out_sems = refs[3:]
    width = rows.shape[1]
    tiles = width // tile
    at = 0
    for i in range(parts):
        place = pl.ds(at, grads_hbm[i].shape[0])
        pltpu.make_async_copy(grads_hbm[i], grads.at[place, :], grad_sem).start()
        at += grads_hbm[i].shape[0]
    for t in range(tiles):
        cols = pl.ds(t * tile, tile)
        at = 0
        for i in range(parts):
            place = pl.ds(at, rows_hbm[i].shape[0])
            pltpu.make_async_copy(
                rows_hbm[i].at[:, cols], rows.at[place, cols], row_sems.at[t]
            ).start()
            at += rows_hbm[i].shape[0]
    pltpu.make_async_copy(grads, grads, grad_sem).wait()
    q_width, kv_width = outs[0].shape[1], outs[1].shape[1]

    def copies(t):
        cols = pl.ds(pl.multiple_of(t * tile, tile), tile)
        return [
            pltpu.make_async_copy(a.at[cols, :], b.at[cols, :], out_sems.at[t, i])
            for i, (a, b) in enumerate(zip(outs, outs_hbm))
        ]

    def products(t, carry):
        cols = pl.ds(pl.multiple_of(t * tile, tile), tile)
        pltpu.make_async_copy(rows.at[:, cols], rows.at[:, cols], row_sems.at[t]).wait()
        total = dot_tn(rows[:, cols], grads[...])
        outs[0][cols, :] = total[:, :q_width]
        outs[1][cols, :] = total[:, q_width : q_width + kv_width]
        outs[2][cols, :] = total[:, q_width + kv_width :]
        for copy in copies(t):
            copy.start()
        return carry

    lax.fori_loop(0, tiles, products, 0)

    def finish(t, carry):
        for copy in copies(t):
            copy.wait()
        return carry

    lax.fori_loop(0, tiles, finish, 0)


def projection_weights(ids, rows, grads, q_width, kv_width, after):
    parts = len(rows)
    width = rows[0].shape[1]
    tokens = sum(a.shape[0] for a in rows)
    tile = 512
    outs = [shape(width, w, dtype=F32) for w in (q_width, kv_width, kv_width)]
    scratch = [shape(tokens, width), shape(tokens, q_width + 2 * kv_width)] + outs
    return pl.pallas_call(
        functools.partial(projection_body, parts, tile, len(after)),
        out_shape=outs,
        in_specs=[SMEM] + [ANY] * (2 * parts + len(after)),
        out_specs=[ANY] * 3,
        scratch_shapes=[pltpu.VMEM(a.shape, a.dtype) for a in scratch]
        + [
            pltpu.SemaphoreType.DMA((width // tile,)),
            pltpu.SemaphoreType.DMA(()),
            pltpu.SemaphoreType.DMA((width // tile, 3)),
        ],
        compiler_params=pltpu.CompilerParams(
            vmem_limit_bytes=VMEM_LIMIT
        ),
        cost_estimate=cost(2 * tokens * width * (q_width + 2 * kv_width), 2 * tokens * width),
        name="projection_weights",
    )(ids, *rows, *grads, *after)


def matmul_tn(left, right):
    return lax.dot_general(left, right, (((0,), (0,)), ((), ())), preferred_element_type=F32)


def rope_tables(position_row):
    half = HD // 2
    freqs = jnp.exp(-(2.0 * jnp.arange(half, dtype=F32) / HD) * jnp.log(F32(THETA)))
    angles = position_row.astype(F32)[:, None] * freqs[None, :]
    cosine, sine = jnp.cos(angles), jnp.sin(angles)
    return jnp.concatenate([cosine, cosine], axis=1), jnp.concatenate([-sine, sine], axis=1)


def per_device(
    inputs,
    cotangent,
    segments,
    positions,
    attention_gain,
    query_weight,
    key_weight,
    value_weight,
    query_gain,
    key_gain,
    output_weight,
    feed_gain,
    gate_weight,
    up_weight,
    down_weight,
):
    count, shard = inputs.shape
    width = cotangent.shape[1]
    tensor = lax.axis_size("tensor")
    me = lax.axis_index("tensor")
    column = me * shard
    place = lax.axis_index("ctx")
    core = lax.axis_index("dp") % 2
    ids = jnp.stack([me, place, core, lax.axis_index("dp")]).astype(jnp.int32)
    q_width, kv_width = query_weight.shape[1], key_weight.shape[1]
    group = q_width // kv_width
    blocks = lax.axis_size("ctx")
    gain_one = attention_gain.astype(F32)[None]
    gain_two = feed_gain.astype(F32)[None]
    gain_q = query_gain.astype(F32)[None]
    gain_k = key_gain.astype(F32)[None]
    gain_one_part = lax.dynamic_slice_in_dim(gain_one, column, shard, 1)
    hidden_units = gate_weight.shape[1]
    block = 256 if (hidden_units // 2) % 256 == 0 else 128

    masks = far_masks()
    first_masks = len(masks) // 2 or 1
    x_pieces = gather_pieces(inputs, "tensor")
    cot_parts = [send_plane(cotangent, mask) for mask in masks[:first_masks + 1]]
    cosine, sine = rope_tables(positions[0])
    normed_one, kv_rows, key_raw, inverse_one = kernel_call(
        functools.partial(key_value_body, tensor),
        ids,
        [*x_pieces, gain_one, gain_k, cosine, sine, key_weight, value_weight],
        [
            shape(count, width),
            shape(count, 2 * kv_width),
            shape(count, kv_width, dtype=F32),
            shape(count, 1, dtype=F32),
        ],
        4 * count * width * kv_width,
        "key_value",
        after=cot_parts[1:],
    )
    kv_pieces = gather_pieces(kv_rows, "ctx")
    all_normed_one = plane_all(order_after(normed_one, *kv_pieces[1:]))
    query_rows, query_raw = kernel_call(
        query_body,
        ids,
        [normed_one, query_weight, gain_q, cosine, sine],
        [shape(count, q_width), shape(count, q_width, dtype=F32)],
        2 * count * width * q_width,
        "query",
    )

    segment_row = segments[0]
    row_segment = lax.dynamic_slice_in_dim(segment_row, place * count, count)[:, None]
    key_segments = [
        lax.dynamic_slice_in_dim(segment_row, (place ^ s) * count, count)[None]
        for s in range(blocks)
    ]
    mixed_rows, *branch_pieces = kernel_call(
        functools.partial(attention_body, tensor, group, blocks),
        ids,
        [query_rows, row_segment, *kv_pieces, *key_segments, output_weight],
        [shape(count, q_width)] + [shape(count, shard)] * tensor,
        4 * count * count * blocks * q_width + 2 * count * width * q_width,
        "attention",
    )
    branch = second_half(first_half(branch_pieces, "tensor"), "tensor")
    resid_part = (inputs.astype(F32) + branch).astype(BF)
    resid_pieces = gather_pieces(resid_part, "tensor")
    cot_partners = partners(cot_parts[: first_masks + 1])

    normed_two, resid, inverse_two = kernel_call(
        functools.partial(second_norm_body, tensor),
        ids,
        [*resid_pieces, gain_two],
        [shape(count, width), shape(count, width), shape(count, 1, dtype=F32)],
        8 * count * width,
        "second_norm",
        after=cot_partners,
    )
    two_parts = [send_plane(normed_two, mask) for mask in masks[: first_masks + 1]]
    grad_two_part, feed_part = feed_forward(
        ids, normed_two, cotangent, gate_weight, up_weight, down_weight
    )
    feed_done = feed_part
    grad_two_part = sum_tensor(grad_two_part)
    late = order_after(normed_two, feed_done)
    two_parts += [send_plane(late, mask) for mask in masks[first_masks + 1 :]]
    late = order_after(cotangent, feed_done)
    cot_parts += [send_plane(late, mask) for mask in masks[first_masks + 1 :]]
    groups = [slice(0, first_masks), slice(first_masks, None)] if len(masks) > 1 else [slice(0, None)]
    last = len(groups) - 1
    two_partners = partners(two_parts[:1]) + partners(two_parts[1 : first_masks + 1], feed_done)

    def weights_of(g, held, after):
        return feed_weights(
            ids,
            two_parts[groups[g]] + two_partners[groups[g]],
            cot_parts[groups[g]] + cot_partners[groups[g]],
            gate_weight,
            up_weight,
            down_weight,
            block,
            held,
            g == last,
            after,
        )

    held, done = None, [feed_done, *two_partners, all_normed_one]
    for g in range(last):
        held = weights_of(g, held, done)
        done = held[:1]
    two_partners += partners(two_parts[first_masks + 1 :], *done)
    cot_partners += partners(cot_parts[first_masks + 1 :], *done)
    grad_two = lax.all_gather(grad_two_part, "tensor", axis=1, tiled=True)
    *held, gate_low, up_low, down_low = weights_of(last, held, [grad_two_part])
    lows = [gate_low, up_low, down_low]
    feed = sum_tensor(order_after(feed_part, gate_low))
    lows = [swap(low, "dp", 1) for low in lows] if has_pair() else lows

    (
        grad_resid_part,
        grad_resid_low,
        feed_sums,
        grad_query_low,
        grad_query_gain,
        grad_kv,
        *grad_kv_sent,
    ) = kernel_call(
        functools.partial(middle_body, tensor, group, blocks),
        ids,
        [
            grad_two,
            resid,
            inverse_two,
            gain_two,
            cotangent,
            output_weight,
            query_rows,
            row_segment,
            *kv_pieces,
            *key_segments,
            query_raw,
            gain_q,
            cosine,
            sine,
        ],
        [
            shape(count, shard, dtype=F32),
            shape(count, width),
            shape(1, width, dtype=F32),
            shape(count, q_width),
            shape(1, HD, dtype=F32),
            shape(count, 2 * kv_width, dtype=F32),
        ]
        + [shape(count, 2 * kv_width)] * (blocks - 1),
        2 * count * width * q_width,
        "middle",
        after=[gate_low],
    )
    kv_sums = [grad_kv] + [
        lax.ppermute(sent, "ctx", [(i, i ^ (s + 1)) for i in range(blocks)])
        for s, sent in enumerate(grad_kv_sent)
    ]
    output_part = matmul_tn(mixed_rows, grad_resid_low).astype(BF)
    if has_pair():
        half = q_width // 2
        keep = lax.dynamic_slice_in_dim(output_part, core * half, half, 0)
        send = lax.dynamic_slice_in_dim(output_part, (1 - core) * half, half, 0)
        output_part = (keep.astype(F32) + swap(send, "dp", 1).astype(F32)).astype(BF)
    half = output_part.shape[0] // 2
    output_parts = [output_part[:half], output_part[half:]]
    bits = [mask for mask in masks if mask and mask & (mask - 1) == 0]

    def summed(parts, bit_of, earlier=(), later=()):
        received = [
            send_plane(order_after(part, *earlier), bit) for part, bit in zip(parts, bit_of)
        ]
        return [
            (part.astype(F32) + order_after(other, *later).astype(F32)).astype(BF)
            for part, other in zip(parts, received)
        ]

    grad_low, grad_key_gain = kernel_call(
        functools.partial(key_backward_body, len(kv_sums)),
        ids,
        [*kv_sums, key_raw, gain_k, cosine, sine, grad_query_low],
        [shape(count, q_width + 2 * kv_width), shape(1, HD, dtype=F32)],
        40 * count * kv_width,
        "key_backward",
        after=[output_part],
    )
    all_grad_low = plane_all(grad_low)
    first_parts = output_parts

    grad_one_pieces = kernel_call(
        functools.partial(first_grad_body, tensor),
        ids,
        [
            *x_pieces,
            inverse_one,
            gain_one,
            grad_query_gain,
            grad_key_gain,
            grad_low,
            query_weight,
            key_weight,
            value_weight,
        ],
        [shape(count + EXTRA, shard)] * tensor,
        2 * count * width * (q_width + 2 * kv_width),
        "first_grad",
    )
    outputs = (resid_part.astype(F32) + order_after(feed, grad_one_pieces[0]).astype(F32)).astype(BF)
    grad_gate_w, grad_up_w, grad_down_w = assemble(ids, lows, block, held, [outputs])

    grad_one = first_half(grad_one_pieces, "tensor", grad_gate_w)
    grad_query_w, grad_key_w, grad_value_w = projection_weights(
        ids, [all_normed_one], [all_grad_low], q_width, kv_width, [grad_gate_w, *grad_one.values()]
    )

    grad_one = second_half(grad_one, "tensor")
    grad_one_part = grad_one[:count]
    small = grad_one[count + 1 : count + 1 + (count + 2 * HD) // shard].reshape(-1)
    row_total_one = small[:count, None]
    feed_part_sums = lax.dynamic_slice_in_dim(feed_sums[0], column, shard)
    small = jnp.concatenate([grad_one[count], feed_part_sums, small[count:]])
    if has_pair():
        small = small + swap(small, "dp", 1)
    unit_one_part = inputs.astype(F32) * inverse_one
    grad_inputs = (
        grad_resid_part
        + inverse_one * (gain_one_part * grad_one_part)
        - unit_one_part * (inverse_one / width) * row_total_one
    )

    output_parts = summed(first_parts, (bits[0], bits[-1]), (), [grad_gate_w])
    for i in range(1, len(bits)):
        output_parts = summed(output_parts, (bits[i], bits[-1 - i]), [grad_gate_w], [grad_query_w])
    small = order_after(small, grad_query_w)
    for bit in bits:
        small = small + send_plane(small, bit)
    grad_attention_gain = small[:shard]
    grad_feed_gain = small[shard : 2 * shard]
    grad_query_gain = small[2 * shard : 2 * shard + HD]
    grad_key_gain = small[2 * shard + HD :]
    if has_pair():
        others = [swap(part, "dp", 1) for part in output_parts]
        grad_output_w = jnp.where(
            core == 0,
            jnp.concatenate(output_parts + others, axis=0),
            jnp.concatenate(others + output_parts, axis=0),
        )
    else:
        grad_output_w = jnp.concatenate(output_parts, axis=0)
    grad_output_w = grad_output_w.astype(F32)

    return (
        outputs,
        grad_inputs,
        grad_attention_gain,
        grad_query_w,
        grad_key_w,
        grad_value_w,
        grad_query_gain,
        grad_key_gain,
        grad_output_w,
        grad_feed_gain,
        grad_gate_w,
        grad_up_w,
        grad_down_w,
    )


def solution(mesh):
    in_specs = (
        P(("dp", "ctx"), "tensor"),
        P(("dp", "ctx"), None),
        P("dp", None),
        P("dp", "ctx"),
        P(),
        P(None, "tensor"),
        P(None, "tensor"),
        P(None, "tensor"),
        P(),
        P(),
        P("tensor", None),
        P(),
        P(None, "tensor"),
        P(None, "tensor"),
        P("tensor", None),
    )
    out_specs = (
        P(("dp", "ctx"), "tensor"),
        P(("dp", "ctx"), "tensor"),
        P("tensor"),
        P(None, "tensor"),
        P(None, "tensor"),
        P(None, "tensor"),
        P(),
        P(),
        P("tensor", None),
        P("tensor"),
        P(None, "tensor"),
        P(None, "tensor"),
        P("tensor", None),
    )
    return jax.shard_map(
        per_device, mesh=mesh, in_specs=in_specs, out_specs=out_specs, check_vma=False
    )
```

time: 506 us -> 324 us (0.64); the launches traced: 496 us -> 323 us
  Pallas kernels: 0 us -> 140 us
  matrix products: 141 us -> 2.07 us
  local copies, waits for them, and re-layouts: 76 us -> 11.2 us
  waiting for transfers between devices: 140 us -> 83.4 us
  other arithmetic: 70.9 us -> 27.5 us
  starting transfers between devices: 65.5 us -> 42.9 us
  between operations: 2.81 us -> 16.1 us
    pallas_call x0 -> x12, Pallas kernels: none -> 140 us  [the longest x2 60.1 us: feed_weights(): pl.pallas_call(functools.partial(feed_weight_body, parts, extra, last, bl...]
    ppermute x69 -> x28, waiting for transfers between devices: 140 us -> 60.8 us  [swap(): return lax.ppermute(value, axis, [(i, i ^ bit) for i in range(size)])]
    dot_general x22 -> x0, matrix products: 71.2 us -> none  [the longest x8 33.1 us: matmul_nt(): lax.dot_general(left, right, (((1,), (1,)), ((), ())), preferred_element_...]
    dot_general x7 -> x1, matrix products: 65.9 us -> 2.07 us  [matmul_tn(): lax.dot_general(left, right, (((0,), (0,)), ((), ())), preferred_element_...]
    unnamed x244 -> x38, local copies, waits for them, and re-layouts: 55 us -> 5.61 us
    ppermute x69 -> x28, starting transfers between devices: 65.5 us -> 23.1 us  [swap(): return lax.ppermute(value, axis, [(i, i ^ bit) for i in range(size)])]
    select_n x8 -> x0, other arithmetic: 27.5 us -> none  [the longest x3 26.9 us: both_halves(): jnp.where(core == 0, jnp.concatenate([mine, other], axis=axis), jnp.conca...]
    ppermute x0 -> x13, waiting for transfers between devices: none -> 22.5 us  [the longest x12 19 us: send_plane(): lax.ppermute(value, ('dp', 'ctx'), [(i, i ^ mask) for i in range(size)])]
  transfers between devices with their start and end apart: 69 -> 46, of which waited for: 25 -> 20; matrix products, arithmetic and copies ran while one was open for 54% -> 10% of each run, Pallas kernels for 0% -> 42%
where the time goes in v2:
time: 324 us; the launch traced here: 323 us
  Pallas kernels  140 us (43%)
  waiting for transfers between devices  83.4 us (26%)
  starting transfers between devices  42.9 us (13%)
  other arithmetic  27.5 us (8%)
  between operations  16.1 us (5%)
  local copies, waits for them, and re-layouts  11.2 us (3%)
    ppermute x28, waiting for transfers between devices, swap(): return lax.ppermute(value, axis, [(i, i ^ bit) for i in range(size)])  60.8 us
    pallas_call x2, Pallas kernels, feed_weights(): pl.pallas_call(functools.partial(feed_weight_body, parts, extra, last, bl...  60.1 us
    pallas_call x7, Pallas kernels, kernel_call(): pl.pallas_call(run, out_shape=tuple(outs), in_specs=[SMEM] + [ANY] * (cou...  36.2 us
    ppermute x28, starting transfers between devices, swap(): return lax.ppermute(value, axis, [(i, i ^ bit) for i in range(size)])  23.1 us
    ppermute x12, starting transfers between devices, send_plane(): lax.ppermute(value, ('dp', 'ctx'), [(i, i ^ mask) for i in range(size)])  19.1 us
    ppermute x12, waiting for transfers between devices, send_plane(): lax.ppermute(value, ('dp', 'ctx'), [(i, i ^ mask) for i in range(size)])  19 us
    pallas_call x1, Pallas kernels, feed_forward(): pl.pallas_call(functools.partial(feed_forward_body, tile, len(after)), ou...  16.5 us
    pallas_call x1, Pallas kernels, projection_weights(): pl.pallas_call(functools.partial(projection_body, parts, tile, len(after)...  15.4 us
  transfers between devices with their start and end apart: 46, of which 20 were waited for; matrix products, arithmetic and copies ran while one was open for 10% of the time, Pallas kernels for 42%

profile of v2, /device:TPU:0, one launch (start us, length us, event | category | flops | bytes accessed | tf_op | source)
XLA Modules:
  0.0 323.5 jit_solution(6612776934834763499)
XLA Ops:
  8.1 3.0 collective-permute-start.3
  11.1 1.5 collective-permute-start.4
  12.6 2.6 collective-permute-start.1
  15.2 1.6 collective-permute-start
  18.9 8.1 %collective-permute-done.1.refs_2_ = bf16[256,512]{1,0:T(8,128)(2,1)S(1)} collective-permute-done((bf16[256,512]{1,0:T(8,128)(2,1)}, bf16[256,512]{1,0:T(8,128)(2,1)S(1)}, u32[]{:S(2)}, u32[]{:S(2)}) %collective-permute-start.1) | collective-permute-done | bytes 262176 | tf_op jit(solution)/shard_map/ppermute | solution.py:24
  31.4 3.4 %collective-permute-done.2.refs_3_ = bf16[256,512]{1,0:T(8,128)(2,1)S(1)} collective-permute-done((bf16[256,512]{1,0:T(8,128)(2,1)S(1)}, bf16[256,512]{1,0:T(8,128)(2,1)S(1)}, u32[]{:S(2)}, u32[]{:S(2)}) %collective-permute-start.2) | collective-permute-done | bytes 262176 | tf_op jit(solution)/shard_map/ppermute | solution.py:24
  36.9 4.5 %key_value.1 = (bf16[256,2048]{1,0:T(8,128)(2,1)}, bf16[256,512]{1,0:T(8,128)(2,1)}, f32[256,256]{1,0:T(8,128)}, f32[256,1]{1,0:T(8,128)}) custom-call(s32[4]{0:T(128)} %pad_add_fusion.ids, bf16[256,512]{1,0:T(8,128)(2,1)} %refs_0_.3, bf16[256,512]{1,0:T(8,128)(2,1)} %copy-done.5, bf16[256,512]{1,0:T(8,128)(2,1)} %copy-done.4, bf16[256,512]{1,0:T(8,128)(2,1)} %copy-done.6, ...), custom_call_target="tpu_custom_call" | custom-call | flops 536870912 | bytes 4990464 | tf_op jit(solution)/shard_map/key_value/pallas_call | solution.py:191
  41.4 1.6 collective-permute-start.5
  43.0 5.7 %collective-permute-done.5.refs_3_.refs_9_ = bf16[256,512]{1,0:T(8,128)(2,1)} collective-permute-done((bf16[256,512]{1,0:T(8,128)(2,1)}, bf16[256,512]{1,0:T(8,128)(2,1)}, u32[]{:S(2)}, u32[]{:S(2)}) %collective-permute-start.5) | collective-permute-done | bytes 262176 | tf_op jit(solution)/shard_map/ppermute | solution.py:24
  50.7 4.5 %query.1 = (bf16[256,512]{1,0:T(8,128)(2,1)}, f32[256,512]{1,0:T(8,128)}) custom-call(s32[4]{0:T(128)} %pad_add_fusion.ids, bf16[256,2048]{1,0:T(8,128)(2,1)} %get-tuple-element.87.refs_0_, bf16[2048,512]{1,0:T(8,128)(2,1)} %refs_9_.7, f32[1,128]{1,0:T(1,128)} %bitcast_convert_fusion.1.refs_2_.refs_13_, ...), custom_call_target="tpu_custom_call" | custom-call | flops 536870912 | bytes 4194816 | tf_op jit(solution)/shard_map/query/pallas_call | solution.py:191
  55.2 5.5 %attention.1 = (bf16[256,512]{1,0:T(8,128)(2,1)}, bf16[256,512]{1,0:T(8,128)(2,1)}, bf16[256,512]{1,0:T(8,128)(2,1)}, bf16[256,512]{1,0:T(8,128)(2,1)}, bf16[256,512]{1,0:T(8,128)(2,1)}) custom-call(s32[4]{0:T(128)} %pad_add_fusion.ids, bf16[256,512]{1,0:T(8,128)(2,1)} %get-tuple-element.76.refs_0_.refs_6_, s32[256,1]{1,0:T(8,128)} %copy.34.refs_1_.refs_7_, ...), custom_call_target="tpu_custom_call" | custom-call | flops 805306368 | bytes 4197376 | tf_op jit(solution)/shard_map/attention/pallas_call | solution.py:191
  60.7 2.2 collective-permute-start.7
  63.6 6.0 %collective-permute-done.7 = bf16[256,512]{1,0:T(8,128)(2,1)S(1)} collective-permute-done((bf16[256,512]{1,0:T(8,128)(2,1)}, bf16[256,512]{1,0:T(8,128)(2,1)S(1)}, u32[]{:S(2)}, u32[]{:S(2)}) %collective-permute-start.7) | collective-permute-done | bytes 262176 | tf_op jit(solution)/shard_map/ppermute | solution.py:24
  70.6 3.9 %collective-permute-start.8 = (bf16[256,512]{1,0:T(8,128)(2,1)S(1)}, bf16[256,512]{1,0:T(8,128)(2,1)S(1)}, u32[]{:S(2)}, u32[]{:S(2)}) collective-permute-start(bf16[256,512]{1,0:T(8,128)(2,1)S(1)} %add_convert_fusion.7), channel_id=1, source_target_pairs={{0,2},{1,3},{2,0},{3,1},{4,6},{5,7},{6,4},{7,5},{8,10},{9,11},{10,... | collective-permute-start | bytes 786440 | tf_op jit(solution)/shard_map/ppermute | solution.py:24
  74.5 1.8 collective-permute-done.6
  76.3 9.2 %collective-permute-done.8 = bf16[256,512]{1,0:T(8,128)(2,1)S(1)} collective-permute-done((bf16[256,512]{1,0:T(8,128)(2,1)S(1)}, bf16[256,512]{1,0:T(8,128)(2,1)S(1)}, u32[]{:S(2)}, u32[]{:S(2)}) %collective-permute-start.8) | collective-permute-done | bytes 262176 | tf_op jit(solution)/shard_map/ppermute | solution.py:24
  87.4 3.8 %collective-permute-start.9 = (bf16[256,512]{1,0:T(8,128)(2,1)S(1)}, bf16[256,512]{1,0:T(8,128)(2,1)S(1)}, u32[]{:S(2)}, u32[]{:S(2)}) collective-permute-start(bf16[256,512]{1,0:T(8,128)(2,1)S(1)} %fusion.1.refs_0_), channel_id=1, source_target_pairs={{0,1},{1,0},{2,3},{3,2},{4,5},{5,4},{6,7},{7,6},{8,9},{9,8},{10,11... | collective-permute-start | bytes 786440 | tf_op jit(solution)/shard_map/ppermute | solution.py:24
  91.2 4.6 %collective-permute-done.10.refs_2_ = bf16[256,512]{1,0:T(8,128)(2,1)S(1)} collective-permute-done((bf16[256,512]{1,0:T(8,128)(2,1)S(1)}, bf16[256,512]{1,0:T(8,128)(2,1)S(1)}, u32[]{:S(2)}, u32[]{:S(2)}) %collective-permute-start.10) | collective-permute-done | bytes 262176 | tf_op jit(solution)/shard_map/ppermute | solution.py:24
  95.8 2.3 collective-permute-start.11
  100.7 1.7 collective-permute-done.11.refs_3_
  103.2 3.7 %second_norm.1 = (bf16[256,2048]{1,0:T(8,128)(2,1)}, bf16[256,2048]{1,0:T(8,128)(2,1)}, f32[256,1]{1,0:T(8,128)}) custom-call(s32[4]{0:T(128)} %pad_add_fusion.ids, bf16[256,512]{1,0:T(8,128)(2,1)} %copy-done, bf16[256,512]{1,0:T(8,128)(2,1)} %copy-done.11, bf16[256,512]{1,0:T(8,128)(2,1)} %copy-done.10, bf16[256,512]{1,0:T(8,128)(2,1)} %copy-done.12, ...), custom_call_target="tpu_custom_call" | custom-call | flops 4194304 | bytes 3154944 | tf_op jit(solution)/shard_map/second_norm/pallas_call | solution.py:191
  107.6 4.6 %collective-permute-start.15 = (bf16[256,2048]{1,0:T(8,128)(2,1)}, bf16[256,2048]{1,0:T(8,128)(2,1)}, u32[]{:S(2)}, u32[]{:S(2)}) collective-permute-start(bf16[256,2048]{1,0:T(8,128)(2,1)} %get-tuple-element.84.normed_hbm.refs_0_), channel_id=1, source_target_pairs={{0,4},{4,0},{8,12},{12,8},{16,20},{20,16},{24,28},{28,24},{1,5},{5... | collective-permute-start | bytes 3145736 | tf_op jit(solution)/shard_map/ppermute | solution.py:96
  112.1 16.5 %feed_forward.1 = (bf16[256,2048]{1,0:T(8,128)(2,1)}, bf16[256,2048]{1,0:T(8,128)(2,1)}) custom-call(s32[4]{0:T(128)} %pad_add_fusion.ids, bf16[256,2048]{1,0:T(8,128)(2,1)} %get-tuple-element.84.normed_hbm.refs_0_, bf16[256,2048]{1,0:T(8,128)(2,1)} %refs_4_.3, bf16[2048,1536]{1,0:T(8,128)(2,1)} %refs_8_.5, bf16[2048,1536]{1,0:T(8,128)(2,1)} %refs_9_.6, ...), custom_call_target="tpu_custom_call" | custom-call | flops 9663676416 | bytes 23068672 | tf_op jit(solution)/shard_map/feed_forward/pallas_call | solution.py:382
  130.9 1.9 collective-permute-start.16
  133.9 28.5 %feed_weights.2 = (f32[2048,1536]{1,0:T(8,128)}, f32[2048,1536]{1,0:T(8,128)}, f32[1536,2048]{1,0:T(8,128)}) custom-call(s32[4]{0:T(128)} %pad_add_fusion.ids, bf16[256,2048]{1,0:T(8,128)(2,1)} %get-tuple-element.84.normed_hbm.refs_0_, bf16[256,2048]{1,0:T(8,128)(2,1)} %collective-permute-done.18.refs_1_, ...), custom_call_target="tpu_custom_call" | custom-call | flops 19327352832 | bytes 8388608 | tf_op jit(solution)/shard_map/feed_weights/pallas_call | solution.py:682
  162.6 16.5 %collective-permute-done.16.refs_1_ = bf16[256,2048]{1,0:T(8,128)(2,1)} collective-permute-done((bf16[256,2048]{1,0:T(8,128)(2,1)}, bf16[256,2048]{1,0:T(8,128)(2,1)}, u32[]{:S(2)}, u32[]{:S(2)}) %collective-permute-start.16) | collective-permute-done | bytes 1048608 | tf_op jit(solution)/shard_map/ppermute | solution.py:96
  179.2 2.9 collective-permute-done.21.refs_3_
  182.1 31.6 %feed_weights.3 = (f32[2048,1536]{1,0:T(8,128)}, f32[2048,1536]{1,0:T(8,128)}, f32[1536,2048]{1,0:T(8,128)}, bf16[2048,768]{1,0:T(8,128)(2,1)}, bf16[2048,768]{1,0:T(8,128)(2,1)}, /*index=5*/bf16[768,2048]{1,0:T(8,128)(2,1)}) custom-call(s32[4]{0:T(128)} %pad_add_fusion.ids, ...), custom_call_target="tpu_custom_call", output_to_operand_aliasing={{0}: (12, {}), {1}: (13, {}), {2}: (14, {})} | custom-call | flops 19327352832 | bytes 8388608 | tf_op jit(solution)/shard_map/feed_weights/pallas_call | solution.py:682
  214.0 8.6 %middle.1 = (f32[256,512]{1,0:T(8,128)}, bf16[256,2048]{1,0:T(8,128)(2,1)}, f32[1,2048]{1,0:T(1,128)}, bf16[256,512]{1,0:T(8,128)(2,1)}, f32[1,128]{1,0:T(1,128)...) custom-call(s32[4]{0:T(128)} %pad_add_fusion.ids, bf16[256,2048]{1,0:T(8,128)(2,1)} %all-gather.6.cloned.1.call-done.refs_0_, ...), custom_call_target="tpu_custom_call" | custom-call | flops 536870912 | bytes 9458688 | tf_op jit(solution)/shard_map/middle/pallas_call | solution.py:191
  222.7 2.1 convolution_convert_fusion
  225.2 2.5 collective-permute-done.25
  227.7 2.6 add_convert_fusion.refs_7_
  230.3 3.4 %collective-permute-done.24.refs_1_ = bf16[256,512]{1,0:T(8,128)(2,1)} collective-permute-done((bf16[256,512]{1,0:T(8,128)(2,1)S(1)}, bf16[256,512]{1,0:T(8,128)(2,1)}, u32[]{:S(2)}, u32[]{:S(2)}) %collective-permute-start.24) | collective-permute-done | bytes 262176 | tf_op jit(solution)/shard_map/ppermute | solution.py:998
  233.8 3.3 %key_backward.1 = (bf16[256,1024]{1,0:T(8,128)(2,1)}, f32[1,128]{1,0:T(1,128)}) custom-call(s32[4]{0:T(128)} %pad_add_fusion.ids, f32[256,512]{1,0:T(8,128)} %get-tuple-element.102.refs_0_, bf16[256,512]{1,0:T(8,128)(2,1)} %collective-permute-done.24.refs_1_, f32[256,256]{1,0:T(8,128)} %get-tuple-element.104.refs_2_, ...), custom_call_target="tpu_custom_call" | custom-call | flops 2621440 | bytes 2098176 | tf_op jit(solution)/shard_map/key_backward/pallas_call | solution.py:191
  237.8 6.1 %first_grad.1 = (bf16[272,512]{1,0:T(8,128)(2,1)}, bf16[272,512]{1,0:T(8,128)(2,1)}, bf16[272,512]{1,0:T(8,128)(2,1)}, bf16[272,512]{1,0:T(8,128)(2,1)}) custom-call(s32[4]{0:T(128)} %pad_add_fusion.ids, bf16[256,512]{1,0:T(8,128)(2,1)} %refs_0_.3, bf16[256,512]{1,0:T(8,128)(2,1)} %copy-done.5, bf16[256,512]{1,0:T(8,128)(2,1)} %copy-done.4, ...), custom_call_target="tpu_custom_call" | custom-call | flops 1073741824 | bytes 6891520 | tf_op jit(solution)/shard_map/first_grad/pallas_call | solution.py:191
  244.0 2.3 fusion.10
  247.8 1.8 add_convert_fusion.6.refs_3_
  249.6 2.0 collective-permute-start.26
  252.2 12.2 %assemble.1 = (f32[2048,1536]{1,0:T(8,128)}, f32[2048,1536]{1,0:T(8,128)}, f32[1536,2048]{1,0:T(8,128)}) custom-call(s32[4]{0:T(128)} %pad_add_fusion.ids, bf16[2048,768]{1,0:T(8,128)(2,1)} %collective-permute-done.27.gate_low, bf16[2048,768]{1,0:T(8,128)(2,1)} %collective-permute-done.28.up_low, ...), custom_call_target="tpu_custom_call", output_to_operand_aliasing={{0}: (4, {}), {1}: (5, {}), {2}: (6, {})} | custom-call | bytes 28311552 | tf_op jit(solution)/shard_map/assemble/pallas_call | solution.py:717
  267.4 12.6 %collective-permute-done.31 = bf16[272,512]{1,0:T(8,128)(2,1)S(1)} collective-permute-done((bf16[272,512]{1,0:T(8,128)(2,1)S(1)}, bf16[272,512]{1,0:T(8,128)(2,1)S(1)}, u32[]{:S(2)}, u32[]{:S(2)}) %collective-permute-start.31) | collective-permute-done | bytes 278560 | tf_op jit(solution)/shard_map/ppermute | solution.py:24
  280.0 2.0 convert_add_fusion.2
  282.9 2.9 add_convert_fusion.4
  287.7 15.4 %projection_weights.1 = (f32[2048,512]{1,0:T(8,128)}, f32[2048,256]{1,0:T(8,128)}, f32[2048,256]{1,0:T(8,128)}) custom-call(s32[4]{0:T(128)} %pad_add_fusion.ids, bf16[2048,2048]{1,0:T(8,128)(2,1)} %all-gather.4.cloned.1.call-done.refs_15_.refs_0_, bf16[2048,1024]{1,0:T(8,128)(2,1)} %all-gather.8.cloned.1.call-done.refs_1_, ...), custom_call_target="tpu_custom_call" | custom-call | flops 8589934592 | bytes 8388608 | tf_op jit(solution)/shard_map/projection_weights/pallas_call | solution.py:792
  303.1 1.4 add_convert_fusion.3
  305.9 1.4 add_convert_fusion.1
  308.3 1.7 collective-permute-start.34
  309.9 2.3 fusion.4
  313.3 2.5 fusion
  (135 shorter events, 34.8 us)
Async XLA Ops:
  8.0 42.1 %copy-start.18 = (bf16[128]{0:T(256)(128)(2,1)S(1)}, bf16[128]{0:T(256)(128)(2,1)}, u32[]{:S(2)}) copy-start(bf16[128]{0:T(256)(128)(2,1)} %param.23) | copy-start | bytes 772
  8.0 125.9 %all-gather.4.cloned.1.call-start = ((), (), s32[]{:S(2)}) async-start(), calls=%async_computation.2 | async-start | bytes 9437184 | tf_op jit(solution)/shard_map/all_gather | solution.py:100
  8.1 26.7 %collective-permute-start.3 = (bf16[256,2048]{1,0:T(8,128)(2,1)}, bf16[256,2048]{1,0:T(8,128)(2,1)S(1)}, u32[]{:S(2)}, u32[]{:S(2)}) collective-permute-start(bf16[256,2048]{1,0:T(8,128)(2,1)} %refs_4_.3), channel_id=1, source_target_pairs={{0,16},{4,20},{8,24},{12,28},{16,0},{20,4},{24,8},{28,12},{1,17},{... | collective-permute-start | bytes 3145736 | tf_op jit(solution)/shard_map/ppermute | solution.py:96
  11.1 24.8 %collective-permute-start.4 = (bf16[256,2048]{1,0:T(8,128)(2,1)}, bf16[256,2048]{1,0:T(8,128)(2,1)S(1)}, u32[]{:S(2)}, u32[]{:S(2)}) collective-permute-start(bf16[256,2048]{1,0:T(8,128)(2,1)} %refs_4_.3), channel_id=1, source_target_pairs={{0,4},{4,0},{8,12},{12,8},{16,20},{20,16},{24,28},{28,24},{1,5},{5... | collective-permute-start | bytes 3145736 | tf_op jit(solution)/shard_map/ppermute | solution.py:96
  12.6 14.3 %collective-permute-start.1 = (bf16[256,512]{1,0:T(8,128)(2,1)}, bf16[256,512]{1,0:T(8,128)(2,1)S(1)}, u32[]{:S(2)}, u32[]{:S(2)}) collective-permute-start(bf16[256,512]{1,0:T(8,128)(2,1)} %refs_0_.3), channel_id=1, source_target_pairs={{0,2},{1,3},{2,0},{3,1},{4,6},{5,7},{6,4},{7,5},{8,10},{9,11},{10,... | collective-permute-start | bytes 786440 | tf_op jit(solution)/shard_map/ppermute | solution.py:24
  15.2 16.2 %collective-permute-start = (bf16[256,512]{1,0:T(8,128)(2,1)}, bf16[256,512]{1,0:T(8,128)(2,1)S(1)}, u32[]{:S(2)}, u32[]{:S(2)}) collective-permute-start(bf16[256,512]{1,0:T(8,128)(2,1)} %refs_0_.3), channel_id=1, source_target_pairs={{0,1},{1,0},{2,3},{3,2},{4,5},{5,4},{6,7},{7,6},{8,9},{9,8},{10,11... | collective-permute-start | bytes 786440 | tf_op jit(solution)/shard_map/ppermute | solution.py:24
  27.6 7.2 %collective-permute-start.2 = (bf16[256,512]{1,0:T(8,128)(2,1)S(1)}, bf16[256,512]{1,0:T(8,128)(2,1)S(1)}, u32[]{:S(2)}, u32[]{:S(2)}) collective-permute-start(bf16[256,512]{1,0:T(8,128)(2,1)S(1)} %collective-permute-done.1.refs_2_), channel_id=1, source_target_pairs={{0,1},{1,0},{2,3},{3,2},{4,5},{5,4},{6,7},{7,6},{8,9},{9,8},{10,11... | collective-permute-start | bytes 786440 | tf_op jit(solution)/shard_map/ppermute | solution.py:24
  41.4 7.3 %collective-permute-start.5 = (bf16[256,512]{1,0:T(8,128)(2,1)}, bf16[256,512]{1,0:T(8,128)(2,1)}, u32[]{:S(2)}, u32[]{:S(2)}) collective-permute-start(bf16[256,512]{1,0:T(8,128)(2,1)} %get-tuple-element.77.refs_2_.refs_8_), channel_id=1, source_target_pairs={{0,4},{4,0},{1,5},{5,1},{2,6},{6,2},{3,7},{7,3},{8,12},{12,8},{9,1... | collective-permute-start | bytes 786440 | tf_op jit(solution)/shard_map/ppermute | solution.py:24
  48.7 130.4 %reduce-scatter.3.cloned.1.call-start = ((), (), s32[]{:S(2)}) async-start(), calls=%async_computation.3 | async-start | bytes 1310720 | tf_op jit(solution)/shard_map/reduce_scatter | solution.py:104
  50.7 47.4 %copy-start.15 = (bf16[2048]{0:T(1024)(128)(2,1)S(1)}, bf16[2048]{0:T(1024)(128)(2,1)}, u32[]{:S(2)}) copy-start(bf16[2048]{0:T(1024)(128)(2,1)} %param.26) | copy-start | bytes 12292
  60.7 8.9 %collective-permute-start.7 = (bf16[256,512]{1,0:T(8,128)(2,1)}, bf16[256,512]{1,0:T(8,128)(2,1)S(1)}, u32[]{:S(2)}, u32[]{:S(2)}) collective-permute-start(bf16[256,512]{1,0:T(8,128)(2,1)} %get-tuple-element.81), channel_id=1, source_target_pairs={{0,1},{1,0},{2,3},{3,2},{4,5},{5,4},{6,7},{7,6},{8,9},{9,8},{10,11... | collective-permute-start | bytes 786440 | tf_op jit(solution)/shard_map/ppermute | solution.py:24
  62.9 35.8 %collective-permute-start.12 = (bf16[256,2048]{1,0:T(8,128)(2,1)}, bf16[256,2048]{1,0:T(8,128)(2,1)S(1)}, u32[]{:S(2)}, u32[]{:S(2)}) collective-permute-start(bf16[256,2048]{1,0:T(8,128)(2,1)} %refs_4_.3), channel_id=1, source_target_pairs={{0,8},{8,0},{16,24},{24,16},{1,9},{9,1},{17,25},{25,17},{2,10},{10... | collective-permute-start | bytes 3145736 | tf_op jit(solution)/shard_map/ppermute | solution.py:24
  62.9 36.8 %collective-permute-start.13 = (bf16[256,2048]{1,0:T(8,128)(2,1)}, bf16[256,2048]{1,0:T(8,128)(2,1)S(1)}, u32[]{:S(2)}, u32[]{:S(2)}) collective-permute-start(bf16[256,2048]{1,0:T(8,128)(2,1)} %copy-done.8), channel_id=1, source_target_pairs={{0,8},{8,0},{16,24},{24,16},{1,9},{9,1},{17,25},{25,17},{2,10},{10... | collective-permute-start | bytes 3145736 | tf_op jit(solution)/shard_map/ppermute | solution.py:24
  63.5 37.3 %collective-permute-start.14 = (bf16[256,2048]{1,0:T(8,128)(2,1)}, bf16[256,2048]{1,0:T(8,128)(2,1)}, u32[]{:S(2)}, u32[]{:S(2)}) collective-permute-start(bf16[256,2048]{1,0:T(8,128)(2,1)} %copy-done.7), channel_id=1, source_target_pairs={{0,8},{8,0},{16,24},{24,16},{1,9},{9,1},{17,25},{25,17},{2,10},{10... | collective-permute-start | bytes 3145736 | tf_op jit(solution)/shard_map/ppermute | solution.py:24
  63.5 12.8 %collective-permute-start.6 = (bf16[256,512]{1,0:T(8,128)(2,1)}, bf16[256,512]{1,0:T(8,128)(2,1)S(1)}, u32[]{:S(2)}, u32[]{:S(2)}) collective-permute-start(bf16[256,512]{1,0:T(8,128)(2,1)} %get-tuple-element.79), channel_id=1, source_target_pairs={{0,1},{1,0},{2,3},{3,2},{4,5},{5,4},{6,7},{7,6},{8,9},{9,8},{10,11... | collective-permute-start | bytes 786440 | tf_op jit(solution)/shard_map/ppermute | solution.py:24
  70.6 14.9 %collective-permute-start.8 = (bf16[256,512]{1,0:T(8,128)(2,1)S(1)}, bf16[256,512]{1,0:T(8,128)(2,1)S(1)}, u32[]{:S(2)}, u32[]{:S(2)}) collective-permute-start(bf16[256,512]{1,0:T(8,128)(2,1)S(1)} %add_convert_fusion.7), channel_id=1, source_target_pairs={{0,2},{1,3},{2,0},{3,1},{4,6},{5,7},{6,4},{7,5},{8,10},{9,11},{10,... | collective-permute-start | bytes 786440 | tf_op jit(solution)/shard_map/ppermute | solution.py:24
  86.7 9.1 %collective-permute-start.10 = (bf16[256,512]{1,0:T(8,128)(2,1)S(1)}, bf16[256,512]{1,0:T(8,128)(2,1)S(1)}, u32[]{:S(2)}, u32[]{:S(2)}) collective-permute-start(bf16[256,512]{1,0:T(8,128)(2,1)S(1)} %fusion.1.refs_0_), channel_id=1, source_target_pairs={{0,2},{1,3},{2,0},{3,1},{4,6},{5,7},{6,4},{7,5},{8,10},{9,11},{10,... | collective-permute-start | bytes 786440 | tf_op jit(solution)/shard_map/ppermute | solution.py:24
  87.4 12.3 %collective-permute-start.9 = (bf16[256,512]{1,0:T(8,128)(2,1)S(1)}, bf16[256,512]{1,0:T(8,128)(2,1)S(1)}, u32[]{:S(2)}, u32[]{:S(2)}) collective-permute-start(bf16[256,512]{1,0:T(8,128)(2,1)S(1)} %fusion.1.refs_0_), channel_id=1, source_target_pairs={{0,1},{1,0},{2,3},{3,2},{4,5},{5,4},{6,7},{7,6},{8,9},{9,8},{10,11... | collective-permute-start | bytes 786440 | tf_op jit(solution)/shard_map/ppermute | solution.py:24
  95.8 6.6 %collective-permute-start.11 = (bf16[256,512]{1,0:T(8,128)(2,1)S(1)}, bf16[256,512]{1,0:T(8,128)(2,1)S(1)}, u32[]{:S(2)}, u32[]{:S(2)}) collective-permute-start(bf16[256,512]{1,0:T(8,128)(2,1)S(1)} %collective-permute-done.10.refs_2_), channel_id=1, source_target_pairs={{0,1},{1,0},{2,3},{3,2},{4,5},{5,4},{6,7},{7,6},{8,9},{9,8},{10,11... | collective-permute-start | bytes 786440 | tf_op jit(solution)/shard_map/ppermute | solution.py:24
  106.9 22.6 %collective-permute-start.18 = (bf16[256,2048]{1,0:T(8,128)(2,1)}, bf16[256,2048]{1,0:T(8,128)(2,1)}, u32[]{:S(2)}, u32[]{:S(2)}) collective-permute-start(bf16[256,2048]{1,0:T(8,128)(2,1)} %get-tuple-element.84.normed_hbm.refs_0_), channel_id=1, source_target_pairs={{0,16},{4,20},{8,24},{12,28},{16,0},{20,4},{24,8},{28,12},{1,17},{... | collective-permute-start | bytes 3145736 | tf_op jit(solution)/shard_map/ppermute | solution.py:96
  107.6 22.3 %collective-permute-start.15 = (bf16[256,2048]{1,0:T(8,128)(2,1)}, bf16[256,2048]{1,0:T(8,128)(2,1)}, u32[]{:S(2)}, u32[]{:S(2)}) collective-permute-start(bf16[256,2048]{1,0:T(8,128)(2,1)} %get-tuple-element.84.normed_hbm.refs_0_), channel_id=1, source_target_pairs={{0,4},{4,0},{8,12},{12,8},{16,20},{20,16},{24,28},{28,24},{1,5},{5... | collective-permute-start | bytes 3145736 | tf_op jit(solution)/shard_map/ppermute | solution.py:96
  112.1 21.0 %collective-permute-start.19 = (bf16[256,2048]{1,0:T(8,128)(2,1)}, bf16[256,2048]{1,0:T(8,128)(2,1)}, u32[]{:S(2)}, u32[]{:S(2)}) collective-permute-start(bf16[256,2048]{1,0:T(8,128)(2,1)} %get-tuple-element.84.normed_hbm.refs_0_), channel_id=1, source_target_pairs={{0,8},{8,0},{16,24},{24,16},{1,9},{9,1},{17,25},{25,17},{2,10},{10... | collective-permute-start | bytes 3145736 | tf_op jit(solution)/shard_map/ppermute | solution.py:24
  129.4 3.7 %collective-permute-start.20 = (bf16[256,2048]{1,0:T(8,128)(2,1)}, bf16[256,2048]{1,0:T(8,128)(2,1)}, u32[]{:S(2)}, u32[]{:S(2)}) collective-permute-start(bf16[256,2048]{1,0:T(8,128)(2,1)} %collective-permute-done.18.refs_1_), channel_id=1, source_target_pairs={{0,8},{8,0},{16,24},{24,16},{1,9},{9,1},{17,25},{25,17},{2,10},{10... | collective-permute-start | bytes 3145736 | tf_op jit(solution)/shard_map/ppermute | solution.py:24
  129.9 4.1 %collective-permute-start.17 = (bf16[256,2048]{1,0:T(8,128)(2,1)}, bf16[256,2048]{1,0:T(8,128)(2,1)}, u32[]{:S(2)}, u32[]{:S(2)}) collective-permute-start(bf16[256,2048]{1,0:T(8,128)(2,1)} %collective-permute-done.15.refs_0_), channel_id=1, source_target_pairs={{0,8},{8,0},{16,24},{24,16},{1,9},{9,1},{17,25},{25,17},{2,10},{10... | collective-permute-start | bytes 3145736 | tf_op jit(solution)/shard_map/ppermute | solution.py:24
  129.9 32.5 %collective-permute-start.22 = (bf16[256,2048]{1,0:T(8,128)(2,1)}, bf16[256,2048]{1,0:T(8,128)(2,1)}, u32[]{:S(2)}, u32[]{:S(2)}) collective-permute-start(bf16[256,2048]{1,0:T(8,128)(2,1)} %refs_4_.3), channel_id=1, source_target_pairs={{0,20},{4,16},{8,28},{12,24},{16,4},{20,0},{24,12},{28,8},{1,21},{... | collective-permute-start | bytes 3145736 | tf_op jit(solution)/shard_map/ppermute | solution.py:96
  130.9 48.2 %collective-permute-start.16 = (bf16[256,2048]{1,0:T(8,128)(2,1)}, bf16[256,2048]{1,0:T(8,128)(2,1)}, u32[]{:S(2)}, u32[]{:S(2)}) collective-permute-start(bf16[256,2048]{1,0:T(8,128)(2,1)} %get-tuple-element.84.normed_hbm.refs_0_), channel_id=1, source_target_pairs={{0,20},{4,16},{8,28},{12,24},{16,4},{20,0},{24,12},{28,8},{1,21},{... | collective-permute-start | bytes 3145736 | tf_op jit(solution)/shard_map/ppermute | solution.py:96
  132.9 81.1 %all-gather.6.cloned.1.call-start = ((), (), s32[]{:S(2)}) async-start(), calls=%async_computation.5 | async-start | bytes 1310720 | tf_op jit(solution)/shard_map/all_gather | solution.py:951
  162.4 16.8 %collective-permute-start.23 = (bf16[256,2048]{1,0:T(8,128)(2,1)}, bf16[256,2048]{1,0:T(8,128)(2,1)}, u32[]{:S(2)}, u32[]{:S(2)}) collective-permute-start(bf16[256,2048]{1,0:T(8,128)(2,1)} %collective-permute-done.22.refs_5_), channel_id=1, source_target_pairs={{0,8},{8,0},{16,24},{24,16},{1,9},{9,1},{17,25},{25,17},{2,10},{10... | collective-permute-start | bytes 3145736 | tf_op jit(solution)/shard_map/ppermute | solution.py:24
  179.1 3.0 collective-permute-start.21
  179.2 67.4 %reduce-scatter.5.cloned.1.call-start = ((), (), s32[]{:S(2)}) async-start(), calls=%async_computation.4 | async-start | bytes 1310720 | tf_op jit(solution)/shard_map/reduce_scatter | solution.py:104
  213.7 74.0 %all-gather.8.cloned.1.call-start = ((), (), s32[]{:S(2)}) async-start(), calls=%async_computation.6 | async-start | bytes 4718592 | tf_op jit(solution)/shard_map/all_gather | solution.py:100
  224.9 2.9 collective-permute-start.25
  225.1 8.7 %collective-permute-start.24 = (bf16[256,512]{1,0:T(8,128)(2,1)S(1)}, bf16[256,512]{1,0:T(8,128)(2,1)}, u32[]{:S(2)}, u32[]{:S(2)}) collective-permute-start(bf16[256,512]{1,0:T(8,128)(2,1)S(1)} %copy-done.17), channel_id=1, source_target_pairs={{0,4},{4,0},{1,5},{5,1},{2,6},{6,2},{3,7},{7,3},{8,12},{12,8},{9,1... | collective-permute-start | bytes 786440 | tf_op jit(solution)/shard_map/ppermute | solution.py:998
  237.1 9.5 %collective-permute-start.27 = (bf16[2048,768]{1,0:T(8,128)(2,1)}, bf16[2048,768]{1,0:T(8,128)(2,1)}, u32[]{:S(2)}, u32[]{:S(2)}) collective-permute-start(bf16[2048,768]{1,0:T(8,128)(2,1)} %get-tuple-element.95.refs_16_), channel_id=1, source_target_pairs={{0,8},{8,0},{16,24},{24,16},{1,9},{9,1},{17,25},{25,17},{2,10},{10... | collective-permute-start | bytes 9437192 | tf_op jit(solution)/shard_map/ppermute | solution.py:24
  237.2 12.4 %collective-permute-start.28 = (bf16[2048,768]{1,0:T(8,128)(2,1)}, bf16[2048,768]{1,0:T(8,128)(2,1)}, u32[]{:S(2)}, u32[]{:S(2)}) collective-permute-start(bf16[2048,768]{1,0:T(8,128)(2,1)} %get-tuple-element.114), channel_id=1, source_target_pairs={{0,8},{8,0},{16,24},{24,16},{1,9},{9,1},{17,25},{25,17},{2,10},{10... | collective-permute-start | bytes 9437192 | tf_op jit(solution)/shard_map/ppermute | solution.py:24
  237.7 14.5 %collective-permute-start.29 = (bf16[768,2048]{1,0:T(8,128)(2,1)}, bf16[768,2048]{1,0:T(8,128)(2,1)}, u32[]{:S(2)}, u32[]{:S(2)}) collective-permute-start(bf16[768,2048]{1,0:T(8,128)(2,1)} %get-tuple-element.115), channel_id=1, source_target_pairs={{0,8},{8,0},{16,24},{24,16},{1,9},{9,1},{17,25},{25,17},{2,10},{10... | collective-permute-start | bytes 9437192 | tf_op jit(solution)/shard_map/ppermute | solution.py:24
  243.9 20.5 %collective-permute-start.30 = (bf16[272,512]{1,0:T(8,128)(2,1)}, bf16[272,512]{1,0:T(8,128)(2,1)}, u32[]{:S(2)}, u32[]{:S(2)}) collective-permute-start(bf16[272,512]{1,0:T(8,128)(2,1)} %get-tuple-element.122), channel_id=1, source_target_pairs={{0,1},{1,0},{2,3},{3,2},{4,5},{5,4},{6,7},{7,6},{8,9},{9,8},{10,11... | collective-permute-start | bytes 835592 | tf_op jit(solution)/shard_map/ppermute | solution.py:24
  246.2 21.2 %collective-permute-start.37 = (bf16[128,2048]{1,0:T(8,128)(2,1)}, bf16[128,2048]{1,0:T(8,128)(2,1)}, u32[]{:S(2)}, u32[]{:S(2)}) collective-permute-start(bf16[128,2048]{1,0:T(8,128)(2,1)} %get-tuple-element.142), channel_id=1, source_target_pairs={{0,4},{4,0},{8,12},{12,8},{16,20},{20,16},{24,28},{28,24},{1,5},{5... | collective-permute-start | bytes 1572872 | tf_op jit(solution)/shard_map/ppermute | solution.py:96
  246.6 20.8 %collective-permute-start.35 = (bf16[128,2048]{1,0:T(8,128)(2,1)}, bf16[128,2048]{1,0:T(8,128)(2,1)}, u32[]{:S(2)}, u32[]{:S(2)}) collective-permute-start(bf16[128,2048]{1,0:T(8,128)(2,1)} %get-tuple-element.141), channel_id=1, source_target_pairs={{0,16},{4,20},{8,24},{12,28},{16,0},{20,4},{24,8},{28,12},{1,17},{... | collective-permute-start | bytes 1572872 | tf_op jit(solution)/shard_map/ppermute | solution.py:96
  249.6 17.8 %collective-permute-start.26 = (bf16[272,512]{1,0:T(8,128)(2,1)}, bf16[272,512]{1,0:T(8,128)(2,1)}, u32[]{:S(2)}, u32[]{:S(2)}) collective-permute-start(bf16[272,512]{1,0:T(8,128)(2,1)} %get-tuple-element.113), channel_id=1, source_target_pairs={{0,1},{1,0},{2,3},{3,2},{4,5},{5,4},{6,7},{7,6},{8,9},{9,8},{10,11... | collective-permute-start | bytes 835592 | tf_op jit(solution)/shard_map/ppermute | solution.py:24
  265.5 14.5 %collective-permute-start.31 = (bf16[272,512]{1,0:T(8,128)(2,1)S(1)}, bf16[272,512]{1,0:T(8,128)(2,1)S(1)}, u32[]{:S(2)}, u32[]{:S(2)}) collective-permute-start(bf16[272,512]{1,0:T(8,128)(2,1)S(1)} %add_convert_fusion.5.refs_4_), channel_id=1, source_target_pairs={{0,2},{1,3},{2,0},{3,1},{4,6},{5,7},{6,4},{7,5},{8,10},{9,11},{10,... | collective-permute-start | bytes 835592 | tf_op jit(solution)/shard_map/ppermute | solution.py:24
  282.9 4.8 %collective-permute-start.32 = (f32[1280]{0:T(1024)S(1)}, f32[1280]{0:T(1024)S(1)}, u32[]{:S(2)}, u32[]{:S(2)}) collective-permute-start(f32[1280]{0:T(1024)S(1)} %pad_maximum_fusion.2), channel_id=1, source_target_pairs={{0,8},{8,0},{16,24},{24,16},{1,9},{9,1},{17,25},{25,17},{2,10},{10... | collective-permute-start | bytes 15368 | tf_op jit(solution)/shard_map/ppermute | solution.py:24
  285.8 17.3 %collective-permute-start.36 = (bf16[128,2048]{1,0:T(8,128)(2,1)}, bf16[128,2048]{1,0:T(8,128)(2,1)}, u32[]{:S(2)}, u32[]{:S(2)}) collective-permute-start(bf16[128,2048]{1,0:T(8,128)(2,1)} %get-tuple-element.130), channel_id=1, source_target_pairs={{0,4},{4,0},{8,12},{12,8},{16,20},{20,16},{24,28},{28,24},{1,5},{5... | collective-permute-start | bytes 1572872 | tf_op jit(solution)/shard_map/ppermute | solution.py:96
  286.9 17.6 %collective-permute-start.38 = (bf16[128,2048]{1,0:T(8,128)(2,1)}, bf16[128,2048]{1,0:T(8,128)(2,1)}, u32[]{:S(2)}, u32[]{:S(2)}) collective-permute-start(bf16[128,2048]{1,0:T(8,128)(2,1)} %get-tuple-element.133), channel_id=1, source_target_pairs={{0,16},{4,20},{8,24},{12,28},{16,0},{20,4},{24,8},{28,12},{1,17},{... | collective-permute-start | bytes 1572872 | tf_op jit(solution)/shard_map/ppermute | solution.py:96
  304.5 8.9 %collective-permute-start.39 = (bf16[128,2048]{1,0:T(8,128)(2,1)S(1)}, bf16[128,2048]{1,0:T(8,128)(2,1)S(1)}, u32[]{:S(2)}, u32[]{:S(2)}) collective-permute-start(bf16[128,2048]{1,0:T(8,128)(2,1)S(1)} %add_convert_fusion.3), channel_id=1, source_target_pairs={{0,8},{8,0},{16,24},{24,16},{1,9},{9,1},{17,25},{25,17},{2,10},{10... | collective-permute-start | bytes 1572872 | tf_op jit(solution)/shard_map/ppermute | solution.py:24
  304.6 3.7 %collective-permute-start.33 = (f32[1280]{0:T(1024)S(1)}, f32[1280]{0:T(1024)S(1)}, u32[]{:S(2)}, u32[]{:S(2)}) collective-permute-start(f32[1280]{0:T(1024)S(1)} %fusion.8), channel_id=1, source_target_pairs={{0,16},{4,20},{8,24},{12,28},{16,0},{20,4},{24,8},{28,12},{1,17},{... | collective-permute-start | bytes 15368 | tf_op jit(solution)/shard_map/ppermute | solution.py:96
  307.2 6.1 %collective-permute-start.40 = (bf16[128,2048]{1,0:T(8,128)(2,1)S(1)}, bf16[128,2048]{1,0:T(8,128)(2,1)S(1)}, u32[]{:S(2)}, u32[]{:S(2)}) collective-permute-start(bf16[128,2048]{1,0:T(8,128)(2,1)S(1)} %add_convert_fusion.1), channel_id=1, source_target_pairs={{0,8},{8,0},{16,24},{24,16},{1,9},{9,1},{17,25},{25,17},{2,10},{10... | collective-permute-start | bytes 1572872 | tf_op jit(solution)/shard_map/ppermute | solution.py:24
  308.3 3.9 %collective-permute-start.34 = (f32[1280]{0:T(1024)S(1)}, f32[1280]{0:T(1024)S(1)}, u32[]{:S(2)}, u32[]{:S(2)}) collective-permute-start(f32[1280]{0:T(1024)S(1)} %add.93), channel_id=1, source_target_pairs={{0,4},{4,0},{8,12},{12,8},{16,20},{20,16},{24,28},{28,24},{1,5},{5... | collective-permute-start | bytes 15368 | tf_op jit(solution)/shard_map/ppermute | solution.py:96
  (17 other events, 98.8 us)
Sparse Core Ops, SparseCore 0:
  48.8 55.0 all-gather.3
  237.2 39.3 all-gather.7
Sparse Core Ops, SparseCore 1:
  133.0 25.6 reduce-scatter.2
  179.2 26.5 all-gather.5
  213.8 25.5 reduce-scatter.4

commit v3 on v2

--- a/solution.py
+++ b/solution.py
@@ -65,10 +65,11 @@
     return pieces
 
 
-def second_half(pieces, axis, *earlier):
+def second_half(pieces, axis, later=()):
+    pieces = dict(pieces)
     for bit in bits_of(lax.axis_size(axis))[1:]:
         for s in [s for s in sorted(pieces, reverse=True) if not s & bit]:
-            other = swap(order_after(pieces.pop(s | bit), *earlier), axis, bit)
+            other = order_after(swap(pieces.pop(s | bit), axis, bit), *later)
             pieces[s] = (pieces[s].astype(F32) + other.astype(F32)).astype(BF if s else F32)
     return pieces[0]
 
@@ -94,6 +95,14 @@
         return value
     size = lax.axis_size("dp") * lax.axis_size("ctx")
     return lax.ppermute(value, ("dp", "ctx"), [(i, i ^ mask) for i in range(size)])
+
+
+def pass_on(parts, masks, highest, *earlier):
+    parts = list(parts)
+    for mask in masks[len(parts) :]:
+        bit = 1 << (mask.bit_length() - 1) if highest else mask & -mask
+        parts.append(send_plane(order_after(parts[masks.index(mask ^ bit)], *earlier), bit))
+    return parts
 
 
 def plane_all(value):
@@ -355,10 +364,10 @@
         cols = pl.ds(pl.multiple_of(t * tile, tile), tile)
         gate_copy, up_copy, down_copy = weights(t)
         gate_copy.wait()
+        gate = dot(normed[...], wg[:, cols])
         up_copy.wait()
+        up = dot(normed[...], wu[:, cols])
         down_copy.wait()
-        gate = dot(normed[...], wg[:, cols])
-        up = dot(normed[...], wu[:, cols])
         grad_hidden = dot_nt(cot[...], wd[cols, :])
         hidden, grad_gate, grad_up = gated_terms(gate, up, grad_hidden)
         total[...] += dot_nt(grad_gate.astype(BF), wg[:, cols]) + dot_nt(
@@ -527,7 +536,7 @@
     row_sems, cot_sems, weight_sems, held_sems, out_sems = refs
     width = rows.shape[1]
     size = rows_hbm[0].shape[0]
-    group = min(2, parts)
+    group = 2 if parts % 2 == 0 else 1
     chunk = group * size
     steps = wg_hbm.shape[1] // block // 2
     tile = width // 2
@@ -861,6 +870,12 @@
     x_pieces = gather_pieces(inputs, "tensor")
     cot_parts = [send_plane(cotangent, mask) for mask in masks[:first_masks + 1]]
     cosine, sine = rope_tables(positions[0])
+    segment_row = segments[0]
+    row_segment = lax.dynamic_slice_in_dim(segment_row, place * count, count)[:, None]
+    key_segments = [
+        lax.dynamic_slice_in_dim(segment_row, (place ^ s) * count, count)[None]
+        for s in range(blocks)
+    ]
     normed_one, kv_rows, key_raw, inverse_one = kernel_call(
         functools.partial(key_value_body, tensor),
         ids,
@@ -873,10 +888,10 @@
         ],
         4 * count * width * kv_width,
         "key_value",
-        after=cot_parts[1:],
+        after=[*cot_parts[1:], row_segment, *key_segments],
     )
     kv_pieces = gather_pieces(kv_rows, "ctx")
-    all_normed_one = plane_all(order_after(normed_one, *kv_pieces[1:]))
+    all_normed_one = plane_all(normed_one)
     query_rows, query_raw = kernel_call(
         query_body,
         ids,
@@ -886,12 +901,6 @@
         "query",
     )
 
-    segment_row = segments[0]
-    row_segment = lax.dynamic_slice_in_dim(segment_row, place * count, count)[:, None]
-    key_segments = [
-        lax.dynamic_slice_in_dim(segment_row, (place ^ s) * count, count)[None]
-        for s in range(blocks)
-    ]
     mixed_rows, *branch_pieces = kernel_call(
         functools.partial(attention_body, tensor, group, blocks),
         ids,
@@ -920,10 +929,8 @@
     )
     feed_done = feed_part
     grad_two_part = sum_tensor(grad_two_part)
-    late = order_after(normed_two, feed_done)
-    two_parts += [send_plane(late, mask) for mask in masks[first_masks + 1 :]]
-    late = order_after(cotangent, feed_done)
-    cot_parts += [send_plane(late, mask) for mask in masks[first_masks + 1 :]]
+    two_parts = pass_on(two_parts, masks, True, feed_done)
+    cot_parts = pass_on(cot_parts, masks, False, feed_done)
     groups = [slice(0, first_masks), slice(first_masks, None)] if len(masks) > 1 else [slice(0, None)]
     last = len(groups) - 1
     two_partners = partners(two_parts[:1]) + partners(two_parts[1 : first_masks + 1], feed_done)
@@ -1024,7 +1031,7 @@
         [shape(count, q_width + 2 * kv_width), shape(1, HD, dtype=F32)],
         40 * count * kv_width,
         "key_backward",
-        after=[output_part],
+        after=output_parts,
     )
     all_grad_low = plane_all(grad_low)
     first_parts = output_parts
@@ -1047,22 +1054,20 @@
         2 * count * width * (q_width + 2 * kv_width),
         "first_grad",
     )
-    outputs = (resid_part.astype(F32) + order_after(feed, grad_one_pieces[0]).astype(F32)).astype(BF)
-    grad_gate_w, grad_up_w, grad_down_w = assemble(ids, lows, block, held, [outputs])
+    grad_gate_w, grad_up_w, grad_down_w = assemble(ids, lows, block, held, grad_one_pieces[:1])
+    outputs = (resid_part.astype(F32) + order_after(feed, grad_gate_w).astype(F32)).astype(BF)
 
     grad_one = first_half(grad_one_pieces, "tensor", grad_gate_w)
     grad_query_w, grad_key_w, grad_value_w = projection_weights(
         ids, [all_normed_one], [all_grad_low], q_width, kv_width, [grad_gate_w, *grad_one.values()]
     )
 
-    grad_one = second_half(grad_one, "tensor")
+    grad_one = second_half(grad_one, "tensor", [grad_query_w])
     grad_one_part = grad_one[:count]
     small = grad_one[count + 1 : count + 1 + (count + 2 * HD) // shard].reshape(-1)
     row_total_one = small[:count, None]
     feed_part_sums = lax.dynamic_slice_in_dim(feed_sums[0], column, shard)
     small = jnp.concatenate([grad_one[count], feed_part_sums, small[count:]])
-    if has_pair():
-        small = small + swap(small, "dp", 1)
     unit_one_part = inputs.astype(F32) * inverse_one
     grad_inputs = (
         grad_resid_part
@@ -1073,7 +1078,8 @@
     output_parts = summed(first_parts, (bits[0], bits[-1]), (), [grad_gate_w])
     for i in range(1, len(bits)):
         output_parts = summed(output_parts, (bits[i], bits[-1 - i]), [grad_gate_w], [grad_query_w])
-    small = order_after(small, grad_query_w)
+    if has_pair():
+        small = small + swap(small, "dp", 1)
     for bit in bits:
         small = small + send_plane(small, bit)
     grad_attention_gain = small[:shard]

time: 324 us -> 301 us (0.929)
  waiting for transfers between devices: 83.4 us -> 62.9 us
    ppermute x12, waiting for transfers between devices: 19 us -> 3.77 us  [send_plane(): lax.ppermute(value, ('dp', 'ctx'), [(i, i ^ mask) for i in range(size)])]
    ppermute x28, waiting for transfers between devices: 60.8 us -> 47.7 us  [swap(): return lax.ppermute(value, axis, [(i, i ^ bit) for i in range(size)])]
    all_gather x2, waiting for transfers between devices: 0.02 us -> 8.87 us  [plane_all(): return lax.all_gather(value, ('dp', 'ctx'), axis=0, tiled=True)]
  transfers between devices with their start and end apart: 46 -> 46, of which waited for: 20 -> 23; matrix products, arithmetic and copies ran while one was open for 10% -> 11% of each run, Pallas kernels for 42% -> 45%
where the time goes in v3:
time: 301 us; the launch traced here: 299 us
  Pallas kernels  140 us (47%)
  waiting for transfers between devices  62.9 us (21%)
  starting transfers between devices  39.9 us (13%)
  other arithmetic  27.1 us (9%)
  between operations  16.1 us (5%)
  local copies, waits for them, and re-layouts  10.8 us (4%)
    pallas_call x2, Pallas kernels, feed_weights(): pl.pallas_call(functools.partial(feed_weight_body, parts, extra, last, bl...  59.9 us
    ppermute x28, waiting for transfers between devices, swap(): return lax.ppermute(value, axis, [(i, i ^ bit) for i in range(size)])  47.7 us
    pallas_call x7, Pallas kernels, kernel_call(): pl.pallas_call(run, out_shape=tuple(outs), in_specs=[SMEM] + [ANY] * (cou...  36.4 us
    ppermute x28, starting transfers between devices, swap(): return lax.ppermute(value, axis, [(i, i ^ bit) for i in range(size)])  22.6 us
    ppermute x12, starting transfers between devices, send_plane(): lax.ppermute(value, ('dp', 'ctx'), [(i, i ^ mask) for i in range(size)])  16.6 us
    pallas_call x1, Pallas kernels, feed_forward(): pl.pallas_call(functools.partial(feed_forward_body, tile, len(after)), ou...  16.3 us
    pallas_call x1, Pallas kernels, projection_weights(): pl.pallas_call(functools.partial(projection_body, parts, tile, len(after)...  15.4 us
    pallas_call x1, Pallas kernels, assemble(): pl.pallas_call(functools.partial(assemble_body, len(after)), out_shape=[s...  11.8 us
  transfers between devices with their start and end apart: 46, of which 23 were waited for; matrix products, arithmetic and copies ran while one was open for 11% of the time, Pallas kernels for 45%

profile of v3, /device:TPU:0, one launch (start us, length us, event | category | flops | bytes accessed | tf_op | source)
XLA Modules:
  0.0 298.7 jit_solution(1297682433186295594)
XLA Ops:
  8.1 3.0 %collective-permute-start.3 = (bf16[256,2048]{1,0:T(8,128)(2,1)}, bf16[256,2048]{1,0:T(8,128)(2,1)S(1)}, u32[]{:S(2)}, u32[]{:S(2)}) collective-permute-start(bf16[256,2048]{1,0:T(8,128)(2,1)} %refs_4_.3), channel_id=1, source_target_pairs={{0,16},{4,20},{8,24},{12,28},{16,0},{20,4},{24,8},{28,12},{1,17},{... | collective-permute-start | bytes 3145736 | tf_op jit(solution)/shard_map/ppermute | solution.py:97
  11.1 1.5 collective-permute-start.4
  12.6 2.6 collective-permute-start.1
  15.2 1.6 collective-permute-start
  20.1 6.8 %collective-permute-done.1.refs_2_ = bf16[256,512]{1,0:T(8,128)(2,1)S(1)} collective-permute-done((bf16[256,512]{1,0:T(8,128)(2,1)}, bf16[256,512]{1,0:T(8,128)(2,1)S(1)}, u32[]{:S(2)}, u32[]{:S(2)}) %collective-permute-start.1) | collective-permute-done | bytes 262176 | tf_op jit(solution)/shard_map/ppermute | solution.py:24
  32.2 2.6 collective-permute-done.2.refs_3_
  36.9 4.6 %key_value.1 = (bf16[256,2048]{1,0:T(8,128)(2,1)}, bf16[256,512]{1,0:T(8,128)(2,1)}, f32[256,256]{1,0:T(8,128)}, f32[256,1]{1,0:T(8,128)}) custom-call(s32[4]{0:T(128)} %pad_add_fusion.ids, bf16[256,512]{1,0:T(8,128)(2,1)} %refs_0_.3, bf16[256,512]{1,0:T(8,128)(2,1)} %copy-done.7, bf16[256,512]{1,0:T(8,128)(2,1)} %copy-done.6, bf16[256,512]{1,0:T(8,128)(2,1)} %copy-done.8, ...), custom_call_target="tpu_custom_call" | custom-call | flops 536870912 | bytes 4990464 | tf_op jit(solution)/shard_map/key_value/pallas_call | solution.py:200
  41.5 1.6 collective-permute-start.5
  43.7 4.4 %query.1 = (bf16[256,512]{1,0:T(8,128)(2,1)}, f32[256,512]{1,0:T(8,128)}) custom-call(s32[4]{0:T(128)} %pad_add_fusion.ids, bf16[256,2048]{1,0:T(8,128)(2,1)} %get-tuple-element.73.refs_0_, bf16[2048,512]{1,0:T(8,128)(2,1)} %refs_9_.7, f32[1,128]{1,0:T(1,128)} %bitcast_convert_fusion.1.refs_2_.refs_13_, ...), custom_call_target="tpu_custom_call" | custom-call | flops 536870912 | bytes 4194816 | tf_op jit(solution)/shard_map/query/pallas_call | solution.py:200
  48.8 5.5 %attention.1 = (bf16[256,512]{1,0:T(8,128)(2,1)}, bf16[256,512]{1,0:T(8,128)(2,1)}, bf16[256,512]{1,0:T(8,128)(2,1)}, bf16[256,512]{1,0:T(8,128)(2,1)}, bf16[256,512]{1,0:T(8,128)(2,1)}) custom-call(s32[4]{0:T(128)} %pad_add_fusion.ids, bf16[256,512]{1,0:T(8,128)(2,1)} %get-tuple-element.74.refs_0_.refs_6_, s32[256,1]{1,0:T(8,128)} %copy.34.refs_12_.refs_1_.refs_7_, ...), custom_call_target="tpu_custom_call" | custom-call | flops 805306368 | bytes 4197376 | tf_op jit(solution)/shard_map/attention/pallas_call | solution.py:200
  54.3 2.2 collective-permute-start.7
  57.1 6.2 %collective-permute-done.7 = bf16[256,512]{1,0:T(8,128)(2,1)S(1)} collective-permute-done((bf16[256,512]{1,0:T(8,128)(2,1)}, bf16[256,512]{1,0:T(8,128)(2,1)S(1)}, u32[]{:S(2)}, u32[]{:S(2)}) %collective-permute-start.7) | collective-permute-done | bytes 262176 | tf_op jit(solution)/shard_map/ppermute | solution.py:24
  64.4 3.7 %collective-permute-start.8 = (bf16[256,512]{1,0:T(8,128)(2,1)S(1)}, bf16[256,512]{1,0:T(8,128)(2,1)S(1)}, u32[]{:S(2)}, u32[]{:S(2)}) collective-permute-start(bf16[256,512]{1,0:T(8,128)(2,1)S(1)} %add_convert_fusion.7), channel_id=1, source_target_pairs={{0,2},{1,3},{2,0},{3,1},{4,6},{5,7},{6,4},{7,5},{8,10},{9,11},{10,... | collective-permute-start | bytes 786440 | tf_op jit(solution)/shard_map/ppermute | solution.py:24
  68.1 2.0 collective-permute-done.6
  70.1 9.0 %collective-permute-done.8 = bf16[256,512]{1,0:T(8,128)(2,1)S(1)} collective-permute-done((bf16[256,512]{1,0:T(8,128)(2,1)S(1)}, bf16[256,512]{1,0:T(8,128)(2,1)S(1)}, u32[]{:S(2)}, u32[]{:S(2)}) %collective-permute-start.8) | collective-permute-done | bytes 262176 | tf_op jit(solution)/shard_map/ppermute | solution.py:24
  81.0 3.6 %collective-permute-start.9 = (bf16[256,512]{1,0:T(8,128)(2,1)S(1)}, bf16[256,512]{1,0:T(8,128)(2,1)S(1)}, u32[]{:S(2)}, u32[]{:S(2)}) collective-permute-start(bf16[256,512]{1,0:T(8,128)(2,1)S(1)} %fusion.1.refs_0_), channel_id=1, source_target_pairs={{0,1},{1,0},{2,3},{3,2},{4,5},{5,4},{6,7},{7,6},{8,9},{9,8},{10,11... | collective-permute-start | bytes 786440 | tf_op jit(solution)/shard_map/ppermute | solution.py:24
  84.6 5.0 %collective-permute-done.10.refs_2_ = bf16[256,512]{1,0:T(8,128)(2,1)S(1)} collective-permute-done((bf16[256,512]{1,0:T(8,128)(2,1)S(1)}, bf16[256,512]{1,0:T(8,128)(2,1)S(1)}, u32[]{:S(2)}, u32[]{:S(2)}) %collective-permute-start.10) | collective-permute-done | bytes 262176 | tf_op jit(solution)/shard_map/ppermute | solution.py:24
  89.6 2.1 collective-permute-start.11
  94.3 1.8 collective-permute-done.11.refs_3_
  96.8 3.7 %second_norm.1 = (bf16[256,2048]{1,0:T(8,128)(2,1)}, bf16[256,2048]{1,0:T(8,128)(2,1)}, f32[256,1]{1,0:T(8,128)}) custom-call(s32[4]{0:T(128)} %pad_add_fusion.ids, bf16[256,512]{1,0:T(8,128)(2,1)} %copy-done.3, bf16[256,512]{1,0:T(8,128)(2,1)} %copy-done.13, bf16[256,512]{1,0:T(8,128)(2,1)} %copy-done.12, bf16[256,512]{1,0:T(8,128)(2,1)} %copy-done.14, ...), custom_call_target="tpu_custom_call" | custom-call | flops 4194304 | bytes 3154944 | tf_op jit(solution)/shard_map/second_norm/pallas_call | solution.py:200
  101.1 4.8 %collective-permute-start.15 = (bf16[256,2048]{1,0:T(8,128)(2,1)}, bf16[256,2048]{1,0:T(8,128)(2,1)}, u32[]{:S(2)}, u32[]{:S(2)}) collective-permute-start(bf16[256,2048]{1,0:T(8,128)(2,1)} %get-tuple-element.80.normed_hbm.refs_0_), channel_id=1, source_target_pairs={{0,4},{4,0},{8,12},{12,8},{16,20},{20,16},{24,28},{28,24},{1,5},{5... | collective-permute-start | bytes 3145736 | tf_op jit(solution)/shard_map/ppermute | solution.py:97
  105.9 16.3 %feed_forward.1 = (bf16[256,2048]{1,0:T(8,128)(2,1)}, bf16[256,2048]{1,0:T(8,128)(2,1)}) custom-call(s32[4]{0:T(128)} %pad_add_fusion.ids, bf16[256,2048]{1,0:T(8,128)(2,1)} %get-tuple-element.80.normed_hbm.refs_0_, bf16[256,2048]{1,0:T(8,128)(2,1)} %refs_4_.3, bf16[2048,1536]{1,0:T(8,128)(2,1)} %refs_8_.5, bf16[2048,1536]{1,0:T(8,128)(2,1)} %refs_9_.6, ...), custom_call_target="tpu_custom_call" | custom-call | flops 9663676416 | bytes 23068672 | tf_op jit(solution)/shard_map/feed_forward/pallas_call | solution.py:391
  124.0 1.6 collective-permute-start.16
  126.2 1.5 collective-permute-done.17.refs_14_.refs_2_
  127.7 28.5 %feed_weights.2 = (f32[2048,1536]{1,0:T(8,128)}, f32[2048,1536]{1,0:T(8,128)}, f32[1536,2048]{1,0:T(8,128)}) custom-call(s32[4]{0:T(128)} %pad_add_fusion.ids, bf16[256,2048]{1,0:T(8,128)(2,1)} %get-tuple-element.80.normed_hbm.refs_0_, bf16[256,2048]{1,0:T(8,128)(2,1)} %collective-permute-done.18.refs_1_, ...), custom_call_target="tpu_custom_call" | custom-call | flops 19327352832 | bytes 8388608 | tf_op jit(solution)/shard_map/feed_weights/pallas_call | solution.py:691
  156.9 2.4 collective-permute-done.23.refs_7_
  159.3 1.5 collective-permute-done.21.refs_3_
  160.8 31.4 %feed_weights.3 = (f32[2048,1536]{1,0:T(8,128)}, f32[2048,1536]{1,0:T(8,128)}, f32[1536,2048]{1,0:T(8,128)}, bf16[2048,768]{1,0:T(8,128)(2,1)}, bf16[2048,768]{1,0:T(8,128)(2,1)}, /*index=5*/bf16[768,2048]{1,0:T(8,128)(2,1)}) custom-call(s32[4]{0:T(128)} %pad_add_fusion.ids, ...), custom_call_target="tpu_custom_call", output_to_operand_aliasing={{0}: (12, {}), {1}: (13, {}), {2}: (14, {})} | custom-call | flops 19327352832 | bytes 8388608 | tf_op jit(solution)/shard_map/feed_weights/pallas_call | solution.py:691
  192.6 8.6 %middle.1 = (f32[256,512]{1,0:T(8,128)}, bf16[256,2048]{1,0:T(8,128)(2,1)}, f32[1,2048]{1,0:T(1,128)}, bf16[256,512]{1,0:T(8,128)(2,1)}, f32[1,128]{1,0:T(1,128)...) custom-call(s32[4]{0:T(128)} %pad_add_fusion.ids, bf16[256,2048]{1,0:T(8,128)(2,1)} %all-gather.6.cloned.1.call-done.refs_0_, ...), custom_call_target="tpu_custom_call" | custom-call | flops 536870912 | bytes 9458688 | tf_op jit(solution)/shard_map/middle/pallas_call | solution.py:200
  201.2 2.1 convolution_convert_fusion
  203.6 2.6 collective-permute-done.28
  206.3 1.6 add_convert_fusion
  209.9 2.4 collective-permute-done.27.refs_1_
  212.3 3.3 %key_backward.1 = (bf16[256,1024]{1,0:T(8,128)(2,1)}, f32[1,128]{1,0:T(1,128)}) custom-call(s32[4]{0:T(128)} %pad_add_fusion.ids, f32[256,512]{1,0:T(8,128)} %get-tuple-element.103.refs_0_, bf16[256,512]{1,0:T(8,128)(2,1)} %collective-permute-done.27.refs_1_, f32[256,256]{1,0:T(8,128)} %get-tuple-element.105.refs_2_, ...), custom_call_target="tpu_custom_call" | custom-call | flops 2621440 | bytes 2098176 | tf_op jit(solution)/shard_map/key_backward/pallas_call | solution.py:200
  218.9 6.4 %first_grad.1 = (bf16[272,512]{1,0:T(8,128)(2,1)}, bf16[272,512]{1,0:T(8,128)(2,1)}, bf16[272,512]{1,0:T(8,128)(2,1)}, bf16[272,512]{1,0:T(8,128)(2,1)}) custom-call(s32[4]{0:T(128)} %pad_add_fusion.ids, bf16[256,512]{1,0:T(8,128)(2,1)} %refs_0_.3, bf16[256,512]{1,0:T(8,128)(2,1)} %copy-done.7, bf16[256,512]{1,0:T(8,128)(2,1)} %copy-done.6, ...), custom_call_target="tpu_custom_call" | custom-call | flops 1073741824 | bytes 6891520 | tf_op jit(solution)/shard_map/first_grad/pallas_call | solution.py:200
  227.4 3.2 %collective-permute-done.26.down_low = bf16[768,2048]{1,0:T(8,128)(2,1)} collective-permute-done((bf16[768,2048]{1,0:T(8,128)(2,1)}, bf16[768,2048]{1,0:T(8,128)(2,1)}, u32[]{:S(2)}, u32[]{:S(2)}) %collective-permute-start.26) | collective-permute-done | bytes 3145760 | tf_op jit(solution)/shard_map/ppermute | solution.py:24
  230.7 11.8 %assemble.1 = (f32[2048,1536]{1,0:T(8,128)}, f32[2048,1536]{1,0:T(8,128)}, f32[1536,2048]{1,0:T(8,128)}) custom-call(s32[4]{0:T(128)} %pad_add_fusion.ids, bf16[2048,768]{1,0:T(8,128)(2,1)} %collective-permute-done.24.gate_low, bf16[2048,768]{1,0:T(8,128)(2,1)} %collective-permute-done.25.up_low, ...), custom_call_target="tpu_custom_call", output_to_operand_aliasing={{0}: (4, {}), {1}: (5, {}), {2}: (6, {})} | custom-call | bytes 28311552 | tf_op jit(solution)/shard_map/assemble/pallas_call | solution.py:726
  242.5 2.9 add_convert_fusion.4
  246.7 1.8 add_convert_fusion.5.refs_4_
  248.5 1.8 add_convert_fusion.6
  250.3 1.8 convert_add_fusion.2.refs_3_
  252.1 8.9 %all-gather.8.cloned.1.call-done.refs_1_ = bf16[2048,1024]{1,0:T(8,128)(2,1)} async-done(((bf16[256,1024]{1,0:T(8,128)(2,1)}), bf16[2048,1024]{1,0:T(8,128)(2,1)}) %all-gather.8.cloned.1.call-update) | async-done | bytes 4194320 | tf_op jit(solution)/shard_map/all_gather | solution.py:109
  261.0 15.4 %projection_weights.1 = (f32[2048,512]{1,0:T(8,128)}, f32[2048,256]{1,0:T(8,128)}, f32[2048,256]{1,0:T(8,128)}) custom-call(s32[4]{0:T(128)} %pad_add_fusion.ids, bf16[2048,2048]{1,0:T(8,128)(2,1)} %all-gather.4.cloned.1.call-done.refs_15_.refs_0_, bf16[2048,1024]{1,0:T(8,128)(2,1)} %all-gather.8.cloned.1.call-done.refs_1_, ...), custom_call_target="tpu_custom_call" | custom-call | flops 8589934592 | bytes 8388608 | tf_op jit(solution)/shard_map/projection_weights/pallas_call | solution.py:801
  278.1 1.4 add_convert_fusion.3
  279.8 2.4 collective-permute-start.33
  282.2 1.4 add_convert_fusion.1
  285.4 2.0 collective-permute-done.34
  288.6 2.5 fusion
  (138 shorter events, 36.8 us)
Async XLA Ops:
  8.0 35.1 %copy-start.19 = (bf16[128]{0:T(256)(128)(2,1)S(1)}, bf16[128]{0:T(256)(128)(2,1)}, u32[]{:S(2)}) copy-start(bf16[128]{0:T(256)(128)(2,1)} %param.23) | copy-start | bytes 772
  8.0 119.7 %all-gather.4.cloned.1.call-start = ((), (), s32[]{:S(2)}) async-start(), calls=%async_computation.2 | async-start | bytes 9437184 | tf_op jit(solution)/shard_map/all_gather | solution.py:109
  8.1 26.7 %collective-permute-start.3 = (bf16[256,2048]{1,0:T(8,128)(2,1)}, bf16[256,2048]{1,0:T(8,128)(2,1)S(1)}, u32[]{:S(2)}, u32[]{:S(2)}) collective-permute-start(bf16[256,2048]{1,0:T(8,128)(2,1)} %refs_4_.3), channel_id=1, source_target_pairs={{0,16},{4,20},{8,24},{12,28},{16,0},{20,4},{24,8},{28,12},{1,17},{... | collective-permute-start | bytes 3145736 | tf_op jit(solution)/shard_map/ppermute | solution.py:97
  11.1 24.8 %collective-permute-start.4 = (bf16[256,2048]{1,0:T(8,128)(2,1)}, bf16[256,2048]{1,0:T(8,128)(2,1)S(1)}, u32[]{:S(2)}, u32[]{:S(2)}) collective-permute-start(bf16[256,2048]{1,0:T(8,128)(2,1)} %refs_4_.3), channel_id=1, source_target_pairs={{0,4},{4,0},{8,12},{12,8},{16,20},{20,16},{24,28},{28,24},{1,5},{5... | collective-permute-start | bytes 3145736 | tf_op jit(solution)/shard_map/ppermute | solution.py:97
  12.6 14.3 %collective-permute-start.1 = (bf16[256,512]{1,0:T(8,128)(2,1)}, bf16[256,512]{1,0:T(8,128)(2,1)S(1)}, u32[]{:S(2)}, u32[]{:S(2)}) collective-permute-start(bf16[256,512]{1,0:T(8,128)(2,1)} %refs_0_.3), channel_id=1, source_target_pairs={{0,2},{1,3},{2,0},{3,1},{4,6},{5,7},{6,4},{7,5},{8,10},{9,11},{10,... | collective-permute-start | bytes 786440 | tf_op jit(solution)/shard_map/ppermute | solution.py:24
  15.2 17.0 %collective-permute-start = (bf16[256,512]{1,0:T(8,128)(2,1)}, bf16[256,512]{1,0:T(8,128)(2,1)S(1)}, u32[]{:S(2)}, u32[]{:S(2)}) collective-permute-start(bf16[256,512]{1,0:T(8,128)(2,1)} %refs_0_.3), channel_id=1, source_target_pairs={{0,1},{1,0},{2,3},{3,2},{4,5},{5,4},{6,7},{7,6},{8,9},{9,8},{10,11... | collective-permute-start | bytes 786440 | tf_op jit(solution)/shard_map/ppermute | solution.py:24
  27.6 7.2 %collective-permute-start.2 = (bf16[256,512]{1,0:T(8,128)(2,1)S(1)}, bf16[256,512]{1,0:T(8,128)(2,1)S(1)}, u32[]{:S(2)}, u32[]{:S(2)}) collective-permute-start(bf16[256,512]{1,0:T(8,128)(2,1)S(1)} %collective-permute-done.1.refs_2_), channel_id=1, source_target_pairs={{0,1},{1,0},{2,3},{3,2},{4,5},{5,4},{6,7},{7,6},{8,9},{9,8},{10,11... | collective-permute-start | bytes 786440 | tf_op jit(solution)/shard_map/ppermute | solution.py:24
  41.5 115.4 %reduce-scatter.3.cloned.1.call-start = ((), (), s32[]{:S(2)}) async-start(), calls=%async_computation.3 | async-start | bytes 1310720 | tf_op jit(solution)/shard_map/reduce_scatter | solution.py:113
  41.5 7.2 %collective-permute-start.5 = (bf16[256,512]{1,0:T(8,128)(2,1)}, bf16[256,512]{1,0:T(8,128)(2,1)}, u32[]{:S(2)}, u32[]{:S(2)}) collective-permute-start(bf16[256,512]{1,0:T(8,128)(2,1)} %get-tuple-element.75.refs_2_.refs_8_), channel_id=1, source_target_pairs={{0,4},{4,0},{1,5},{5,1},{2,6},{6,2},{3,7},{7,3},{8,12},{12,8},{9,1... | collective-permute-start | bytes 786440 | tf_op jit(solution)/shard_map/ppermute | solution.py:24
  43.7 48.0 %copy-start.17 = (bf16[2048]{0:T(1024)(128)(2,1)S(1)}, bf16[2048]{0:T(1024)(128)(2,1)}, u32[]{:S(2)}) copy-start(bf16[2048]{0:T(1024)(128)(2,1)} %param.26) | copy-start | bytes 12292
  54.3 9.1 %collective-permute-start.7 = (bf16[256,512]{1,0:T(8,128)(2,1)}, bf16[256,512]{1,0:T(8,128)(2,1)S(1)}, u32[]{:S(2)}, u32[]{:S(2)}) collective-permute-start(bf16[256,512]{1,0:T(8,128)(2,1)} %get-tuple-element.79), channel_id=1, source_target_pairs={{0,1},{1,0},{2,3},{3,2},{4,5},{5,4},{6,7},{7,6},{8,9},{9,8},{10,11... | collective-permute-start | bytes 786440 | tf_op jit(solution)/shard_map/ppermute | solution.py:24
  56.5 35.9 %collective-permute-start.12 = (bf16[256,2048]{1,0:T(8,128)(2,1)}, bf16[256,2048]{1,0:T(8,128)(2,1)S(1)}, u32[]{:S(2)}, u32[]{:S(2)}) collective-permute-start(bf16[256,2048]{1,0:T(8,128)(2,1)} %refs_4_.3), channel_id=1, source_target_pairs={{0,8},{8,0},{16,24},{24,16},{1,9},{9,1},{17,25},{25,17},{2,10},{10... | collective-permute-start | bytes 3145736 | tf_op jit(solution)/shard_map/ppermute | solution.py:24
  56.5 36.8 %collective-permute-start.13 = (bf16[256,2048]{1,0:T(8,128)(2,1)}, bf16[256,2048]{1,0:T(8,128)(2,1)S(1)}, u32[]{:S(2)}, u32[]{:S(2)}) collective-permute-start(bf16[256,2048]{1,0:T(8,128)(2,1)} %copy-done.10), channel_id=1, source_target_pairs={{0,8},{8,0},{16,24},{24,16},{1,9},{9,1},{17,25},{25,17},{2,10},{10... | collective-permute-start | bytes 3145736 | tf_op jit(solution)/shard_map/ppermute | solution.py:24
  57.0 37.4 %collective-permute-start.14 = (bf16[256,2048]{1,0:T(8,128)(2,1)}, bf16[256,2048]{1,0:T(8,128)(2,1)}, u32[]{:S(2)}, u32[]{:S(2)}) collective-permute-start(bf16[256,2048]{1,0:T(8,128)(2,1)} %copy-done.9), channel_id=1, source_target_pairs={{0,8},{8,0},{16,24},{24,16},{1,9},{9,1},{17,25},{25,17},{2,10},{10... | collective-permute-start | bytes 3145736 | tf_op jit(solution)/shard_map/ppermute | solution.py:24
  57.0 13.1 %collective-permute-start.6 = (bf16[256,512]{1,0:T(8,128)(2,1)}, bf16[256,512]{1,0:T(8,128)(2,1)S(1)}, u32[]{:S(2)}, u32[]{:S(2)}) collective-permute-start(bf16[256,512]{1,0:T(8,128)(2,1)} %get-tuple-element.77), channel_id=1, source_target_pairs={{0,1},{1,0},{2,3},{3,2},{4,5},{5,4},{6,7},{7,6},{8,9},{9,8},{10,11... | collective-permute-start | bytes 786440 | tf_op jit(solution)/shard_map/ppermute | solution.py:24
  64.4 14.7 %collective-permute-start.8 = (bf16[256,512]{1,0:T(8,128)(2,1)S(1)}, bf16[256,512]{1,0:T(8,128)(2,1)S(1)}, u32[]{:S(2)}, u32[]{:S(2)}) collective-permute-start(bf16[256,512]{1,0:T(8,128)(2,1)S(1)} %add_convert_fusion.7), channel_id=1, source_target_pairs={{0,2},{1,3},{2,0},{3,1},{4,6},{5,7},{6,4},{7,5},{8,10},{9,11},{10,... | collective-permute-start | bytes 786440 | tf_op jit(solution)/shard_map/ppermute | solution.py:24
  80.3 9.4 %collective-permute-start.10 = (bf16[256,512]{1,0:T(8,128)(2,1)S(1)}, bf16[256,512]{1,0:T(8,128)(2,1)S(1)}, u32[]{:S(2)}, u32[]{:S(2)}) collective-permute-start(bf16[256,512]{1,0:T(8,128)(2,1)S(1)} %fusion.1.refs_0_), channel_id=1, source_target_pairs={{0,2},{1,3},{2,0},{3,1},{4,6},{5,7},{6,4},{7,5},{8,10},{9,11},{10,... | collective-permute-start | bytes 786440 | tf_op jit(solution)/shard_map/ppermute | solution.py:24
  81.0 12.3 %collective-permute-start.9 = (bf16[256,512]{1,0:T(8,128)(2,1)S(1)}, bf16[256,512]{1,0:T(8,128)(2,1)S(1)}, u32[]{:S(2)}, u32[]{:S(2)}) collective-permute-start(bf16[256,512]{1,0:T(8,128)(2,1)S(1)} %fusion.1.refs_0_), channel_id=1, source_target_pairs={{0,1},{1,0},{2,3},{3,2},{4,5},{5,4},{6,7},{7,6},{8,9},{9,8},{10,11... | collective-permute-start | bytes 786440 | tf_op jit(solution)/shard_map/ppermute | solution.py:24
  89.6 6.5 %collective-permute-start.11 = (bf16[256,512]{1,0:T(8,128)(2,1)S(1)}, bf16[256,512]{1,0:T(8,128)(2,1)S(1)}, u32[]{:S(2)}, u32[]{:S(2)}) collective-permute-start(bf16[256,512]{1,0:T(8,128)(2,1)S(1)} %collective-permute-done.10.refs_2_), channel_id=1, source_target_pairs={{0,1},{1,0},{2,3},{3,2},{4,5},{5,4},{6,7},{7,6},{8,9},{9,8},{10,11... | collective-permute-start | bytes 786440 | tf_op jit(solution)/shard_map/ppermute | solution.py:24
  100.5 22.8 %collective-permute-start.18 = (bf16[256,2048]{1,0:T(8,128)(2,1)}, bf16[256,2048]{1,0:T(8,128)(2,1)}, u32[]{:S(2)}, u32[]{:S(2)}) collective-permute-start(bf16[256,2048]{1,0:T(8,128)(2,1)} %get-tuple-element.80.normed_hbm.refs_0_), channel_id=1, source_target_pairs={{0,16},{4,20},{8,24},{12,28},{16,0},{20,4},{24,8},{28,12},{1,17},{... | collective-permute-start | bytes 3145736 | tf_op jit(solution)/shard_map/ppermute | solution.py:97
  101.1 22.2 %collective-permute-start.15 = (bf16[256,2048]{1,0:T(8,128)(2,1)}, bf16[256,2048]{1,0:T(8,128)(2,1)}, u32[]{:S(2)}, u32[]{:S(2)}) collective-permute-start(bf16[256,2048]{1,0:T(8,128)(2,1)} %get-tuple-element.80.normed_hbm.refs_0_), channel_id=1, source_target_pairs={{0,4},{4,0},{8,12},{12,8},{16,20},{20,16},{24,28},{28,24},{1,5},{5... | collective-permute-start | bytes 3145736 | tf_op jit(solution)/shard_map/ppermute | solution.py:97
  105.9 19.7 %collective-permute-start.19 = (bf16[256,2048]{1,0:T(8,128)(2,1)}, bf16[256,2048]{1,0:T(8,128)(2,1)}, u32[]{:S(2)}, u32[]{:S(2)}) collective-permute-start(bf16[256,2048]{1,0:T(8,128)(2,1)} %get-tuple-element.80.normed_hbm.refs_0_), channel_id=1, source_target_pairs={{0,8},{8,0},{16,24},{24,16},{1,9},{9,1},{17,25},{25,17},{2,10},{10... | collective-permute-start | bytes 3145736 | tf_op jit(solution)/shard_map/ppermute | solution.py:24
  123.2 3.0 %collective-permute-start.20 = (bf16[256,2048]{1,0:T(8,128)(2,1)}, bf16[256,2048]{1,0:T(8,128)(2,1)}, u32[]{:S(2)}, u32[]{:S(2)}) collective-permute-start(bf16[256,2048]{1,0:T(8,128)(2,1)} %collective-permute-done.18.refs_1_), channel_id=1, source_target_pairs={{0,8},{8,0},{16,24},{24,16},{1,9},{9,1},{17,25},{25,17},{2,10},{10... | collective-permute-start | bytes 3145736 | tf_op jit(solution)/shard_map/ppermute | solution.py:24
  123.4 4.4 %collective-permute-start.17 = (bf16[256,2048]{1,0:T(8,128)(2,1)}, bf16[256,2048]{1,0:T(8,128)(2,1)}, u32[]{:S(2)}, u32[]{:S(2)}) collective-permute-start(bf16[256,2048]{1,0:T(8,128)(2,1)} %collective-permute-done.15.refs_0_), channel_id=1, source_target_pairs={{0,8},{8,0},{16,24},{24,16},{1,9},{9,1},{17,25},{25,17},{2,10},{10... | collective-permute-start | bytes 3145736 | tf_op jit(solution)/shard_map/ppermute | solution.py:24
  123.8 32.5 %collective-permute-start.22 = (bf16[256,2048]{1,0:T(8,128)(2,1)}, bf16[256,2048]{1,0:T(8,128)(2,1)}, u32[]{:S(2)}, u32[]{:S(2)}) collective-permute-start(bf16[256,2048]{1,0:T(8,128)(2,1)} %copy-done.10), channel_id=1, source_target_pairs={{0,4},{4,0},{8,12},{12,8},{16,20},{20,16},{24,28},{28,24},{1,5},{5... | collective-permute-start | bytes 3145736 | tf_op jit(solution)/shard_map/ppermute | solution.py:97
  123.8 68.8 %all-gather.6.cloned.1.call-start = ((), (), s32[]{:S(2)}) async-start(), calls=%async_computation.5 | async-start | bytes 1310720 | tf_op jit(solution)/shard_map/all_gather | solution.py:958
  124.0 32.5 %collective-permute-start.16 = (bf16[256,2048]{1,0:T(8,128)(2,1)}, bf16[256,2048]{1,0:T(8,128)(2,1)}, u32[]{:S(2)}, u32[]{:S(2)}) collective-permute-start(bf16[256,2048]{1,0:T(8,128)(2,1)} %collective-permute-done.15.refs_0_), channel_id=1, source_target_pairs={{0,16},{4,20},{8,24},{12,28},{16,0},{20,4},{24,8},{28,12},{1,17},{... | collective-permute-start | bytes 3145736 | tf_op jit(solution)/shard_map/ppermute | solution.py:97
  156.3 3.1 %collective-permute-start.23 = (bf16[256,2048]{1,0:T(8,128)(2,1)}, bf16[256,2048]{1,0:T(8,128)(2,1)}, u32[]{:S(2)}, u32[]{:S(2)}) collective-permute-start(bf16[256,2048]{1,0:T(8,128)(2,1)} %collective-permute-done.22.refs_5_), channel_id=1, source_target_pairs={{0,8},{8,0},{16,24},{24,16},{1,9},{9,1},{17,25},{25,17},{2,10},{10... | collective-permute-start | bytes 3145736 | tf_op jit(solution)/shard_map/ppermute | solution.py:24
  156.5 4.4 %collective-permute-start.21 = (bf16[256,2048]{1,0:T(8,128)(2,1)}, bf16[256,2048]{1,0:T(8,128)(2,1)}, u32[]{:S(2)}, u32[]{:S(2)}) collective-permute-start(bf16[256,2048]{1,0:T(8,128)(2,1)} %collective-permute-done.16.refs_1_), channel_id=1, source_target_pairs={{0,8},{8,0},{16,24},{24,16},{1,9},{9,1},{17,25},{25,17},{2,10},{10... | collective-permute-start | bytes 3145736 | tf_op jit(solution)/shard_map/ppermute | solution.py:24
  156.9 91.6 %reduce-scatter.5.cloned.1.call-start = ((), (), s32[]{:S(2)}) async-start(), calls=%async_computation.4 | async-start | bytes 1310720 | tf_op jit(solution)/shard_map/reduce_scatter | solution.py:113
  192.3 68.7 %all-gather.8.cloned.1.call-start = ((), (), s32[]{:S(2)}) async-start(), calls=%async_computation.6 | async-start | bytes 4718592 | tf_op jit(solution)/shard_map/all_gather | solution.py:109
  203.4 2.9 collective-permute-start.28
  203.6 8.7 %collective-permute-start.27 = (bf16[256,512]{1,0:T(8,128)(2,1)S(1)}, bf16[256,512]{1,0:T(8,128)(2,1)}, u32[]{:S(2)}, u32[]{:S(2)}) collective-permute-start(bf16[256,512]{1,0:T(8,128)(2,1)S(1)} %copy-done.18), channel_id=1, source_target_pairs={{0,4},{4,0},{1,5},{5,1},{2,6},{6,2},{3,7},{7,3},{8,12},{12,8},{9,1... | collective-permute-start | bytes 786440 | tf_op jit(solution)/shard_map/ppermute | solution.py:1005
  215.6 9.7 %collective-permute-start.24 = (bf16[2048,768]{1,0:T(8,128)(2,1)}, bf16[2048,768]{1,0:T(8,128)(2,1)}, u32[]{:S(2)}, u32[]{:S(2)}) collective-permute-start(bf16[2048,768]{1,0:T(8,128)(2,1)} %get-tuple-element.91.refs_16_), channel_id=1, source_target_pairs={{0,8},{8,0},{16,24},{24,16},{1,9},{9,1},{17,25},{25,17},{2,10},{10... | collective-permute-start | bytes 9437192 | tf_op jit(solution)/shard_map/ppermute | solution.py:24
  215.7 10.5 %collective-permute-start.25 = (bf16[2048,768]{1,0:T(8,128)(2,1)}, bf16[2048,768]{1,0:T(8,128)(2,1)}, u32[]{:S(2)}, u32[]{:S(2)}) collective-permute-start(bf16[2048,768]{1,0:T(8,128)(2,1)} %get-tuple-element.93), channel_id=1, source_target_pairs={{0,8},{8,0},{16,24},{24,16},{1,9},{9,1},{17,25},{25,17},{2,10},{10... | collective-permute-start | bytes 9437192 | tf_op jit(solution)/shard_map/ppermute | solution.py:24
  216.2 14.5 %collective-permute-start.26 = (bf16[768,2048]{1,0:T(8,128)(2,1)}, bf16[768,2048]{1,0:T(8,128)(2,1)}, u32[]{:S(2)}, u32[]{:S(2)}) collective-permute-start(bf16[768,2048]{1,0:T(8,128)(2,1)} %get-tuple-element.94), channel_id=1, source_target_pairs={{0,8},{8,0},{16,24},{24,16},{1,9},{9,1},{17,25},{25,17},{2,10},{10... | collective-permute-start | bytes 9437192 | tf_op jit(solution)/shard_map/ppermute | solution.py:24
  216.3 26.3 %collective-permute-start.37 = (bf16[128,2048]{1,0:T(8,128)(2,1)}, bf16[128,2048]{1,0:T(8,128)(2,1)}, u32[]{:S(2)}, u32[]{:S(2)}) collective-permute-start(bf16[128,2048]{1,0:T(8,128)(2,1)} %get-tuple-element.137.refs_8_), channel_id=1, source_target_pairs={{0,4},{4,0},{8,12},{12,8},{16,20},{20,16},{24,28},{28,24},{1,5},{5... | collective-permute-start | bytes 1572872 | tf_op jit(solution)/shard_map/ppermute | solution.py:97
  216.5 26.0 %collective-permute-start.35 = (bf16[128,2048]{1,0:T(8,128)(2,1)}, bf16[128,2048]{1,0:T(8,128)(2,1)}, u32[]{:S(2)}, u32[]{:S(2)}) collective-permute-start(bf16[128,2048]{1,0:T(8,128)(2,1)} %get-tuple-element.138.refs_7_), channel_id=1, source_target_pairs={{0,16},{4,20},{8,24},{12,28},{16,0},{20,4},{24,8},{28,12},{1,17},{... | collective-permute-start | bytes 1572872 | tf_op jit(solution)/shard_map/ppermute | solution.py:97
  225.3 20.4 %collective-permute-start.29 = (bf16[272,512]{1,0:T(8,128)(2,1)}, bf16[272,512]{1,0:T(8,128)(2,1)}, u32[]{:S(2)}, u32[]{:S(2)}) collective-permute-start(bf16[272,512]{1,0:T(8,128)(2,1)} %get-tuple-element.115), channel_id=1, source_target_pairs={{0,1},{1,0},{2,3},{3,2},{4,5},{5,4},{6,7},{7,6},{8,9},{9,8},{10,11... | collective-permute-start | bytes 835592 | tf_op jit(solution)/shard_map/ppermute | solution.py:24
  226.2 19.6 %collective-permute-start.30 = (bf16[272,512]{1,0:T(8,128)(2,1)}, bf16[272,512]{1,0:T(8,128)(2,1)}, u32[]{:S(2)}, u32[]{:S(2)}) collective-permute-start(bf16[272,512]{1,0:T(8,128)(2,1)} %get-tuple-element.118), channel_id=1, source_target_pairs={{0,1},{1,0},{2,3},{3,2},{4,5},{5,4},{6,7},{7,6},{8,9},{9,8},{10,11... | collective-permute-start | bytes 835592 | tf_op jit(solution)/shard_map/ppermute | solution.py:24
  245.4 32.3 %collective-permute-start.36 = (bf16[128,2048]{1,0:T(8,128)(2,1)}, bf16[128,2048]{1,0:T(8,128)(2,1)}, u32[]{:S(2)}, u32[]{:S(2)}) collective-permute-start(bf16[128,2048]{1,0:T(8,128)(2,1)} %get-tuple-element.126), channel_id=1, source_target_pairs={{0,4},{4,0},{8,12},{12,8},{16,20},{20,16},{24,28},{28,24},{1,5},{5... | collective-permute-start | bytes 1572872 | tf_op jit(solution)/shard_map/ppermute | solution.py:97
  245.8 34.0 %collective-permute-start.38 = (bf16[128,2048]{1,0:T(8,128)(2,1)}, bf16[128,2048]{1,0:T(8,128)(2,1)}, u32[]{:S(2)}, u32[]{:S(2)}) collective-permute-start(bf16[128,2048]{1,0:T(8,128)(2,1)} %get-tuple-element.129), channel_id=1, source_target_pairs={{0,16},{4,20},{8,24},{12,28},{16,0},{20,4},{24,8},{28,12},{1,17},{... | collective-permute-start | bytes 1572872 | tf_op jit(solution)/shard_map/ppermute | solution.py:97
  248.5 27.9 %collective-permute-start.31 = (bf16[272,512]{1,0:T(8,128)(2,1)}, bf16[272,512]{1,0:T(8,128)(2,1)}, u32[]{:S(2)}, u32[]{:S(2)}) collective-permute-start(bf16[272,512]{1,0:T(8,128)(2,1)} %add_convert_fusion.5.refs_4_), channel_id=1, source_target_pairs={{0,2},{1,3},{2,0},{3,1},{4,6},{5,7},{6,4},{7,5},{8,10},{9,11},{10,... | collective-permute-start | bytes 835592 | tf_op jit(solution)/shard_map/ppermute | solution.py:24
  277.7 2.0 collective-permute-start.32
  279.4 9.1 %collective-permute-start.39 = (bf16[128,2048]{1,0:T(8,128)(2,1)S(1)}, bf16[128,2048]{1,0:T(8,128)(2,1)S(1)}, u32[]{:S(2)}, u32[]{:S(2)}) collective-permute-start(bf16[128,2048]{1,0:T(8,128)(2,1)S(1)} %add_convert_fusion.3), channel_id=1, source_target_pairs={{0,8},{8,0},{16,24},{24,16},{1,9},{9,1},{17,25},{25,17},{2,10},{10... | collective-permute-start | bytes 1572872 | tf_op jit(solution)/shard_map/ppermute | solution.py:24
  279.8 4.0 %collective-permute-start.33 = (f32[1280]{0:T(1024)S(1)}, f32[1280]{0:T(1024)S(1)}, u32[]{:S(2)}, u32[]{:S(2)}) collective-permute-start(f32[1280]{0:T(1024)S(1)} %fusion.8), channel_id=1, source_target_pairs={{0,16},{4,20},{8,24},{12,28},{16,0},{20,4},{24,8},{28,12},{1,17},{... | collective-permute-start | bytes 15368 | tf_op jit(solution)/shard_map/ppermute | solution.py:97
  283.5 5.0 %collective-permute-start.40 = (bf16[128,2048]{1,0:T(8,128)(2,1)S(1)}, bf16[128,2048]{1,0:T(8,128)(2,1)S(1)}, u32[]{:S(2)}, u32[]{:S(2)}) collective-permute-start(bf16[128,2048]{1,0:T(8,128)(2,1)S(1)} %add_convert_fusion.1), channel_id=1, source_target_pairs={{0,8},{8,0},{16,24},{24,16},{1,9},{9,1},{17,25},{25,17},{2,10},{10... | collective-permute-start | bytes 1572872 | tf_op jit(solution)/shard_map/ppermute | solution.py:24
  283.8 3.7 %collective-permute-start.34 = (f32[1280]{0:T(1024)S(1)}, f32[1280]{0:T(1024)S(1)}, u32[]{:S(2)}, u32[]{:S(2)}) collective-permute-start(f32[1280]{0:T(1024)S(1)} %add.93), channel_id=1, source_target_pairs={{0,4},{4,0},{8,12},{12,8},{16,20},{20,16},{24,28},{28,24},{1,5},{5... | collective-permute-start | bytes 15368 | tf_op jit(solution)/shard_map/ppermute | solution.py:97
  (18 other events, 75.7 us)
Sparse Core Ops, SparseCore 0:
  41.6 54.7 all-gather.3
  215.7 45.2 all-gather.7
Sparse Core Ops, SparseCore 1:
  123.9 27.0 reduce-scatter.2
  157.0 25.6 all-gather.5
  192.3 25.0 reduce-scatter.4

commit v4 on v3

--- a/solution.py
+++ b/solution.py
@@ -16,7 +16,7 @@
 MIB = 1024 * 1024
 VMEM_LIMIT = 63 * MIB + 900 * 1024
 EXTRA = 16
-SCALE = 1
+SCALE = 2
 
 
 def swap(value, axis, bit):

time: 301 us -> 299 us (level)
  starting transfers between devices: 39.9 us -> 43.4 us
where the time goes in v4:
time: 299 us; the launch traced here: 298 us
  Pallas kernels  140 us (47%)
  waiting for transfers between devices  60.7 us (20%)
  starting transfers between devices  43.4 us (15%)
  other arithmetic  27.1 us (9%)
  between operations  16.1 us (5%)
  local copies, waits for them, and re-layouts  8.83 us (3%)
    pallas_call x2, Pallas kernels, feed_weights(): pl.pallas_call(functools.partial(feed_weight_body, parts, extra, last, bl...  59.8 us
    ppermute x28, waiting for transfers between devices, swap(): return lax.ppermute(value, axis, [(i, i ^ bit) for i in range(size)])  45.9 us
    pallas_call x7, Pallas kernels, kernel_call(): pl.pallas_call(run, out_shape=tuple(outs), in_specs=[SMEM] + [ANY] * (cou...  36.5 us
    ppermute x28, starting transfers between devices, swap(): return lax.ppermute(value, axis, [(i, i ^ bit) for i in range(size)])  25 us
    ppermute x12, starting transfers between devices, send_plane(): lax.ppermute(value, ('dp', 'ctx'), [(i, i ^ mask) for i in range(size)])  17.7 us
    pallas_call x1, Pallas kernels, feed_forward(): pl.pallas_call(functools.partial(feed_forward_body, tile, len(after)), ou...  16.3 us
    pallas_call x1, Pallas kernels, projection_weights(): pl.pallas_call(functools.partial(projection_body, parts, tile, len(after)...  15.4 us
    pallas_call x1, Pallas kernels, assemble(): pl.pallas_call(functools.partial(assemble_body, len(after)), out_shape=[s...  11.8 us
  transfers between devices with their start and end apart: 46, of which 23 were waited for; matrix products, arithmetic and copies ran while one was open for 11% of the time, Pallas kernels for 45%

profile of v4, /device:TPU:0, one launch (start us, length us, event | category | flops | bytes accessed | tf_op | source)
XLA Modules:
  0.0 298.0 jit_solution(12531780307694226687)
XLA Ops:
  8.1 3.0 %collective-permute-start.3 = (bf16[256,2048]{1,0:T(8,128)(2,1)}, bf16[256,2048]{1,0:T(8,128)(2,1)}, u32[]{:S(2)}, u32[]{:S(2)}) collective-permute-start(bf16[256,2048]{1,0:T(8,128)(2,1)} %refs_4_.3), channel_id=1, source_target_pairs={{0,16},{4,20},{8,24},{12,28},{16,0},{20,4},{24,8},{28,12},{1,17},{... | collective-permute-start | bytes 3145736 | tf_op jit(solution)/shard_map/ppermute | solution.py:97
  11.1 1.5 collective-permute-start.4
  12.6 2.6 collective-permute-start.1
  15.2 1.6 collective-permute-start
  20.1 6.8 %collective-permute-done.1.refs_2_ = bf16[256,512]{1,0:T(8,128)(2,1)S(1)} collective-permute-done((bf16[256,512]{1,0:T(8,128)(2,1)}, bf16[256,512]{1,0:T(8,128)(2,1)S(1)}, u32[]{:S(2)}, u32[]{:S(2)}) %collective-permute-start.1) | collective-permute-done | bytes 262176 | tf_op jit(solution)/shard_map/ppermute | solution.py:24
  32.1 2.7 collective-permute-done.2.refs_3_
  36.0 4.6 %key_value.1 = (bf16[256,2048]{1,0:T(8,128)(2,1)}, bf16[256,512]{1,0:T(8,128)(2,1)}, f32[256,256]{1,0:T(8,128)}, f32[256,1]{1,0:T(8,128)}) custom-call(s32[4]{0:T(128)} %pad_add_fusion.ids, bf16[256,512]{1,0:T(8,128)(2,1)} %refs_0_.3, bf16[256,512]{1,0:T(8,128)(2,1)} %copy-done.5, bf16[256,512]{1,0:T(8,128)(2,1)} %copy-done.4, bf16[256,512]{1,0:T(8,128)(2,1)} %copy-done.6, ...), custom_call_target="tpu_custom_call" | custom-call | flops 268435456 | bytes 2495232 | tf_op jit(solution)/shard_map/key_value/pallas_call | solution.py:200
  40.7 1.6 collective-permute-start.5
  42.8 4.4 %query.1 = (bf16[256,512]{1,0:T(8,128)(2,1)}, f32[256,512]{1,0:T(8,128)}) custom-call(s32[4]{0:T(128)} %pad_add_fusion.ids, bf16[256,2048]{1,0:T(8,128)(2,1)} %get-tuple-element.73.refs_0_, bf16[2048,512]{1,0:T(8,128)(2,1)} %refs_9_.7, f32[1,128]{1,0:T(1,128)} %bitcast_convert_fusion.1.refs_2_.refs_13_, ...), custom_call_target="tpu_custom_call" | custom-call | flops 268435456 | bytes 2097408 | tf_op jit(solution)/shard_map/query/pallas_call | solution.py:200
  47.9 5.5 %attention.1 = (bf16[256,512]{1,0:T(8,128)(2,1)}, bf16[256,512]{1,0:T(8,128)(2,1)}, bf16[256,512]{1,0:T(8,128)(2,1)}, bf16[256,512]{1,0:T(8,128)(2,1)}, bf16[256,512]{1,0:T(8,128)(2,1)}) custom-call(s32[4]{0:T(128)} %pad_add_fusion.ids, bf16[256,512]{1,0:T(8,128)(2,1)} %get-tuple-element.74.refs_0_.refs_6_, s32[256,1]{1,0:T(8,128)} %copy.34.refs_12_.refs_1_.refs_7_, ...), custom_call_target="tpu_custom_call" | custom-call | flops 402653184 | bytes 2098688 | tf_op jit(solution)/shard_map/attention/pallas_call | solution.py:200
  53.4 1.9 collective-permute-start.7
  56.0 6.0 %collective-permute-done.7 = bf16[256,512]{1,0:T(8,128)(2,1)S(1)} collective-permute-done((bf16[256,512]{1,0:T(8,128)(2,1)}, bf16[256,512]{1,0:T(8,128)(2,1)S(1)}, u32[]{:S(2)}, u32[]{:S(2)}) %collective-permute-start.7) | collective-permute-done | bytes 262176 | tf_op jit(solution)/shard_map/ppermute | solution.py:24
  63.0 4.2 %collective-permute-start.8 = (bf16[256,512]{1,0:T(8,128)(2,1)S(1)}, bf16[256,512]{1,0:T(8,128)(2,1)S(1)}, u32[]{:S(2)}, u32[]{:S(2)}) collective-permute-start(bf16[256,512]{1,0:T(8,128)(2,1)S(1)} %add_convert_fusion.7), channel_id=1, source_target_pairs={{0,2},{1,3},{2,0},{3,1},{4,6},{5,7},{6,4},{7,5},{8,10},{9,11},{10,... | collective-permute-start | bytes 786440 | tf_op jit(solution)/shard_map/ppermute | solution.py:24
  68.5 9.6 %collective-permute-done.8 = bf16[256,512]{1,0:T(8,128)(2,1)S(1)} collective-permute-done((bf16[256,512]{1,0:T(8,128)(2,1)S(1)}, bf16[256,512]{1,0:T(8,128)(2,1)S(1)}, u32[]{:S(2)}, u32[]{:S(2)}) %collective-permute-start.8) | collective-permute-done | bytes 262176 | tf_op jit(solution)/shard_map/ppermute | solution.py:24
  80.0 4.1 %collective-permute-start.9 = (bf16[256,512]{1,0:T(8,128)(2,1)S(1)}, bf16[256,512]{1,0:T(8,128)(2,1)S(1)}, u32[]{:S(2)}, u32[]{:S(2)}) collective-permute-start(bf16[256,512]{1,0:T(8,128)(2,1)S(1)} %fusion.1.refs_0_), channel_id=1, source_target_pairs={{0,1},{1,0},{2,3},{3,2},{4,5},{5,4},{6,7},{7,6},{8,9},{9,8},{10,11... | collective-permute-start | bytes 786440 | tf_op jit(solution)/shard_map/ppermute | solution.py:24
  84.1 4.1 %collective-permute-done.10.refs_2_ = bf16[256,512]{1,0:T(8,128)(2,1)S(1)} collective-permute-done((bf16[256,512]{1,0:T(8,128)(2,1)S(1)}, bf16[256,512]{1,0:T(8,128)(2,1)S(1)}, u32[]{:S(2)}, u32[]{:S(2)}) %collective-permute-start.10) | collective-permute-done | bytes 262176 | tf_op jit(solution)/shard_map/ppermute | solution.py:24
  88.2 2.6 collective-permute-start.11
  92.2 2.9 collective-permute-done.11.refs_3_
  95.9 3.7 %second_norm.1 = (bf16[256,2048]{1,0:T(8,128)(2,1)}, bf16[256,2048]{1,0:T(8,128)(2,1)}, f32[256,1]{1,0:T(8,128)}) custom-call(s32[4]{0:T(128)} %pad_add_fusion.ids, bf16[256,512]{1,0:T(8,128)(2,1)} %copy-done.3, bf16[256,512]{1,0:T(8,128)(2,1)} %copy-done.9, bf16[256,512]{1,0:T(8,128)(2,1)} %copy-done.8, bf16[256,512]{1,0:T(8,128)(2,1)} %copy-done.10, ...), custom_call_target="tpu_custom_call" | custom-call | flops 2097152 | bytes 1577472 | tf_op jit(solution)/shard_map/second_norm/pallas_call | solution.py:200
  100.1 5.1 %collective-permute-start.15 = (bf16[256,2048]{1,0:T(8,128)(2,1)}, bf16[256,2048]{1,0:T(8,128)(2,1)}, u32[]{:S(2)}, u32[]{:S(2)}) collective-permute-start(bf16[256,2048]{1,0:T(8,128)(2,1)} %get-tuple-element.80.normed_hbm.refs_0_), channel_id=1, source_target_pairs={{0,4},{4,0},{8,12},{12,8},{16,20},{20,16},{24,28},{28,24},{1,5},{5... | collective-permute-start | bytes 3145736 | tf_op jit(solution)/shard_map/ppermute | solution.py:97
  105.2 16.3 %feed_forward.1 = (bf16[256,2048]{1,0:T(8,128)(2,1)}, bf16[256,2048]{1,0:T(8,128)(2,1)}) custom-call(s32[4]{0:T(128)} %pad_add_fusion.ids, bf16[256,2048]{1,0:T(8,128)(2,1)} %get-tuple-element.80.normed_hbm.refs_0_, bf16[256,2048]{1,0:T(8,128)(2,1)} %refs_4_.3, bf16[2048,1536]{1,0:T(8,128)(2,1)} %refs_8_.5, bf16[2048,1536]{1,0:T(8,128)(2,1)} %refs_9_.6, ...), custom_call_target="tpu_custom_call" | custom-call | flops 4831838208 | bytes 11534336 | tf_op jit(solution)/shard_map/feed_forward/pallas_call | solution.py:391
  122.9 1.5 collective-permute-start.16
  125.0 1.5 collective-permute-done.17.refs_14_.refs_2_
  126.5 28.3 %feed_weights.2 = (f32[2048,1536]{1,0:T(8,128)}, f32[2048,1536]{1,0:T(8,128)}, f32[1536,2048]{1,0:T(8,128)}) custom-call(s32[4]{0:T(128)} %pad_add_fusion.ids, bf16[256,2048]{1,0:T(8,128)(2,1)} %get-tuple-element.80.normed_hbm.refs_0_, bf16[256,2048]{1,0:T(8,128)(2,1)} %collective-permute-done.18.refs_1_, ...), custom_call_target="tpu_custom_call" | custom-call | flops 9663676416 | bytes 4194304 | tf_op jit(solution)/shard_map/feed_weights/pallas_call | solution.py:691
  155.5 2.4 collective-permute-done.23.refs_7_
  157.9 1.5 collective-permute-done.21.refs_3_
  159.4 31.4 %feed_weights.3 = (f32[2048,1536]{1,0:T(8,128)}, f32[2048,1536]{1,0:T(8,128)}, f32[1536,2048]{1,0:T(8,128)}, bf16[2048,768]{1,0:T(8,128)(2,1)}, bf16[2048,768]{1,0:T(8,128)(2,1)}, /*index=5*/bf16[768,2048]{1,0:T(8,128)(2,1)}) custom-call(s32[4]{0:T(128)} %pad_add_fusion.ids, ...), custom_call_target="tpu_custom_call", output_to_operand_aliasing={{0}: (12, {}), {1}: (13, {}), {2}: (14, {})} | custom-call | flops 9663676416 | bytes 4194304 | tf_op jit(solution)/shard_map/feed_weights/pallas_call | solution.py:691
  191.2 8.6 %middle.1 = (f32[256,512]{1,0:T(8,128)}, bf16[256,2048]{1,0:T(8,128)(2,1)}, f32[1,2048]{1,0:T(1,128)}, bf16[256,512]{1,0:T(8,128)(2,1)}, f32[1,128]{1,0:T(1,128)...) custom-call(s32[4]{0:T(128)} %pad_add_fusion.ids, bf16[256,2048]{1,0:T(8,128)(2,1)} %all-gather.6.cloned.1.call-done.refs_0_, ...), custom_call_target="tpu_custom_call" | custom-call | flops 268435456 | bytes 4729344 | tf_op jit(solution)/shard_map/middle/pallas_call | solution.py:200
  199.8 2.1 convolution_convert_fusion
  202.5 2.4 collective-permute-done.28
  204.9 1.6 add_convert_fusion
  208.5 2.4 collective-permute-done.27.refs_1_
  210.9 3.3 %key_backward.1 = (bf16[256,1024]{1,0:T(8,128)(2,1)}, f32[1,128]{1,0:T(1,128)}) custom-call(s32[4]{0:T(128)} %pad_add_fusion.ids, f32[256,512]{1,0:T(8,128)} %get-tuple-element.103.refs_0_, bf16[256,512]{1,0:T(8,128)(2,1)} %collective-permute-done.27.refs_1_, f32[256,256]{1,0:T(8,128)} %get-tuple-element.105.refs_2_, ...), custom_call_target="tpu_custom_call" | custom-call | flops 1310720 | bytes 1049088 | tf_op jit(solution)/shard_map/key_backward/pallas_call | solution.py:200
  218.2 6.4 %first_grad.1 = (bf16[272,512]{1,0:T(8,128)(2,1)}, bf16[272,512]{1,0:T(8,128)(2,1)}, bf16[272,512]{1,0:T(8,128)(2,1)}, bf16[272,512]{1,0:T(8,128)(2,1)}) custom-call(s32[4]{0:T(128)} %pad_add_fusion.ids, bf16[256,512]{1,0:T(8,128)(2,1)} %refs_0_.3, bf16[256,512]{1,0:T(8,128)(2,1)} %copy-done.5, bf16[256,512]{1,0:T(8,128)(2,1)} %copy-done.4, ...), custom_call_target="tpu_custom_call" | custom-call | flops 536870912 | bytes 3445760 | tf_op jit(solution)/shard_map/first_grad/pallas_call | solution.py:200
  224.8 1.9 collective-permute-start.30
  226.7 2.6 collective-permute-done.26.down_low
  229.3 11.8 %assemble.1 = (f32[2048,1536]{1,0:T(8,128)}, f32[2048,1536]{1,0:T(8,128)}, f32[1536,2048]{1,0:T(8,128)}) custom-call(s32[4]{0:T(128)} %pad_add_fusion.ids, bf16[2048,768]{1,0:T(8,128)(2,1)} %collective-permute-done.24.gate_low, bf16[2048,768]{1,0:T(8,128)(2,1)} %collective-permute-done.25.up_low, ...), custom_call_target="tpu_custom_call", output_to_operand_aliasing={{0}: (4, {}), {1}: (5, {}), {2}: (6, {})} | custom-call | bytes 14155776 | tf_op jit(solution)/shard_map/assemble/pallas_call | solution.py:726
  241.2 2.9 add_convert_fusion.4
  244.4 1.4 collective-permute-start.38
  245.9 1.8 add_convert_fusion.5.refs_4_
  248.0 1.8 add_convert_fusion.6
  249.8 1.8 convert_add_fusion.2.refs_3_
  251.6 9.0 %all-gather.8.cloned.1.call-done.refs_1_ = bf16[2048,1024]{1,0:T(8,128)(2,1)} async-done(((bf16[256,1024]{1,0:T(8,128)(2,1)}), bf16[2048,1024]{1,0:T(8,128)(2,1)}) %all-gather.8.cloned.1.call-update) | async-done | bytes 4194320 | tf_op jit(solution)/shard_map/all_gather | solution.py:109
  260.6 15.4 %projection_weights.1 = (f32[2048,512]{1,0:T(8,128)}, f32[2048,256]{1,0:T(8,128)}, f32[2048,256]{1,0:T(8,128)}) custom-call(s32[4]{0:T(128)} %pad_add_fusion.ids, bf16[2048,2048]{1,0:T(8,128)(2,1)} %all-gather.4.cloned.1.call-done.refs_15_.refs_0_, bf16[2048,1024]{1,0:T(8,128)(2,1)} %all-gather.8.cloned.1.call-done.refs_1_, ...), custom_call_target="tpu_custom_call" | custom-call | flops 4294967296 | bytes 4194304 | tf_op jit(solution)/shard_map/projection_weights/pallas_call | solution.py:801
  277.7 1.4 add_convert_fusion.3
  279.4 1.7 collective-permute-start.33
  285.1 1.7 collective-permute-done.34
  287.9 2.5 fusion
  (130 shorter events, 35.8 us)
Async XLA Ops:
  8.0 34.2 %copy-start.15 = (bf16[128]{0:T(256)(128)(2,1)S(1)}, bf16[128]{0:T(256)(128)(2,1)}, u32[]{:S(2)}) copy-start(bf16[128]{0:T(256)(128)(2,1)} %param.23) | copy-start | bytes 772
  8.0 118.5 %all-gather.4.cloned.1.call-start = ((), (), s32[]{:S(2)}) async-start(), calls=%async_computation.2 | async-start | bytes 9437184 | tf_op jit(solution)/shard_map/all_gather | solution.py:109
  8.1 26.7 %collective-permute-start.3 = (bf16[256,2048]{1,0:T(8,128)(2,1)}, bf16[256,2048]{1,0:T(8,128)(2,1)}, u32[]{:S(2)}, u32[]{:S(2)}) collective-permute-start(bf16[256,2048]{1,0:T(8,128)(2,1)} %refs_4_.3), channel_id=1, source_target_pairs={{0,16},{4,20},{8,24},{12,28},{16,0},{20,4},{24,8},{28,12},{1,17},{... | collective-permute-start | bytes 3145736 | tf_op jit(solution)/shard_map/ppermute | solution.py:97
  11.1 24.9 %collective-permute-start.4 = (bf16[256,2048]{1,0:T(8,128)(2,1)}, bf16[256,2048]{1,0:T(8,128)(2,1)}, u32[]{:S(2)}, u32[]{:S(2)}) collective-permute-start(bf16[256,2048]{1,0:T(8,128)(2,1)} %refs_4_.3), channel_id=1, source_target_pairs={{0,4},{4,0},{8,12},{12,8},{16,20},{20,16},{24,28},{28,24},{1,5},{5... | collective-permute-start | bytes 3145736 | tf_op jit(solution)/shard_map/ppermute | solution.py:97
  12.6 14.3 %collective-permute-start.1 = (bf16[256,512]{1,0:T(8,128)(2,1)}, bf16[256,512]{1,0:T(8,128)(2,1)S(1)}, u32[]{:S(2)}, u32[]{:S(2)}) collective-permute-start(bf16[256,512]{1,0:T(8,128)(2,1)} %refs_0_.3), channel_id=1, source_target_pairs={{0,2},{1,3},{2,0},{3,1},{4,6},{5,7},{6,4},{7,5},{8,10},{9,11},{10,... | collective-permute-start | bytes 786440 | tf_op jit(solution)/shard_map/ppermute | solution.py:24
  15.2 16.9 %collective-permute-start = (bf16[256,512]{1,0:T(8,128)(2,1)}, bf16[256,512]{1,0:T(8,128)(2,1)S(1)}, u32[]{:S(2)}, u32[]{:S(2)}) collective-permute-start(bf16[256,512]{1,0:T(8,128)(2,1)} %refs_0_.3), channel_id=1, source_target_pairs={{0,1},{1,0},{2,3},{3,2},{4,5},{5,4},{6,7},{7,6},{8,9},{9,8},{10,11... | collective-permute-start | bytes 786440 | tf_op jit(solution)/shard_map/ppermute | solution.py:24
  27.6 7.2 %collective-permute-start.2 = (bf16[256,512]{1,0:T(8,128)(2,1)S(1)}, bf16[256,512]{1,0:T(8,128)(2,1)S(1)}, u32[]{:S(2)}, u32[]{:S(2)}) collective-permute-start(bf16[256,512]{1,0:T(8,128)(2,1)S(1)} %collective-permute-done.1.refs_2_), channel_id=1, source_target_pairs={{0,1},{1,0},{2,3},{3,2},{4,5},{5,4},{6,7},{7,6},{8,9},{9,8},{10,11... | collective-permute-start | bytes 786440 | tf_op jit(solution)/shard_map/ppermute | solution.py:24
  40.6 114.8 %reduce-scatter.3.cloned.1.call-start = ((), (), s32[]{:S(2)}) async-start(), calls=%async_computation.3 | async-start | bytes 1310720 | tf_op jit(solution)/shard_map/reduce_scatter | solution.py:113
  40.7 7.2 %collective-permute-start.5 = (bf16[256,512]{1,0:T(8,128)(2,1)}, bf16[256,512]{1,0:T(8,128)(2,1)}, u32[]{:S(2)}, u32[]{:S(2)}) collective-permute-start(bf16[256,512]{1,0:T(8,128)(2,1)} %get-tuple-element.75.refs_2_.refs_8_), channel_id=1, source_target_pairs={{0,4},{4,0},{1,5},{5,1},{2,6},{6,2},{3,7},{7,3},{8,12},{12,8},{9,1... | collective-permute-start | bytes 786440 | tf_op jit(solution)/shard_map/ppermute | solution.py:24
  42.8 48.0 %copy-start.13 = (bf16[2048]{0:T(1024)(128)(2,1)S(1)}, bf16[2048]{0:T(1024)(128)(2,1)}, u32[]{:S(2)}) copy-start(bf16[2048]{0:T(1024)(128)(2,1)} %param.26) | copy-start | bytes 12292
  53.4 8.6 %collective-permute-start.7 = (bf16[256,512]{1,0:T(8,128)(2,1)}, bf16[256,512]{1,0:T(8,128)(2,1)S(1)}, u32[]{:S(2)}, u32[]{:S(2)}) collective-permute-start(bf16[256,512]{1,0:T(8,128)(2,1)} %get-tuple-element.79), channel_id=1, source_target_pairs={{0,1},{1,0},{2,3},{3,2},{4,5},{5,4},{6,7},{7,6},{8,9},{9,8},{10,11... | collective-permute-start | bytes 786440 | tf_op jit(solution)/shard_map/ppermute | solution.py:24
  55.3 36.1 %collective-permute-start.12 = (bf16[256,2048]{1,0:T(8,128)(2,1)}, bf16[256,2048]{1,0:T(8,128)(2,1)}, u32[]{:S(2)}, u32[]{:S(2)}) collective-permute-start(bf16[256,2048]{1,0:T(8,128)(2,1)} %refs_4_.3), channel_id=1, source_target_pairs={{0,8},{8,0},{16,24},{24,16},{1,9},{9,1},{17,25},{25,17},{2,10},{10... | collective-permute-start | bytes 3145736 | tf_op jit(solution)/shard_map/ppermute | solution.py:24
  55.3 36.9 %collective-permute-start.13 = (bf16[256,2048]{1,0:T(8,128)(2,1)}, bf16[256,2048]{1,0:T(8,128)(2,1)}, u32[]{:S(2)}, u32[]{:S(2)}) collective-permute-start(bf16[256,2048]{1,0:T(8,128)(2,1)} %collective-permute-done.3.refs_10_.refs_5_), channel_id=1, source_target_pairs={{0,8},{8,0},{16,24},{24,16},{1,9},{9,1},{17,25},{25,17},{2,10},{10... | collective-permute-start | bytes 3145736 | tf_op jit(solution)/shard_map/ppermute | solution.py:24
  55.8 36.4 %collective-permute-start.14 = (bf16[256,2048]{1,0:T(8,128)(2,1)}, bf16[256,2048]{1,0:T(8,128)(2,1)}, u32[]{:S(2)}, u32[]{:S(2)}) collective-permute-start(bf16[256,2048]{1,0:T(8,128)(2,1)} %collective-permute-done.4.refs_11_.refs_4_), channel_id=1, source_target_pairs={{0,8},{8,0},{16,24},{24,16},{1,9},{9,1},{17,25},{25,17},{2,10},{10... | collective-permute-start | bytes 3145736 | tf_op jit(solution)/shard_map/ppermute | solution.py:24
  55.8 12.7 %collective-permute-start.6 = (bf16[256,512]{1,0:T(8,128)(2,1)}, bf16[256,512]{1,0:T(8,128)(2,1)S(1)}, u32[]{:S(2)}, u32[]{:S(2)}) collective-permute-start(bf16[256,512]{1,0:T(8,128)(2,1)} %get-tuple-element.77), channel_id=1, source_target_pairs={{0,1},{1,0},{2,3},{3,2},{4,5},{5,4},{6,7},{7,6},{8,9},{9,8},{10,11... | collective-permute-start | bytes 786440 | tf_op jit(solution)/shard_map/ppermute | solution.py:24
  63.0 15.1 %collective-permute-start.8 = (bf16[256,512]{1,0:T(8,128)(2,1)S(1)}, bf16[256,512]{1,0:T(8,128)(2,1)S(1)}, u32[]{:S(2)}, u32[]{:S(2)}) collective-permute-start(bf16[256,512]{1,0:T(8,128)(2,1)S(1)} %add_convert_fusion.7), channel_id=1, source_target_pairs={{0,2},{1,3},{2,0},{3,1},{4,6},{5,7},{6,4},{7,5},{8,10},{9,11},{10,... | collective-permute-start | bytes 786440 | tf_op jit(solution)/shard_map/ppermute | solution.py:24
  79.3 9.0 %collective-permute-start.10 = (bf16[256,512]{1,0:T(8,128)(2,1)S(1)}, bf16[256,512]{1,0:T(8,128)(2,1)S(1)}, u32[]{:S(2)}, u32[]{:S(2)}) collective-permute-start(bf16[256,512]{1,0:T(8,128)(2,1)S(1)} %fusion.1.refs_0_), channel_id=1, source_target_pairs={{0,2},{1,3},{2,0},{3,1},{4,6},{5,7},{6,4},{7,5},{8,10},{9,11},{10,... | collective-permute-start | bytes 786440 | tf_op jit(solution)/shard_map/ppermute | solution.py:24
  80.0 12.2 %collective-permute-start.9 = (bf16[256,512]{1,0:T(8,128)(2,1)S(1)}, bf16[256,512]{1,0:T(8,128)(2,1)S(1)}, u32[]{:S(2)}, u32[]{:S(2)}) collective-permute-start(bf16[256,512]{1,0:T(8,128)(2,1)S(1)} %fusion.1.refs_0_), channel_id=1, source_target_pairs={{0,1},{1,0},{2,3},{3,2},{4,5},{5,4},{6,7},{7,6},{8,9},{9,8},{10,11... | collective-permute-start | bytes 786440 | tf_op jit(solution)/shard_map/ppermute | solution.py:24
  88.2 6.9 %collective-permute-start.11 = (bf16[256,512]{1,0:T(8,128)(2,1)S(1)}, bf16[256,512]{1,0:T(8,128)(2,1)S(1)}, u32[]{:S(2)}, u32[]{:S(2)}) collective-permute-start(bf16[256,512]{1,0:T(8,128)(2,1)S(1)} %collective-permute-done.10.refs_2_), channel_id=1, source_target_pairs={{0,1},{1,0},{2,3},{3,2},{4,5},{5,4},{6,7},{7,6},{8,9},{9,8},{10,11... | collective-permute-start | bytes 786440 | tf_op jit(solution)/shard_map/ppermute | solution.py:24
  99.5 22.5 %collective-permute-start.18 = (bf16[256,2048]{1,0:T(8,128)(2,1)}, bf16[256,2048]{1,0:T(8,128)(2,1)}, u32[]{:S(2)}, u32[]{:S(2)}) collective-permute-start(bf16[256,2048]{1,0:T(8,128)(2,1)} %get-tuple-element.80.normed_hbm.refs_0_), channel_id=1, source_target_pairs={{0,16},{4,20},{8,24},{12,28},{16,0},{20,4},{24,8},{28,12},{1,17},{... | collective-permute-start | bytes 3145736 | tf_op jit(solution)/shard_map/ppermute | solution.py:97
  100.1 22.1 %collective-permute-start.15 = (bf16[256,2048]{1,0:T(8,128)(2,1)}, bf16[256,2048]{1,0:T(8,128)(2,1)}, u32[]{:S(2)}, u32[]{:S(2)}) collective-permute-start(bf16[256,2048]{1,0:T(8,128)(2,1)} %get-tuple-element.80.normed_hbm.refs_0_), channel_id=1, source_target_pairs={{0,4},{4,0},{8,12},{12,8},{16,20},{20,16},{24,28},{28,24},{1,5},{5... | collective-permute-start | bytes 3145736 | tf_op jit(solution)/shard_map/ppermute | solution.py:97
  105.2 19.2 %collective-permute-start.19 = (bf16[256,2048]{1,0:T(8,128)(2,1)}, bf16[256,2048]{1,0:T(8,128)(2,1)}, u32[]{:S(2)}, u32[]{:S(2)}) collective-permute-start(bf16[256,2048]{1,0:T(8,128)(2,1)} %get-tuple-element.80.normed_hbm.refs_0_), channel_id=1, source_target_pairs={{0,8},{8,0},{16,24},{24,16},{1,9},{9,1},{17,25},{25,17},{2,10},{10... | collective-permute-start | bytes 3145736 | tf_op jit(solution)/shard_map/ppermute | solution.py:24
  122.0 3.0 %collective-permute-start.20 = (bf16[256,2048]{1,0:T(8,128)(2,1)}, bf16[256,2048]{1,0:T(8,128)(2,1)}, u32[]{:S(2)}, u32[]{:S(2)}) collective-permute-start(bf16[256,2048]{1,0:T(8,128)(2,1)} %collective-permute-done.18.refs_1_), channel_id=1, source_target_pairs={{0,8},{8,0},{16,24},{24,16},{1,9},{9,1},{17,25},{25,17},{2,10},{10... | collective-permute-start | bytes 3145736 | tf_op jit(solution)/shard_map/ppermute | solution.py:24
  122.2 4.3 %collective-permute-start.17 = (bf16[256,2048]{1,0:T(8,128)(2,1)}, bf16[256,2048]{1,0:T(8,128)(2,1)}, u32[]{:S(2)}, u32[]{:S(2)}) collective-permute-start(bf16[256,2048]{1,0:T(8,128)(2,1)} %collective-permute-done.15.refs_0_), channel_id=1, source_target_pairs={{0,8},{8,0},{16,24},{24,16},{1,9},{9,1},{17,25},{25,17},{2,10},{10... | collective-permute-start | bytes 3145736 | tf_op jit(solution)/shard_map/ppermute | solution.py:24
  122.5 68.6 %all-gather.6.cloned.1.call-start = ((), (), s32[]{:S(2)}) async-start(), calls=%async_computation.5 | async-start | bytes 1310720 | tf_op jit(solution)/shard_map/all_gather | solution.py:958
  122.8 32.0 %collective-permute-start.22 = (bf16[256,2048]{1,0:T(8,128)(2,1)}, bf16[256,2048]{1,0:T(8,128)(2,1)}, u32[]{:S(2)}, u32[]{:S(2)}) collective-permute-start(bf16[256,2048]{1,0:T(8,128)(2,1)} %collective-permute-done.3.refs_10_.refs_5_), channel_id=1, source_target_pairs={{0,4},{4,0},{8,12},{12,8},{16,20},{20,16},{24,28},{28,24},{1,5},{5... | collective-permute-start | bytes 3145736 | tf_op jit(solution)/shard_map/ppermute | solution.py:97
  122.9 32.2 %collective-permute-start.16 = (bf16[256,2048]{1,0:T(8,128)(2,1)}, bf16[256,2048]{1,0:T(8,128)(2,1)}, u32[]{:S(2)}, u32[]{:S(2)}) collective-permute-start(bf16[256,2048]{1,0:T(8,128)(2,1)} %collective-permute-done.15.refs_0_), channel_id=1, source_target_pairs={{0,16},{4,20},{8,24},{12,28},{16,0},{20,4},{24,8},{28,12},{1,17},{... | collective-permute-start | bytes 3145736 | tf_op jit(solution)/shard_map/ppermute | solution.py:97
  154.8 3.1 %collective-permute-start.23 = (bf16[256,2048]{1,0:T(8,128)(2,1)}, bf16[256,2048]{1,0:T(8,128)(2,1)}, u32[]{:S(2)}, u32[]{:S(2)}) collective-permute-start(bf16[256,2048]{1,0:T(8,128)(2,1)} %collective-permute-done.22.refs_5_), channel_id=1, source_target_pairs={{0,8},{8,0},{16,24},{24,16},{1,9},{9,1},{17,25},{25,17},{2,10},{10... | collective-permute-start | bytes 3145736 | tf_op jit(solution)/shard_map/ppermute | solution.py:24
  155.0 4.4 %collective-permute-start.21 = (bf16[256,2048]{1,0:T(8,128)(2,1)}, bf16[256,2048]{1,0:T(8,128)(2,1)}, u32[]{:S(2)}, u32[]{:S(2)}) collective-permute-start(bf16[256,2048]{1,0:T(8,128)(2,1)} %collective-permute-done.16.refs_1_), channel_id=1, source_target_pairs={{0,8},{8,0},{16,24},{24,16},{1,9},{9,1},{17,25},{25,17},{2,10},{10... | collective-permute-start | bytes 3145736 | tf_op jit(solution)/shard_map/ppermute | solution.py:24
  155.4 92.6 %reduce-scatter.5.cloned.1.call-start = ((), (), s32[]{:S(2)}) async-start(), calls=%async_computation.4 | async-start | bytes 1310720 | tf_op jit(solution)/shard_map/reduce_scatter | solution.py:113
  190.9 69.8 %all-gather.8.cloned.1.call-start = ((), (), s32[]{:S(2)}) async-start(), calls=%async_computation.6 | async-start | bytes 4718592 | tf_op jit(solution)/shard_map/all_gather | solution.py:109
  202.0 2.9 collective-permute-start.28
  202.3 8.7 %collective-permute-start.27 = (bf16[256,512]{1,0:T(8,128)(2,1)S(1)}, bf16[256,512]{1,0:T(8,128)(2,1)}, u32[]{:S(2)}, u32[]{:S(2)}) collective-permute-start(bf16[256,512]{1,0:T(8,128)(2,1)S(1)} %copy-done.14), channel_id=1, source_target_pairs={{0,4},{4,0},{1,5},{5,1},{2,6},{6,2},{3,7},{7,3},{8,12},{12,8},{9,1... | collective-permute-start | bytes 786440 | tf_op jit(solution)/shard_map/ppermute | solution.py:1005
  214.3 10.3 %collective-permute-start.24 = (bf16[2048,768]{1,0:T(8,128)(2,1)}, bf16[2048,768]{1,0:T(8,128)(2,1)}, u32[]{:S(2)}, u32[]{:S(2)}) collective-permute-start(bf16[2048,768]{1,0:T(8,128)(2,1)} %get-tuple-element.91.refs_16_), channel_id=1, source_target_pairs={{0,8},{8,0},{16,24},{24,16},{1,9},{9,1},{17,25},{25,17},{2,10},{10... | collective-permute-start | bytes 9437192 | tf_op jit(solution)/shard_map/ppermute | solution.py:24
  214.3 10.5 %collective-permute-start.25 = (bf16[2048,768]{1,0:T(8,128)(2,1)}, bf16[2048,768]{1,0:T(8,128)(2,1)}, u32[]{:S(2)}, u32[]{:S(2)}) collective-permute-start(bf16[2048,768]{1,0:T(8,128)(2,1)} %get-tuple-element.93), channel_id=1, source_target_pairs={{0,8},{8,0},{16,24},{24,16},{1,9},{9,1},{17,25},{25,17},{2,10},{10... | collective-permute-start | bytes 9437192 | tf_op jit(solution)/shard_map/ppermute | solution.py:24
  214.8 14.5 %collective-permute-start.26 = (bf16[768,2048]{1,0:T(8,128)(2,1)}, bf16[768,2048]{1,0:T(8,128)(2,1)}, u32[]{:S(2)}, u32[]{:S(2)}) collective-permute-start(bf16[768,2048]{1,0:T(8,128)(2,1)} %get-tuple-element.94), channel_id=1, source_target_pairs={{0,8},{8,0},{16,24},{24,16},{1,9},{9,1},{17,25},{25,17},{2,10},{10... | collective-permute-start | bytes 9437192 | tf_op jit(solution)/shard_map/ppermute | solution.py:24
  214.9 26.2 %collective-permute-start.37 = (bf16[128,2048]{1,0:T(8,128)(2,1)}, bf16[128,2048]{1,0:T(8,128)(2,1)}, u32[]{:S(2)}, u32[]{:S(2)}) collective-permute-start(bf16[128,2048]{1,0:T(8,128)(2,1)} %get-tuple-element.137.refs_8_), channel_id=1, source_target_pairs={{0,4},{4,0},{8,12},{12,8},{16,20},{20,16},{24,28},{28,24},{1,5},{5... | collective-permute-start | bytes 1572872 | tf_op jit(solution)/shard_map/ppermute | solution.py:97
  215.2 26.0 %collective-permute-start.35 = (bf16[128,2048]{1,0:T(8,128)(2,1)}, bf16[128,2048]{1,0:T(8,128)(2,1)}, u32[]{:S(2)}, u32[]{:S(2)}) collective-permute-start(bf16[128,2048]{1,0:T(8,128)(2,1)} %get-tuple-element.138.refs_7_), channel_id=1, source_target_pairs={{0,16},{4,20},{8,24},{12,28},{16,0},{20,4},{24,8},{28,12},{1,17},{... | collective-permute-start | bytes 1572872 | tf_op jit(solution)/shard_map/ppermute | solution.py:97
  224.6 19.8 %collective-permute-start.29 = (bf16[272,512]{1,0:T(8,128)(2,1)}, bf16[272,512]{1,0:T(8,128)(2,1)}, u32[]{:S(2)}, u32[]{:S(2)}) collective-permute-start(bf16[272,512]{1,0:T(8,128)(2,1)} %get-tuple-element.115), channel_id=1, source_target_pairs={{0,1},{1,0},{2,3},{3,2},{4,5},{5,4},{6,7},{7,6},{8,9},{9,8},{10,11... | collective-permute-start | bytes 835592 | tf_op jit(solution)/shard_map/ppermute | solution.py:24
  224.8 19.6 %collective-permute-start.30 = (bf16[272,512]{1,0:T(8,128)(2,1)}, bf16[272,512]{1,0:T(8,128)(2,1)}, u32[]{:S(2)}, u32[]{:S(2)}) collective-permute-start(bf16[272,512]{1,0:T(8,128)(2,1)} %get-tuple-element.118), channel_id=1, source_target_pairs={{0,1},{1,0},{2,3},{3,2},{4,5},{5,4},{6,7},{7,6},{8,9},{9,8},{10,11... | collective-permute-start | bytes 835592 | tf_op jit(solution)/shard_map/ppermute | solution.py:24
  244.1 33.2 %collective-permute-start.36 = (bf16[128,2048]{1,0:T(8,128)(2,1)}, bf16[128,2048]{1,0:T(8,128)(2,1)}, u32[]{:S(2)}, u32[]{:S(2)}) collective-permute-start(bf16[128,2048]{1,0:T(8,128)(2,1)} %get-tuple-element.126), channel_id=1, source_target_pairs={{0,4},{4,0},{8,12},{12,8},{16,20},{20,16},{24,28},{28,24},{1,5},{5... | collective-permute-start | bytes 1572872 | tf_op jit(solution)/shard_map/ppermute | solution.py:97
  244.4 35.0 %collective-permute-start.38 = (bf16[128,2048]{1,0:T(8,128)(2,1)}, bf16[128,2048]{1,0:T(8,128)(2,1)}, u32[]{:S(2)}, u32[]{:S(2)}) collective-permute-start(bf16[128,2048]{1,0:T(8,128)(2,1)} %get-tuple-element.129), channel_id=1, source_target_pairs={{0,16},{4,20},{8,24},{12,28},{16,0},{20,4},{24,8},{28,12},{1,17},{... | collective-permute-start | bytes 1572872 | tf_op jit(solution)/shard_map/ppermute | solution.py:97
  247.7 28.4 %collective-permute-start.31 = (bf16[272,512]{1,0:T(8,128)(2,1)}, bf16[272,512]{1,0:T(8,128)(2,1)}, u32[]{:S(2)}, u32[]{:S(2)}) collective-permute-start(bf16[272,512]{1,0:T(8,128)(2,1)} %add_convert_fusion.5.refs_4_), channel_id=1, source_target_pairs={{0,2},{1,3},{2,0},{3,1},{4,6},{5,7},{6,4},{7,5},{8,10},{9,11},{10,... | collective-permute-start | bytes 835592 | tf_op jit(solution)/shard_map/ppermute | solution.py:24
  277.4 2.0 collective-permute-start.32
  279.1 8.8 %collective-permute-start.39 = (bf16[128,2048]{1,0:T(8,128)(2,1)S(1)}, bf16[128,2048]{1,0:T(8,128)(2,1)S(1)}, u32[]{:S(2)}, u32[]{:S(2)}) collective-permute-start(bf16[128,2048]{1,0:T(8,128)(2,1)S(1)} %add_convert_fusion.3), channel_id=1, source_target_pairs={{0,8},{8,0},{16,24},{24,16},{1,9},{9,1},{17,25},{25,17},{2,10},{10... | collective-permute-start | bytes 1572872 | tf_op jit(solution)/shard_map/ppermute | solution.py:24
  279.4 3.7 %collective-permute-start.33 = (f32[1280]{0:T(1024)S(1)}, f32[1280]{0:T(1024)S(1)}, u32[]{:S(2)}, u32[]{:S(2)}) collective-permute-start(f32[1280]{0:T(1024)S(1)} %fusion.8), channel_id=1, source_target_pairs={{0,16},{4,20},{8,24},{12,28},{16,0},{20,4},{24,8},{28,12},{1,17},{... | collective-permute-start | bytes 15368 | tf_op jit(solution)/shard_map/ppermute | solution.py:97
  282.5 5.4 %collective-permute-start.40 = (bf16[128,2048]{1,0:T(8,128)(2,1)S(1)}, bf16[128,2048]{1,0:T(8,128)(2,1)S(1)}, u32[]{:S(2)}, u32[]{:S(2)}) collective-permute-start(bf16[128,2048]{1,0:T(8,128)(2,1)S(1)} %add_convert_fusion.1), channel_id=1, source_target_pairs={{0,8},{8,0},{16,24},{24,16},{1,9},{9,1},{17,25},{25,17},{2,10},{10... | collective-permute-start | bytes 1572872 | tf_op jit(solution)/shard_map/ppermute | solution.py:24
  283.1 3.7 %collective-permute-start.34 = (f32[1280]{0:T(1024)S(1)}, f32[1280]{0:T(1024)S(1)}, u32[]{:S(2)}, u32[]{:S(2)}) collective-permute-start(f32[1280]{0:T(1024)S(1)} %add.93), channel_id=1, source_target_pairs={{0,4},{4,0},{8,12},{12,8},{16,20},{20,16},{24,28},{28,24},{1,5},{5... | collective-permute-start | bytes 15368 | tf_op jit(solution)/shard_map/ppermute | solution.py:97
  (14 other events, 71.5 us)
Sparse Core Ops, SparseCore 0:
  40.7 54.6 all-gather.3
  214.4 46.2 all-gather.7
Sparse Core Ops, SparseCore 1:
  122.6 25.5 reduce-scatter.2
  155.5 26.2 all-gather.5
  191.0 25.5 reduce-scatter.4

commit v5 on v3

--- a/solution.py
+++ b/solution.py
@@ -153,7 +153,7 @@
 
 def cost(flops, moved):
     return pl.CostEstimate(
-        flops=int(flops) // SCALE, bytes_accessed=int(moved) // SCALE, transcendentals=0
+        flops=int(flops) * 2, bytes_accessed=int(moved) * 2, transcendentals=0
     )
 
 

time: 301 us -> 300 us (level)
  starting transfers between devices: 39.9 us -> 43.2 us
  waiting for transfers between devices: 62.9 us -> 59.8 us
  transfers between devices with their start and end apart: 46 -> 46, of which waited for: 23 -> 22; matrix products, arithmetic and copies ran while one was open for 11% -> 11% of each run, Pallas kernels for 45% -> 45%
where the time goes in v5:
time: 300 us; the launch traced here: 298 us
  Pallas kernels  140 us (47%)
  waiting for transfers between devices  59.8 us (20%)
  starting transfers between devices  43.2 us (14%)
  other arithmetic  27 us (9%)
  between operations  16.1 us (5%)
  local copies, waits for them, and re-layouts  10 us (3%)
    pallas_call x2, Pallas kernels, feed_weights(): pl.pallas_call(functools.partial(feed_weight_body, parts, extra, last, bl...  59.9 us
    ppermute x28, waiting for transfers between devices, swap(): return lax.ppermute(value, axis, [(i, i ^ bit) for i in range(size)])  45 us
    pallas_call x7, Pallas kernels, kernel_call(): pl.pallas_call(run, out_shape=tuple(outs), in_specs=[SMEM] + [ANY] * (cou...  36.3 us
    ppermute x28, starting transfers between devices, swap(): return lax.ppermute(value, axis, [(i, i ^ bit) for i in range(size)])  24.9 us
    ppermute x12, starting transfers between devices, send_plane(): lax.ppermute(value, ('dp', 'ctx'), [(i, i ^ mask) for i in range(size)])  17.7 us
    pallas_call x1, Pallas kernels, feed_forward(): pl.pallas_call(functools.partial(feed_forward_body, tile, len(after)), ou...  16.3 us
    pallas_call x1, Pallas kernels, projection_weights(): pl.pallas_call(functools.partial(projection_body, parts, tile, len(after)...  15.4 us
    pallas_call x1, Pallas kernels, assemble(): pl.pallas_call(functools.partial(assemble_body, len(after)), out_shape=[s...  11.8 us
  transfers between devices with their start and end apart: 46, of which 22 were waited for; matrix products, arithmetic and copies ran while one was open for 11% of the time, Pallas kernels for 45%

profile of v5, /device:TPU:0, one launch (start us, length us, event | category | flops | bytes accessed | tf_op | source)
XLA Modules:
  0.0 297.8 jit_solution(2545691943264239916)
XLA Ops:
  8.1 3.0 %collective-permute-start.3 = (bf16[256,2048]{1,0:T(8,128)(2,1)}, bf16[256,2048]{1,0:T(8,128)(2,1)}, u32[]{:S(2)}, u32[]{:S(2)}) collective-permute-start(bf16[256,2048]{1,0:T(8,128)(2,1)} %refs_4_.3), channel_id=1, source_target_pairs={{0,16},{4,20},{8,24},{12,28},{16,0},{20,4},{24,8},{28,12},{1,17},{... | collective-permute-start | bytes 3145736 | tf_op jit(solution)/shard_map/ppermute | solution.py:97
  11.1 1.5 collective-permute-start.4
  12.6 2.6 collective-permute-start.1
  15.2 1.6 collective-permute-start
  20.1 6.8 %collective-permute-done.1.refs_2_ = bf16[256,512]{1,0:T(8,128)(2,1)S(1)} collective-permute-done((bf16[256,512]{1,0:T(8,128)(2,1)}, bf16[256,512]{1,0:T(8,128)(2,1)S(1)}, u32[]{:S(2)}, u32[]{:S(2)}) %collective-permute-start.1) | collective-permute-done | bytes 262176 | tf_op jit(solution)/shard_map/ppermute | solution.py:24
  32.1 2.6 collective-permute-done.2.refs_3_
  36.0 4.6 %key_value.1 = (bf16[256,2048]{1,0:T(8,128)(2,1)}, bf16[256,512]{1,0:T(8,128)(2,1)}, f32[256,256]{1,0:T(8,128)}, f32[256,1]{1,0:T(8,128)}) custom-call(s32[4]{0:T(128)} %pad_add_fusion.ids, bf16[256,512]{1,0:T(8,128)(2,1)} %refs_0_.3, bf16[256,512]{1,0:T(8,128)(2,1)} %copy-done.8, bf16[256,512]{1,0:T(8,128)(2,1)} %copy-done.7, bf16[256,512]{1,0:T(8,128)(2,1)} %copy-done.9, ...), custom_call_target="tpu_custom_call" | custom-call | flops 1073741824 | bytes 9980928 | tf_op jit(solution)/shard_map/key_value/pallas_call | solution.py:200
  40.7 1.6 collective-permute-start.5
  42.8 4.3 %query.1 = (bf16[256,512]{1,0:T(8,128)(2,1)}, f32[256,512]{1,0:T(8,128)}) custom-call(s32[4]{0:T(128)} %pad_add_fusion.ids, bf16[256,2048]{1,0:T(8,128)(2,1)} %get-tuple-element.73.refs_0_, bf16[2048,512]{1,0:T(8,128)(2,1)} %refs_9_.7, f32[1,128]{1,0:T(1,128)} %bitcast_convert_fusion.1.refs_2_.refs_13_, ...), custom_call_target="tpu_custom_call" | custom-call | flops 1073741824 | bytes 8389632 | tf_op jit(solution)/shard_map/query/pallas_call | solution.py:200
  47.9 5.5 %attention.1 = (bf16[256,512]{1,0:T(8,128)(2,1)}, bf16[256,512]{1,0:T(8,128)(2,1)}, bf16[256,512]{1,0:T(8,128)(2,1)}, bf16[256,512]{1,0:T(8,128)(2,1)}, bf16[256,512]{1,0:T(8,128)(2,1)}) custom-call(s32[4]{0:T(128)} %pad_add_fusion.ids, bf16[256,512]{1,0:T(8,128)(2,1)} %get-tuple-element.74.refs_0_.refs_6_, s32[256,1]{1,0:T(8,128)} %copy.34.refs_12_.refs_1_.refs_7_, ...), custom_call_target="tpu_custom_call" | custom-call | flops 1610612736 | bytes 8394752 | tf_op jit(solution)/shard_map/attention/pallas_call | solution.py:200
  53.4 1.9 collective-permute-start.7
  56.0 6.0 %collective-permute-done.7 = bf16[256,512]{1,0:T(8,128)(2,1)S(1)} collective-permute-done((bf16[256,512]{1,0:T(8,128)(2,1)}, bf16[256,512]{1,0:T(8,128)(2,1)S(1)}, u32[]{:S(2)}, u32[]{:S(2)}) %collective-permute-start.7) | collective-permute-done | bytes 262176 | tf_op jit(solution)/shard_map/ppermute | solution.py:24
  63.0 4.3 %collective-permute-start.8 = (bf16[256,512]{1,0:T(8,128)(2,1)S(1)}, bf16[256,512]{1,0:T(8,128)(2,1)S(1)}, u32[]{:S(2)}, u32[]{:S(2)}) collective-permute-start(bf16[256,512]{1,0:T(8,128)(2,1)S(1)} %add_convert_fusion.7), channel_id=1, source_target_pairs={{0,2},{1,3},{2,0},{3,1},{4,6},{5,7},{6,4},{7,5},{8,10},{9,11},{10,... | collective-permute-start | bytes 786440 | tf_op jit(solution)/shard_map/ppermute | solution.py:24
  68.5 9.6 %collective-permute-done.8 = bf16[256,512]{1,0:T(8,128)(2,1)S(1)} collective-permute-done((bf16[256,512]{1,0:T(8,128)(2,1)S(1)}, bf16[256,512]{1,0:T(8,128)(2,1)S(1)}, u32[]{:S(2)}, u32[]{:S(2)}) %collective-permute-start.8) | collective-permute-done | bytes 262176 | tf_op jit(solution)/shard_map/ppermute | solution.py:24
  79.9 4.1 %collective-permute-start.9 = (bf16[256,512]{1,0:T(8,128)(2,1)S(1)}, bf16[256,512]{1,0:T(8,128)(2,1)S(1)}, u32[]{:S(2)}, u32[]{:S(2)}) collective-permute-start(bf16[256,512]{1,0:T(8,128)(2,1)S(1)} %fusion.1.refs_0_), channel_id=1, source_target_pairs={{0,1},{1,0},{2,3},{3,2},{4,5},{5,4},{6,7},{7,6},{8,9},{9,8},{10,11... | collective-permute-start | bytes 786440 | tf_op jit(solution)/shard_map/ppermute | solution.py:24
  84.1 4.1 %collective-permute-done.10.refs_2_ = bf16[256,512]{1,0:T(8,128)(2,1)S(1)} collective-permute-done((bf16[256,512]{1,0:T(8,128)(2,1)S(1)}, bf16[256,512]{1,0:T(8,128)(2,1)S(1)}, u32[]{:S(2)}, u32[]{:S(2)}) %collective-permute-start.10) | collective-permute-done | bytes 262176 | tf_op jit(solution)/shard_map/ppermute | solution.py:24
  88.2 2.6 collective-permute-start.11
  93.4 1.7 collective-permute-done.11.refs_3_
  95.8 3.7 %second_norm.1 = (bf16[256,2048]{1,0:T(8,128)(2,1)}, bf16[256,2048]{1,0:T(8,128)(2,1)}, f32[256,1]{1,0:T(8,128)}) custom-call(s32[4]{0:T(128)} %pad_add_fusion.ids, bf16[256,512]{1,0:T(8,128)(2,1)} %copy-done.3, bf16[256,512]{1,0:T(8,128)(2,1)} %copy-done.11, bf16[256,512]{1,0:T(8,128)(2,1)} %copy-done.10, bf16[256,512]{1,0:T(8,128)(2,1)} %copy-done.12, ...), custom_call_target="tpu_custom_call" | custom-call | flops 8388608 | bytes 6309888 | tf_op jit(solution)/shard_map/second_norm/pallas_call | solution.py:200
  100.1 5.2 %collective-permute-start.15 = (bf16[256,2048]{1,0:T(8,128)(2,1)}, bf16[256,2048]{1,0:T(8,128)(2,1)}, u32[]{:S(2)}, u32[]{:S(2)}) collective-permute-start(bf16[256,2048]{1,0:T(8,128)(2,1)} %get-tuple-element.80.normed_hbm.refs_0_), channel_id=1, source_target_pairs={{0,4},{4,0},{8,12},{12,8},{16,20},{20,16},{24,28},{28,24},{1,5},{5... | collective-permute-start | bytes 3145736 | tf_op jit(solution)/shard_map/ppermute | solution.py:97
  105.3 16.3 %feed_forward.1 = (bf16[256,2048]{1,0:T(8,128)(2,1)}, bf16[256,2048]{1,0:T(8,128)(2,1)}) custom-call(s32[4]{0:T(128)} %pad_add_fusion.ids, bf16[256,2048]{1,0:T(8,128)(2,1)} %get-tuple-element.80.normed_hbm.refs_0_, bf16[256,2048]{1,0:T(8,128)(2,1)} %refs_4_.3, bf16[2048,1536]{1,0:T(8,128)(2,1)} %refs_8_.5, bf16[2048,1536]{1,0:T(8,128)(2,1)} %refs_9_.6, ...), custom_call_target="tpu_custom_call" | custom-call | flops 19327352832 | bytes 46137344 | tf_op jit(solution)/shard_map/feed_forward/pallas_call | solution.py:391
  122.7 1.6 collective-permute-start.16
  125.0 1.5 collective-permute-done.17.refs_14_.refs_2_
  126.5 28.5 %feed_weights.2 = (f32[2048,1536]{1,0:T(8,128)}, f32[2048,1536]{1,0:T(8,128)}, f32[1536,2048]{1,0:T(8,128)}) custom-call(s32[4]{0:T(128)} %pad_add_fusion.ids, bf16[256,2048]{1,0:T(8,128)(2,1)} %get-tuple-element.80.normed_hbm.refs_0_, bf16[256,2048]{1,0:T(8,128)(2,1)} %collective-permute-done.18.refs_1_, ...), custom_call_target="tpu_custom_call" | custom-call | flops 38654705664 | bytes 16777216 | tf_op jit(solution)/shard_map/feed_weights/pallas_call | solution.py:691
  155.6 2.4 collective-permute-done.23.refs_7_
  158.0 1.5 collective-permute-done.21.refs_3_
  159.5 31.5 %feed_weights.3 = (f32[2048,1536]{1,0:T(8,128)}, f32[2048,1536]{1,0:T(8,128)}, f32[1536,2048]{1,0:T(8,128)}, bf16[2048,768]{1,0:T(8,128)(2,1)}, bf16[2048,768]{1,0:T(8,128)(2,1)}, /*index=5*/bf16[768,2048]{1,0:T(8,128)(2,1)}) custom-call(s32[4]{0:T(128)} %pad_add_fusion.ids, ...), custom_call_target="tpu_custom_call", output_to_operand_aliasing={{0}: (12, {}), {1}: (13, {}), {2}: (14, {})} | custom-call | flops 38654705664 | bytes 16777216 | tf_op jit(solution)/shard_map/feed_weights/pallas_call | solution.py:691
  191.3 8.6 %middle.1 = (f32[256,512]{1,0:T(8,128)}, bf16[256,2048]{1,0:T(8,128)(2,1)}, f32[1,2048]{1,0:T(1,128)}, bf16[256,512]{1,0:T(8,128)(2,1)}, f32[1,128]{1,0:T(1,128)...) custom-call(s32[4]{0:T(128)} %pad_add_fusion.ids, bf16[256,2048]{1,0:T(8,128)(2,1)} %all-gather.6.cloned.1.call-done.refs_0_, ...), custom_call_target="tpu_custom_call" | custom-call | flops 1073741824 | bytes 18917376 | tf_op jit(solution)/shard_map/middle/pallas_call | solution.py:200
  200.0 2.1 convolution_convert_fusion
  202.5 2.5 collective-permute-done.28
  205.0 1.6 add_convert_fusion
  208.6 2.4 collective-permute-done.27.refs_1_
  211.0 3.3 %key_backward.1 = (bf16[256,1024]{1,0:T(8,128)(2,1)}, f32[1,128]{1,0:T(1,128)}) custom-call(s32[4]{0:T(128)} %pad_add_fusion.ids, f32[256,512]{1,0:T(8,128)} %get-tuple-element.103.refs_0_, bf16[256,512]{1,0:T(8,128)(2,1)} %collective-permute-done.27.refs_1_, f32[256,256]{1,0:T(8,128)} %get-tuple-element.105.refs_2_, ...), custom_call_target="tpu_custom_call" | custom-call | flops 5242880 | bytes 4196352 | tf_op jit(solution)/shard_map/key_backward/pallas_call | solution.py:200
  218.3 6.4 %first_grad.1 = (bf16[272,512]{1,0:T(8,128)(2,1)}, bf16[272,512]{1,0:T(8,128)(2,1)}, bf16[272,512]{1,0:T(8,128)(2,1)}, bf16[272,512]{1,0:T(8,128)(2,1)}) custom-call(s32[4]{0:T(128)} %pad_add_fusion.ids, bf16[256,512]{1,0:T(8,128)(2,1)} %refs_0_.3, bf16[256,512]{1,0:T(8,128)(2,1)} %copy-done.8, bf16[256,512]{1,0:T(8,128)(2,1)} %copy-done.7, ...), custom_call_target="tpu_custom_call" | custom-call | flops 2147483648 | bytes 13783040 | tf_op jit(solution)/shard_map/first_grad/pallas_call | solution.py:200
  224.9 1.9 collective-permute-start.30
  226.8 2.6 collective-permute-done.26.down_low
  229.4 11.8 %assemble.1 = (f32[2048,1536]{1,0:T(8,128)}, f32[2048,1536]{1,0:T(8,128)}, f32[1536,2048]{1,0:T(8,128)}) custom-call(s32[4]{0:T(128)} %pad_add_fusion.ids, bf16[2048,768]{1,0:T(8,128)(2,1)} %collective-permute-done.24.gate_low, bf16[2048,768]{1,0:T(8,128)(2,1)} %collective-permute-done.25.up_low, ...), custom_call_target="tpu_custom_call", output_to_operand_aliasing={{0}: (4, {}), {1}: (5, {}), {2}: (6, {})} | custom-call | bytes 56623104 | tf_op jit(solution)/shard_map/assemble/pallas_call | solution.py:726
  241.3 2.9 add_convert_fusion.4
  245.8 1.8 add_convert_fusion.5.refs_4_
  247.7 1.8 add_convert_fusion.6
  249.5 1.8 convert_add_fusion.2.refs_3_
  251.3 9.2 %all-gather.8.cloned.1.call-done.refs_1_ = bf16[2048,1024]{1,0:T(8,128)(2,1)} async-done(((bf16[256,1024]{1,0:T(8,128)(2,1)}), bf16[2048,1024]{1,0:T(8,128)(2,1)}) %all-gather.8.cloned.1.call-update) | async-done | bytes 4194320 | tf_op jit(solution)/shard_map/all_gather | solution.py:109
  260.5 15.4 %projection_weights.1 = (f32[2048,512]{1,0:T(8,128)}, f32[2048,256]{1,0:T(8,128)}, f32[2048,256]{1,0:T(8,128)}) custom-call(s32[4]{0:T(128)} %pad_add_fusion.ids, bf16[2048,2048]{1,0:T(8,128)(2,1)} %all-gather.4.cloned.1.call-done.refs_15_.refs_0_, bf16[2048,1024]{1,0:T(8,128)(2,1)} %all-gather.8.cloned.1.call-done.refs_1_, ...), custom_call_target="tpu_custom_call" | custom-call | flops 17179869184 | bytes 16777216 | tf_op jit(solution)/shard_map/projection_weights/pallas_call | solution.py:801
  277.5 1.4 add_convert_fusion.3
  279.2 1.8 collective-permute-start.33
  281.0 1.4 add_convert_fusion.1
  284.9 1.7 collective-permute-done.34
  287.7 2.5 fusion
  (134 shorter events, 36.4 us)
Async XLA Ops:
  8.0 34.2 %copy-start.17 = (bf16[128]{0:T(256)(128)(2,1)S(1)}, bf16[128]{0:T(256)(128)(2,1)}, u32[]{:S(2)}) copy-start(bf16[128]{0:T(256)(128)(2,1)} %param.23) | copy-start | bytes 772
  8.0 118.4 %all-gather.4.cloned.1.call-start = ((), (), s32[]{:S(2)}) async-start(), calls=%async_computation.2 | async-start | bytes 9437184 | tf_op jit(solution)/shard_map/all_gather | solution.py:109
  8.1 26.7 %collective-permute-start.3 = (bf16[256,2048]{1,0:T(8,128)(2,1)}, bf16[256,2048]{1,0:T(8,128)(2,1)}, u32[]{:S(2)}, u32[]{:S(2)}) collective-permute-start(bf16[256,2048]{1,0:T(8,128)(2,1)} %refs_4_.3), channel_id=1, source_target_pairs={{0,16},{4,20},{8,24},{12,28},{16,0},{20,4},{24,8},{28,12},{1,17},{... | collective-permute-start | bytes 3145736 | tf_op jit(solution)/shard_map/ppermute | solution.py:97
  11.1 24.9 %collective-permute-start.4 = (bf16[256,2048]{1,0:T(8,128)(2,1)}, bf16[256,2048]{1,0:T(8,128)(2,1)}, u32[]{:S(2)}, u32[]{:S(2)}) collective-permute-start(bf16[256,2048]{1,0:T(8,128)(2,1)} %refs_4_.3), channel_id=1, source_target_pairs={{0,4},{4,0},{8,12},{12,8},{16,20},{20,16},{24,28},{28,24},{1,5},{5... | collective-permute-start | bytes 3145736 | tf_op jit(solution)/shard_map/ppermute | solution.py:97
  12.6 14.3 %collective-permute-start.1 = (bf16[256,512]{1,0:T(8,128)(2,1)}, bf16[256,512]{1,0:T(8,128)(2,1)S(1)}, u32[]{:S(2)}, u32[]{:S(2)}) collective-permute-start(bf16[256,512]{1,0:T(8,128)(2,1)} %refs_0_.3), channel_id=1, source_target_pairs={{0,2},{1,3},{2,0},{3,1},{4,6},{5,7},{6,4},{7,5},{8,10},{9,11},{10,... | collective-permute-start | bytes 786440 | tf_op jit(solution)/shard_map/ppermute | solution.py:24
  15.2 16.9 %collective-permute-start = (bf16[256,512]{1,0:T(8,128)(2,1)}, bf16[256,512]{1,0:T(8,128)(2,1)S(1)}, u32[]{:S(2)}, u32[]{:S(2)}) collective-permute-start(bf16[256,512]{1,0:T(8,128)(2,1)} %refs_0_.3), channel_id=1, source_target_pairs={{0,1},{1,0},{2,3},{3,2},{4,5},{5,4},{6,7},{7,6},{8,9},{9,8},{10,11... | collective-permute-start | bytes 786440 | tf_op jit(solution)/shard_map/ppermute | solution.py:24
  27.6 7.2 %collective-permute-start.2 = (bf16[256,512]{1,0:T(8,128)(2,1)S(1)}, bf16[256,512]{1,0:T(8,128)(2,1)S(1)}, u32[]{:S(2)}, u32[]{:S(2)}) collective-permute-start(bf16[256,512]{1,0:T(8,128)(2,1)S(1)} %collective-permute-done.1.refs_2_), channel_id=1, source_target_pairs={{0,1},{1,0},{2,3},{3,2},{4,5},{5,4},{6,7},{7,6},{8,9},{9,8},{10,11... | collective-permute-start | bytes 786440 | tf_op jit(solution)/shard_map/ppermute | solution.py:24
  40.6 114.9 %reduce-scatter.3.cloned.1.call-start = ((), (), s32[]{:S(2)}) async-start(), calls=%async_computation.3 | async-start | bytes 1310720 | tf_op jit(solution)/shard_map/reduce_scatter | solution.py:113
  40.7 7.2 %collective-permute-start.5 = (bf16[256,512]{1,0:T(8,128)(2,1)}, bf16[256,512]{1,0:T(8,128)(2,1)}, u32[]{:S(2)}, u32[]{:S(2)}) collective-permute-start(bf16[256,512]{1,0:T(8,128)(2,1)} %get-tuple-element.75.refs_2_.refs_8_), channel_id=1, source_target_pairs={{0,4},{4,0},{1,5},{5,1},{2,6},{6,2},{3,7},{7,3},{8,12},{12,8},{9,1... | collective-permute-start | bytes 786440 | tf_op jit(solution)/shard_map/ppermute | solution.py:24
  47.1 43.7 %copy-start.15 = (bf16[2048]{0:T(1024)(128)(2,1)S(1)}, bf16[2048]{0:T(1024)(128)(2,1)}, u32[]{:S(2)}) copy-start(bf16[2048]{0:T(1024)(128)(2,1)} %param.26) | copy-start | bytes 12292
  53.4 8.6 %collective-permute-start.7 = (bf16[256,512]{1,0:T(8,128)(2,1)}, bf16[256,512]{1,0:T(8,128)(2,1)S(1)}, u32[]{:S(2)}, u32[]{:S(2)}) collective-permute-start(bf16[256,512]{1,0:T(8,128)(2,1)} %get-tuple-element.79), channel_id=1, source_target_pairs={{0,1},{1,0},{2,3},{3,2},{4,5},{5,4},{6,7},{7,6},{8,9},{9,8},{10,11... | collective-permute-start | bytes 786440 | tf_op jit(solution)/shard_map/ppermute | solution.py:24
  55.3 36.1 %collective-permute-start.12 = (bf16[256,2048]{1,0:T(8,128)(2,1)}, bf16[256,2048]{1,0:T(8,128)(2,1)S(1)}, u32[]{:S(2)}, u32[]{:S(2)}) collective-permute-start(bf16[256,2048]{1,0:T(8,128)(2,1)} %refs_4_.3), channel_id=1, source_target_pairs={{0,8},{8,0},{16,24},{24,16},{1,9},{9,1},{17,25},{25,17},{2,10},{10... | collective-permute-start | bytes 3145736 | tf_op jit(solution)/shard_map/ppermute | solution.py:24
  55.3 37.1 %collective-permute-start.13 = (bf16[256,2048]{1,0:T(8,128)(2,1)}, bf16[256,2048]{1,0:T(8,128)(2,1)S(1)}, u32[]{:S(2)}, u32[]{:S(2)}) collective-permute-start(bf16[256,2048]{1,0:T(8,128)(2,1)} %collective-permute-done.3.refs_10_.refs_5_), channel_id=1, source_target_pairs={{0,8},{8,0},{16,24},{24,16},{1,9},{9,1},{17,25},{25,17},{2,10},{10... | collective-permute-start | bytes 3145736 | tf_op jit(solution)/shard_map/ppermute | solution.py:24
  55.8 37.6 %collective-permute-start.14 = (bf16[256,2048]{1,0:T(8,128)(2,1)}, bf16[256,2048]{1,0:T(8,128)(2,1)}, u32[]{:S(2)}, u32[]{:S(2)}) collective-permute-start(bf16[256,2048]{1,0:T(8,128)(2,1)} %collective-permute-done.4.refs_11_.refs_4_), channel_id=1, source_target_pairs={{0,8},{8,0},{16,24},{24,16},{1,9},{9,1},{17,25},{25,17},{2,10},{10... | collective-permute-start | bytes 3145736 | tf_op jit(solution)/shard_map/ppermute | solution.py:24
  55.8 12.7 %collective-permute-start.6 = (bf16[256,512]{1,0:T(8,128)(2,1)}, bf16[256,512]{1,0:T(8,128)(2,1)S(1)}, u32[]{:S(2)}, u32[]{:S(2)}) collective-permute-start(bf16[256,512]{1,0:T(8,128)(2,1)} %get-tuple-element.77), channel_id=1, source_target_pairs={{0,1},{1,0},{2,3},{3,2},{4,5},{5,4},{6,7},{7,6},{8,9},{9,8},{10,11... | collective-permute-start | bytes 786440 | tf_op jit(solution)/shard_map/ppermute | solution.py:24
  63.0 15.1 %collective-permute-start.8 = (bf16[256,512]{1,0:T(8,128)(2,1)S(1)}, bf16[256,512]{1,0:T(8,128)(2,1)S(1)}, u32[]{:S(2)}, u32[]{:S(2)}) collective-permute-start(bf16[256,512]{1,0:T(8,128)(2,1)S(1)} %add_convert_fusion.7), channel_id=1, source_target_pairs={{0,2},{1,3},{2,0},{3,1},{4,6},{5,7},{6,4},{7,5},{8,10},{9,11},{10,... | collective-permute-start | bytes 786440 | tf_op jit(solution)/shard_map/ppermute | solution.py:24
  79.2 8.9 %collective-permute-start.10 = (bf16[256,512]{1,0:T(8,128)(2,1)S(1)}, bf16[256,512]{1,0:T(8,128)(2,1)S(1)}, u32[]{:S(2)}, u32[]{:S(2)}) collective-permute-start(bf16[256,512]{1,0:T(8,128)(2,1)S(1)} %fusion.1.refs_0_), channel_id=1, source_target_pairs={{0,2},{1,3},{2,0},{3,1},{4,6},{5,7},{6,4},{7,5},{8,10},{9,11},{10,... | collective-permute-start | bytes 786440 | tf_op jit(solution)/shard_map/ppermute | solution.py:24
  79.9 12.2 %collective-permute-start.9 = (bf16[256,512]{1,0:T(8,128)(2,1)S(1)}, bf16[256,512]{1,0:T(8,128)(2,1)S(1)}, u32[]{:S(2)}, u32[]{:S(2)}) collective-permute-start(bf16[256,512]{1,0:T(8,128)(2,1)S(1)} %fusion.1.refs_0_), channel_id=1, source_target_pairs={{0,1},{1,0},{2,3},{3,2},{4,5},{5,4},{6,7},{7,6},{8,9},{9,8},{10,11... | collective-permute-start | bytes 786440 | tf_op jit(solution)/shard_map/ppermute | solution.py:24
  88.2 7.0 %collective-permute-start.11 = (bf16[256,512]{1,0:T(8,128)(2,1)S(1)}, bf16[256,512]{1,0:T(8,128)(2,1)S(1)}, u32[]{:S(2)}, u32[]{:S(2)}) collective-permute-start(bf16[256,512]{1,0:T(8,128)(2,1)S(1)} %collective-permute-done.10.refs_2_), channel_id=1, source_target_pairs={{0,1},{1,0},{2,3},{3,2},{4,5},{5,4},{6,7},{7,6},{8,9},{9,8},{10,11... | collective-permute-start | bytes 786440 | tf_op jit(solution)/shard_map/ppermute | solution.py:24
  99.5 22.4 %collective-permute-start.18 = (bf16[256,2048]{1,0:T(8,128)(2,1)}, bf16[256,2048]{1,0:T(8,128)(2,1)}, u32[]{:S(2)}, u32[]{:S(2)}) collective-permute-start(bf16[256,2048]{1,0:T(8,128)(2,1)} %get-tuple-element.80.normed_hbm.refs_0_), channel_id=1, source_target_pairs={{0,16},{4,20},{8,24},{12,28},{16,0},{20,4},{24,8},{28,12},{1,17},{... | collective-permute-start | bytes 3145736 | tf_op jit(solution)/shard_map/ppermute | solution.py:97
  100.1 22.1 %collective-permute-start.15 = (bf16[256,2048]{1,0:T(8,128)(2,1)}, bf16[256,2048]{1,0:T(8,128)(2,1)}, u32[]{:S(2)}, u32[]{:S(2)}) collective-permute-start(bf16[256,2048]{1,0:T(8,128)(2,1)} %get-tuple-element.80.normed_hbm.refs_0_), channel_id=1, source_target_pairs={{0,4},{4,0},{8,12},{12,8},{16,20},{20,16},{24,28},{28,24},{1,5},{5... | collective-permute-start | bytes 3145736 | tf_op jit(solution)/shard_map/ppermute | solution.py:97
  105.3 19.1 %collective-permute-start.19 = (bf16[256,2048]{1,0:T(8,128)(2,1)}, bf16[256,2048]{1,0:T(8,128)(2,1)}, u32[]{:S(2)}, u32[]{:S(2)}) collective-permute-start(bf16[256,2048]{1,0:T(8,128)(2,1)} %get-tuple-element.80.normed_hbm.refs_0_), channel_id=1, source_target_pairs={{0,8},{8,0},{16,24},{24,16},{1,9},{9,1},{17,25},{25,17},{2,10},{10... | collective-permute-start | bytes 3145736 | tf_op jit(solution)/shard_map/ppermute | solution.py:24
  122.0 3.0 %collective-permute-start.20 = (bf16[256,2048]{1,0:T(8,128)(2,1)}, bf16[256,2048]{1,0:T(8,128)(2,1)}, u32[]{:S(2)}, u32[]{:S(2)}) collective-permute-start(bf16[256,2048]{1,0:T(8,128)(2,1)} %collective-permute-done.18.refs_1_), channel_id=1, source_target_pairs={{0,8},{8,0},{16,24},{24,16},{1,9},{9,1},{17,25},{25,17},{2,10},{10... | collective-permute-start | bytes 3145736 | tf_op jit(solution)/shard_map/ppermute | solution.py:24
  122.2 4.3 %collective-permute-start.17 = (bf16[256,2048]{1,0:T(8,128)(2,1)}, bf16[256,2048]{1,0:T(8,128)(2,1)}, u32[]{:S(2)}, u32[]{:S(2)}) collective-permute-start(bf16[256,2048]{1,0:T(8,128)(2,1)} %collective-permute-done.15.refs_0_), channel_id=1, source_target_pairs={{0,8},{8,0},{16,24},{24,16},{1,9},{9,1},{17,25},{25,17},{2,10},{10... | collective-permute-start | bytes 3145736 | tf_op jit(solution)/shard_map/ppermute | solution.py:24
  122.5 32.5 %collective-permute-start.22 = (bf16[256,2048]{1,0:T(8,128)(2,1)}, bf16[256,2048]{1,0:T(8,128)(2,1)}, u32[]{:S(2)}, u32[]{:S(2)}) collective-permute-start(bf16[256,2048]{1,0:T(8,128)(2,1)} %collective-permute-done.3.refs_10_.refs_5_), channel_id=1, source_target_pairs={{0,4},{4,0},{8,12},{12,8},{16,20},{20,16},{24,28},{28,24},{1,5},{5... | collective-permute-start | bytes 3145736 | tf_op jit(solution)/shard_map/ppermute | solution.py:97
  122.5 68.8 %all-gather.6.cloned.1.call-start = ((), (), s32[]{:S(2)}) async-start(), calls=%async_computation.5 | async-start | bytes 1310720 | tf_op jit(solution)/shard_map/all_gather | solution.py:958
  122.7 32.5 %collective-permute-start.16 = (bf16[256,2048]{1,0:T(8,128)(2,1)}, bf16[256,2048]{1,0:T(8,128)(2,1)}, u32[]{:S(2)}, u32[]{:S(2)}) collective-permute-start(bf16[256,2048]{1,0:T(8,128)(2,1)} %collective-permute-done.15.refs_0_), channel_id=1, source_target_pairs={{0,16},{4,20},{8,24},{12,28},{16,0},{20,4},{24,8},{28,12},{1,17},{... | collective-permute-start | bytes 3145736 | tf_op jit(solution)/shard_map/ppermute | solution.py:97
  155.0 3.1 %collective-permute-start.23 = (bf16[256,2048]{1,0:T(8,128)(2,1)}, bf16[256,2048]{1,0:T(8,128)(2,1)}, u32[]{:S(2)}, u32[]{:S(2)}) collective-permute-start(bf16[256,2048]{1,0:T(8,128)(2,1)} %collective-permute-done.22.refs_5_), channel_id=1, source_target_pairs={{0,8},{8,0},{16,24},{24,16},{1,9},{9,1},{17,25},{25,17},{2,10},{10... | collective-permute-start | bytes 3145736 | tf_op jit(solution)/shard_map/ppermute | solution.py:24
  155.3 4.3 %collective-permute-start.21 = (bf16[256,2048]{1,0:T(8,128)(2,1)}, bf16[256,2048]{1,0:T(8,128)(2,1)}, u32[]{:S(2)}, u32[]{:S(2)}) collective-permute-start(bf16[256,2048]{1,0:T(8,128)(2,1)} %collective-permute-done.16.refs_1_), channel_id=1, source_target_pairs={{0,8},{8,0},{16,24},{24,16},{1,9},{9,1},{17,25},{25,17},{2,10},{10... | collective-permute-start | bytes 3145736 | tf_op jit(solution)/shard_map/ppermute | solution.py:24
  155.6 92.1 %reduce-scatter.5.cloned.1.call-start = ((), (), s32[]{:S(2)}) async-start(), calls=%async_computation.4 | async-start | bytes 1310720 | tf_op jit(solution)/shard_map/reduce_scatter | solution.py:113
  191.0 69.5 %all-gather.8.cloned.1.call-start = ((), (), s32[]{:S(2)}) async-start(), calls=%async_computation.6 | async-start | bytes 4718592 | tf_op jit(solution)/shard_map/all_gather | solution.py:109
  202.2 2.9 collective-permute-start.28
  202.5 8.6 %collective-permute-start.27 = (bf16[256,512]{1,0:T(8,128)(2,1)S(1)}, bf16[256,512]{1,0:T(8,128)(2,1)}, u32[]{:S(2)}, u32[]{:S(2)}) collective-permute-start(bf16[256,512]{1,0:T(8,128)(2,1)S(1)} %copy-done.16), channel_id=1, source_target_pairs={{0,4},{4,0},{1,5},{5,1},{2,6},{6,2},{3,7},{7,3},{8,12},{12,8},{9,1... | collective-permute-start | bytes 786440 | tf_op jit(solution)/shard_map/ppermute | solution.py:1005
  214.4 10.3 %collective-permute-start.24 = (bf16[2048,768]{1,0:T(8,128)(2,1)}, bf16[2048,768]{1,0:T(8,128)(2,1)}, u32[]{:S(2)}, u32[]{:S(2)}) collective-permute-start(bf16[2048,768]{1,0:T(8,128)(2,1)} %get-tuple-element.91.refs_16_), channel_id=1, source_target_pairs={{0,8},{8,0},{16,24},{24,16},{1,9},{9,1},{17,25},{25,17},{2,10},{10... | collective-permute-start | bytes 9437192 | tf_op jit(solution)/shard_map/ppermute | solution.py:24
  214.4 10.5 %collective-permute-start.25 = (bf16[2048,768]{1,0:T(8,128)(2,1)}, bf16[2048,768]{1,0:T(8,128)(2,1)}, u32[]{:S(2)}, u32[]{:S(2)}) collective-permute-start(bf16[2048,768]{1,0:T(8,128)(2,1)} %get-tuple-element.93), channel_id=1, source_target_pairs={{0,8},{8,0},{16,24},{24,16},{1,9},{9,1},{17,25},{25,17},{2,10},{10... | collective-permute-start | bytes 9437192 | tf_op jit(solution)/shard_map/ppermute | solution.py:24
  214.9 14.5 %collective-permute-start.26 = (bf16[768,2048]{1,0:T(8,128)(2,1)}, bf16[768,2048]{1,0:T(8,128)(2,1)}, u32[]{:S(2)}, u32[]{:S(2)}) collective-permute-start(bf16[768,2048]{1,0:T(8,128)(2,1)} %get-tuple-element.94), channel_id=1, source_target_pairs={{0,8},{8,0},{16,24},{24,16},{1,9},{9,1},{17,25},{25,17},{2,10},{10... | collective-permute-start | bytes 9437192 | tf_op jit(solution)/shard_map/ppermute | solution.py:24
  215.0 26.2 %collective-permute-start.37 = (bf16[128,2048]{1,0:T(8,128)(2,1)}, bf16[128,2048]{1,0:T(8,128)(2,1)}, u32[]{:S(2)}, u32[]{:S(2)}) collective-permute-start(bf16[128,2048]{1,0:T(8,128)(2,1)} %get-tuple-element.137.refs_8_), channel_id=1, source_target_pairs={{0,4},{4,0},{8,12},{12,8},{16,20},{20,16},{24,28},{28,24},{1,5},{5... | collective-permute-start | bytes 1572872 | tf_op jit(solution)/shard_map/ppermute | solution.py:97
  215.3 26.0 %collective-permute-start.35 = (bf16[128,2048]{1,0:T(8,128)(2,1)}, bf16[128,2048]{1,0:T(8,128)(2,1)}, u32[]{:S(2)}, u32[]{:S(2)}) collective-permute-start(bf16[128,2048]{1,0:T(8,128)(2,1)} %get-tuple-element.138.refs_7_), channel_id=1, source_target_pairs={{0,16},{4,20},{8,24},{12,28},{16,0},{20,4},{24,8},{28,12},{1,17},{... | collective-permute-start | bytes 1572872 | tf_op jit(solution)/shard_map/ppermute | solution.py:97
  224.7 19.8 %collective-permute-start.29 = (bf16[272,512]{1,0:T(8,128)(2,1)}, bf16[272,512]{1,0:T(8,128)(2,1)}, u32[]{:S(2)}, u32[]{:S(2)}) collective-permute-start(bf16[272,512]{1,0:T(8,128)(2,1)} %get-tuple-element.115), channel_id=1, source_target_pairs={{0,1},{1,0},{2,3},{3,2},{4,5},{5,4},{6,7},{7,6},{8,9},{9,8},{10,11... | collective-permute-start | bytes 835592 | tf_op jit(solution)/shard_map/ppermute | solution.py:24
  224.9 19.6 %collective-permute-start.30 = (bf16[272,512]{1,0:T(8,128)(2,1)}, bf16[272,512]{1,0:T(8,128)(2,1)}, u32[]{:S(2)}, u32[]{:S(2)}) collective-permute-start(bf16[272,512]{1,0:T(8,128)(2,1)} %get-tuple-element.118), channel_id=1, source_target_pairs={{0,1},{1,0},{2,3},{3,2},{4,5},{5,4},{6,7},{7,6},{8,9},{9,8},{10,11... | collective-permute-start | bytes 835592 | tf_op jit(solution)/shard_map/ppermute | solution.py:24
  244.2 33.0 %collective-permute-start.36 = (bf16[128,2048]{1,0:T(8,128)(2,1)}, bf16[128,2048]{1,0:T(8,128)(2,1)}, u32[]{:S(2)}, u32[]{:S(2)}) collective-permute-start(bf16[128,2048]{1,0:T(8,128)(2,1)} %get-tuple-element.126), channel_id=1, source_target_pairs={{0,4},{4,0},{8,12},{12,8},{16,20},{20,16},{24,28},{28,24},{1,5},{5... | collective-permute-start | bytes 1572872 | tf_op jit(solution)/shard_map/ppermute | solution.py:97
  244.5 34.7 %collective-permute-start.38 = (bf16[128,2048]{1,0:T(8,128)(2,1)}, bf16[128,2048]{1,0:T(8,128)(2,1)}, u32[]{:S(2)}, u32[]{:S(2)}) collective-permute-start(bf16[128,2048]{1,0:T(8,128)(2,1)} %get-tuple-element.129), channel_id=1, source_target_pairs={{0,16},{4,20},{8,24},{12,28},{16,0},{20,4},{24,8},{28,12},{1,17},{... | collective-permute-start | bytes 1572872 | tf_op jit(solution)/shard_map/ppermute | solution.py:97
  247.6 28.3 %collective-permute-start.31 = (bf16[272,512]{1,0:T(8,128)(2,1)}, bf16[272,512]{1,0:T(8,128)(2,1)}, u32[]{:S(2)}, u32[]{:S(2)}) collective-permute-start(bf16[272,512]{1,0:T(8,128)(2,1)} %add_convert_fusion.5.refs_4_), channel_id=1, source_target_pairs={{0,2},{1,3},{2,0},{3,1},{4,6},{5,7},{6,4},{7,5},{8,10},{9,11},{10,... | collective-permute-start | bytes 835592 | tf_op jit(solution)/shard_map/ppermute | solution.py:24
  277.2 2.0 collective-permute-start.32
  278.9 8.8 %collective-permute-start.39 = (bf16[128,2048]{1,0:T(8,128)(2,1)S(1)}, bf16[128,2048]{1,0:T(8,128)(2,1)S(1)}, u32[]{:S(2)}, u32[]{:S(2)}) collective-permute-start(bf16[128,2048]{1,0:T(8,128)(2,1)S(1)} %add_convert_fusion.3), channel_id=1, source_target_pairs={{0,8},{8,0},{16,24},{24,16},{1,9},{9,1},{17,25},{25,17},{2,10},{10... | collective-permute-start | bytes 1572872 | tf_op jit(solution)/shard_map/ppermute | solution.py:24
  279.2 3.7 %collective-permute-start.33 = (f32[1280]{0:T(1024)S(1)}, f32[1280]{0:T(1024)S(1)}, u32[]{:S(2)}, u32[]{:S(2)}) collective-permute-start(f32[1280]{0:T(1024)S(1)} %fusion.8), channel_id=1, source_target_pairs={{0,16},{4,20},{8,24},{12,28},{16,0},{20,4},{24,8},{28,12},{1,17},{... | collective-permute-start | bytes 15368 | tf_op jit(solution)/shard_map/ppermute | solution.py:97
  282.4 5.3 %collective-permute-start.40 = (bf16[128,2048]{1,0:T(8,128)(2,1)S(1)}, bf16[128,2048]{1,0:T(8,128)(2,1)S(1)}, u32[]{:S(2)}, u32[]{:S(2)}) collective-permute-start(bf16[128,2048]{1,0:T(8,128)(2,1)S(1)} %add_convert_fusion.1), channel_id=1, source_target_pairs={{0,8},{8,0},{16,24},{24,16},{1,9},{9,1},{17,25},{25,17},{2,10},{10... | collective-permute-start | bytes 1572872 | tf_op jit(solution)/shard_map/ppermute | solution.py:24
  283.0 3.7 %collective-permute-start.34 = (f32[1280]{0:T(1024)S(1)}, f32[1280]{0:T(1024)S(1)}, u32[]{:S(2)}, u32[]{:S(2)}) collective-permute-start(f32[1280]{0:T(1024)S(1)} %add.93), channel_id=1, source_target_pairs={{0,4},{4,0},{8,12},{12,8},{16,20},{20,16},{24,28},{28,24},{1,5},{5... | collective-permute-start | bytes 15368 | tf_op jit(solution)/shard_map/ppermute | solution.py:97
  (16 other events, 74.0 us)
Sparse Core Ops, SparseCore 0:
  40.7 54.6 all-gather.3
  214.5 45.9 all-gather.7
Sparse Core Ops, SparseCore 1:
  122.6 26.8 reduce-scatter.2
  155.7 26.1 all-gather.5
  191.1 25.4 reduce-scatter.4
